TPU v7x, 32 devices: a whole 2x2x4 slice. The times are simulated.
32 devices in a mesh: grp: 2 (over z_hi), tile: 8 (over y, x, core), spec: 2 (over z_lo).
Axes of the slice: x: 2, y: 2, z: 4 (z_hi: 2, z_lo: 2; z = z_hi * 2 + z_lo), core: 2. Of those that a mesh axis runs over, the one named last changes fastest.
Arguments:
- spectrum: float32 [2, 32, 36, 64, 256], P('grp', None, 'spec', 'tile'), may hold values from 0.01 to 1
- wind: float32 [2, 64, 256], P(None, 'tile'), may hold values from -48 to 48
- land_mask: int32 [64, 256], P('tile'), may hold values 0 or 1
- intersection: int32 [64, 256], P('tile'), may hold values from 0 to 255, as said below
- ocean_state: float32 [2, 3, 16, 256, 64], P('grp', None, 'spec', 'tile'), may hold values from -1 to 1
- sea_level: float32 [2, 256, 64], P('grp', 'tile'), may hold values from -1 to 1
Outputs:
- spectrum_next: float32 [2, 32, 36, 64, 256], P('grp', None, 'spec', 'tile')
- ocean_next: float32 [2, 3, 16, 256, 64], P('grp', None, 'spec', 'tile')
Inputs may be any that keep to these rules, and one draw needn't show every extreme that they name: In each row i, intersection[i, j] = (j + s_i) mod 256 for a shift s_i of that row.
All inputs are finite; a program needn't handle non-finite values. No bound on the sum of `land_mask` on one device may be relied on, other than what follows from the above.
Results may differ from a plain program's by a relative error of at most 0.0001.
Values sent between devices are 32-bit elements; how exact they have to be, the bound alone decides.
No kernel may reach another device: no remote copies, remote signals or barrier semaphores. Data moves between devices by JAX's collectives and lax.ppermute only.
A program may use at most 128 MiB of HBM per device.

v0:
```python
import functools
import math

import jax
import jax.numpy as jnp
import numpy as np
from jax import lax
from jax.experimental import pallas as pl
from jax.experimental.pallas import tpu as pltpu
from jax.sharding import PartitionSpec as P

WSTEPS = 4
OSTEPS = 2
LANES = 128
SUB = 8
UNROLL = 4
AXES = ("grp", "tile", "spec")

BW, GE, GN, WE, WN, SX, SY, DX, DY, INV = range(10)

VM = pl.BlockSpec(memory_space=pltpu.VMEM)
SM = pl.BlockSpec(memory_space=pltpu.SMEM)
HB = pl.BlockSpec(memory_space=pl.ANY)


def f32(*shape):
    return jax.ShapeDtypeStruct(shape, jnp.float32)


def wave_table(freqs, dirs, parts):
    frequency = 0.04 * 1.1 ** np.arange(freqs)
    celerity = 1.56 / frequency
    group = 0.4 * 1.1 ** (-np.arange(freqs, dtype=np.float64))
    width = 0.1 * frequency * (2.0 * math.pi / dirs)
    angle = 2.0 * math.pi * (np.arange(dirs) + 0.5) / dirs
    cos, sin, one = np.cos(angle), np.sin(angle), np.ones(dirs)
    columns = [
        np.outer(width, one),
        np.outer(group, cos),
        np.outer(group, sin),
        np.outer(0.05 / celerity, cos),
        np.outer(0.05 / celerity, sin),
        np.outer(5.0 / celerity, cos),
        np.outer(5.0 / celerity, sin),
        np.outer(20.0 * frequency**3, cos),
        np.outer(20.0 * frequency**3, sin),
        np.outer(1.0 / width, one),
    ]
    table = np.zeros((parts, freqs * dirs // parts, 16), np.float32)
    for k, column in enumerate(columns):
        split = column.reshape(freqs, parts, dirs // parts).transpose(1, 0, 2)
        table[:, :, k] = split.reshape(parts, -1)
    return table


def level_table(levels, parts, own):
    depth = (np.arange(levels) + 0.5) / levels
    profile = np.exp(-2.0 * depth)
    weights = profile / profile.sum()
    table = np.zeros((parts, 3, own + 4), np.float32)
    for s in range(parts):
        table[s, 0, :own] = weights[s * own : (s + 1) * own]
        for l in range(own + 4):
            g = s * own + l - 2
            if 0 <= g < levels:
                table[s, 1, l] = profile[g]
                table[s, 2, l] = 1.0
    return table


def lanes_of(shape):
    return lax.broadcasted_iota(jnp.int32, shape, len(shape) - 1)


def wide(column):
    return jnp.broadcast_to(column, (SUB, LANES))


def half(h):
    return slice(h * LANES, (h + 1) * LANES)


def barrel(values, shift, size, left):
    bit = 1
    while bit < size:
        taken = (shift & bit) != 0
        amount = size - bit if left else bit
        values = [jnp.where(taken, pltpu.roll(v, amount, 1), v) for v in values]
        bit *= 2
    return values


def send_kernel(n, level_ref, ocean_ref, sea_ref, out_ref, rim_ref):
    t_n, s_n, rows, cols, own, ny = n
    s = lax.axis_index("spec")
    pad = -(-ny // LANES) * LANES
    parts = []
    for c in range(2):
        total = None
        for k in range(own):
            term = level_ref[s, 0, k] * ocean_ref[c, k]
            total = term if total is None else total + term
        parts.append(total)
    parts.append(jnp.where(s == 0, sea_ref[...], 0.0))
    for c in range(3):
        rim_ref[c] = jnp.where(s == 0, ocean_ref[c, own - 2 : own], ocean_ref[c, 0:2])
    stack = jnp.concatenate(parts, axis=0)
    stack = jnp.pad(stack, ((0, LANES - 3 * cols), (0, pad - ny)))
    turned = jnp.transpose(stack)
    for t in range(t_n):
        for q in range(s_n):
            out_ref[t * s_n + q] = turned[t * rows : (t + 1) * rows, : 4 * cols]


def load_kernel(n, table_ref, spectrum_ref, wind_ref, ocean_ref, sea_ref, mid_ref, lo_ref, hi_ref, growth_ref, raw, windb, sem):
    rows, fd, nx, cols, own, chunks = n
    s = lax.axis_index("spec")
    part = fd * rows // chunks
    copies = []
    halves = nx // LANES
    for c in range(chunks):
        span = pl.ds(c * part, part)
        for h in range(halves):
            copy = pltpu.make_async_copy(spectrum_ref.at[span, half(h)], raw.at[h, span], sem.at[c, h])
            copy.start()
            copies.append(copy)
    for c in range(2):
        for r in range(rows):
            windb[c, r] = jnp.broadcast_to(wind_ref[c, r : r + 1], (SUB, nx))

    def grow(i, carry):
        for k in range(2):
            sl = pl.ds(pl.multiple_of(i * 2 * SUB + k * SUB, SUB), SUB)
            we, wn = wide(table_ref[s, sl, WE : WE + 1]), wide(table_ref[s, sl, WN : WN + 1])
            for r in range(rows):
                for h in range(nx // LANES):
                    drive = we * windb[0, r, :, half(h)] + wn * windb[1, r, :, half(h)]
                    growth_ref[r, sl, half(h)] = 1.0 + jnp.maximum(drive - 0.05, 0.0)
        return carry

    lax.fori_loop(0, fd // (2 * SUB), grow, 0)
    for c in range(chunks):
        for h in range(halves):
            copies[c * halves + h].wait()
        count = fd // chunks

        def turn(i, carry):
            at = pl.multiple_of(c * count + i * SUB, SUB)
            sl = pl.ds(at, SUB)
            bw = wide(table_ref[s, sl, BW : BW + 1])
            for r in range(rows):
                for h in range(nx // LANES):
                    value = bw * raw[h, pl.ds(at * rows + r, SUB, stride=rows), :]
                    if r == 0:
                        lo_ref[sl, half(h)] = value
                    elif r == rows - 1:
                        hi_ref[sl, half(h)] = value
                    else:
                        mid_ref[r - 1, sl, half(h)] = value
            return carry

        lax.fori_loop(0, count // SUB, turn, 0)

    ny = ocean_ref.shape[1]

    @pl.when(lax.axis_index("grp") == 1)
    def _():
        stack = 3 * own
        for k in range(2):
            for ref, at in ((lo_ref, k), (hi_ref, cols - 2 + k)):
                for m in range(stack):
                    ref[k * stack + m : k * stack + m + 1, 0:ny] = ocean_ref[m * cols + at : m * cols + at + 1, :]
                ref[2 * stack + k : 2 * stack + k + 1, 0:ny] = sea_ref[at : at + 1, :]


def pick_kernel(n, got_ref, mask_ref, cross_ref, u_ref, v_ref, depth_ref, rim_ref):
    t_n, s_n, rows, cols, nx = n
    lane = lanes_of((rows, LANES))
    per = LANES // cols
    fields = [[jnp.zeros((rows, LANES), jnp.float32) for _ in range(nx // LANES)] for _ in range(3)]
    for t in range(t_n):
        tile = got_ref[(t_n + t) * s_n]
        for q in range(1, s_n):
            tile = tile + got_ref[(t_n + t) * s_n + q]
        if tile.shape[1] < LANES:
            tile = jnp.pad(tile, ((0, 0), (0, LANES - tile.shape[1])))
        h, at = t // per, (t % per) * cols
        inside = (lane >= at) & (lane < at + cols)
        for c in range(3):
            moved = pltpu.roll(tile, (at - c * cols) % LANES, 1) if (at - c * cols) % LANES else tile
            fields[c][h] = jnp.where(inside, moved, fields[c][h])
    whole = [jnp.concatenate(f, axis=1) for f in fields]
    shift = jnp.broadcast_to(cross_ref[:, 0:1], (rows, nx))
    u, v, sea = barrel(whole, shift, nx, True)
    depth = 10.0 + 4.0 * sea
    u_ref[...] = 0.1 * u
    v_ref[...] = 0.1 * v
    depth_ref[...] = 25.0 / (depth * depth)
    rim_ref[0:rows] = mask_ref[...].astype(jnp.float32)
    rim_ref[rows : 2 * rows] = 0.1 * v


def advance(segments, fd, nx, s, table_ref, energy, growth, store, splat, acc, sums):
    halves = nx // LANES
    lane = lanes_of((SUB, LANES))
    first, last = lane == 0, lane == LANES - 1
    acc[...] = jnp.zeros(acc.shape, jnp.float32)

    def body(i, carry):
        totals = {}

        def add(key, value):
            totals[key] = totals[key] + value if key in totals else value

        for k in range(UNROLL):
            sl = pl.ds(pl.multiple_of((i * UNROLL + k) * SUB, SUB), SUB)
            ge, gn = wide(table_ref[s, sl, GE : GE + 1]), wide(table_ref[s, sl, GN : GN + 1])
            bands = [wide(table_ref[s, sl, b : b + 1]) for b in (SX, SY, DX, DY)] if sums else None
            for segment in segments:
                def state(r):
                    e = [energy(r, sl, h) * splat[2, r + 1, :, half(h)] for h in range(halves)]
                    north = [(gn + splat[1, r + 1, :, half(h)]) * e[h] for h in range(halves)]
                    return e, north

                here, below = state(segment[0]), state(segment[0] - 1)
                flow = [jnp.maximum(below[1][h], 0.0) + jnp.minimum(here[1][h], 0.0) for h in range(halves)]
                for r in segment:
                    above = state(r + 1)
                    e, north = here
                    upper = [jnp.maximum(north[h], 0.0) + jnp.minimum(above[1][h], 0.0) for h in range(halves)]
                    east = [(ge + splat[0, r + 1, :, half(h)]) * e[h] for h in range(halves)]
                    left = [pltpu.roll(x, LANES - 1, 1) for x in east]
                    flux = [
                        jnp.maximum(east[h], 0.0)
                        + jnp.minimum(jnp.where(last, left[h + 1] if h + 1 < halves else 0.0, left[h]), 0.0)
                        for h in range(halves)
                    ]
                    right = [pltpu.roll(x, 1, 1) for x in flux]
                    for h in range(halves):
                        behind = jnp.where(first, right[h - 1] if h else jnp.minimum(east[0], 0.0), right[h])
                        advected = (e[h] - (flux[h] - behind)) - (upper[h] - flow[h])
                        g = growth(r, sl, h)
                        add((0, r, h), advected)
                        if sums:
                            pushed = (g - 1.0) * advected
                            grown = advected + pushed
                            for b in range(2):
                                add((1 + b, r, h), bands[b] * pushed)
                                add((3 + b, r, h), bands[2 + b] * grown)
                        else:
                            grown = g * advected
                        store(r, sl, h, grown)
                    here, flow = above, upper
        for (kind, r, h), value in totals.items():
            acc[kind, r, :, half(h)] += value
        return carry

    lax.fori_loop(0, fd // (SUB * UNROLL), body, 0)


def folded(acc, kind, rows):
    return [jnp.sum(acc[kind, r], axis=0, keepdims=True) for r in rows]


def fill(splat, kind, row, value, nx):
    splat[kind, row + 1] = jnp.broadcast_to(value, (SUB, nx))


def middle_kernel(n, begin, sums, *refs):
    rows, fd, nx = n
    table_ref, u_ref, v_ref, *refs = refs
    s = lax.axis_index("spec")
    if begin:
        rim_ref, mid_ref, lo_ref, hi_ref, growth_ref, out_ref, total_ref, splat, acc = refs
        breaking = rim_ref[0:rows]
    else:
        (rim_ref, depth_ref, own_ref, got_ref, mid_ref, lo_ref, hi_ref, growth_ref,
         out_ref, total_ref, breaking_ref, splat, acc) = refs
        wet = rim_ref[0:rows]
        breaking = wet / (1.0 + (own_ref[...] + got_ref[...]) * depth_ref[...])
        breaking_ref[...] = breaking
    for r in range(rows):
        fill(splat, 0, r, u_ref[r : r + 1], nx)
        fill(splat, 1, r, v_ref[r : r + 1], nx)
        fill(splat, 2, r, breaking[r : r + 1], nx)

    def energy(r, sl, h):
        if r == 0:
            return lo_ref[sl, half(h)]
        if r == rows - 1:
            return hi_ref[sl, half(h)]
        return mid_ref[r - 1, sl, half(h)]

    def store(r, sl, h, value):
        out_ref[r - 1, sl, half(h)] = value

    inner = list(range(1, rows - 1))
    advance([inner], fd, nx, s, table_ref, energy, lambda r, sl, h: growth_ref[r, sl, half(h)], store, splat, acc, sums)
    zero = jnp.zeros((1, nx), jnp.float32)
    for kind in range(acc.shape[0]):
        total_ref[kind] = jnp.concatenate([zero] + folded(acc, kind, inner) + [zero], axis=0)


def edge_kernel(n, begin, sums, *refs):
    rows, fd, nx, t_n, s_n, cols, own = n
    (table_ref, u_ref, v_ref, breaking_ref, below_ref, above_ref, vb_ref, va_ref, rim_ref, mid_ref, lo_ref, hi_ref,
     hb_ref, ha_ref, growth_ref, part_ref, *refs) = refs
    s = lax.axis_index("spec")
    if begin:
        level_ref, newlo_ref, newhi_ref, total_ref, splat, acc = refs
    elif sums:
        cross_ref, newlo_ref, newhi_ref, send_ref, splat, acc = refs
    else:
        newlo_ref, newhi_ref, total_ref, splat, acc = refs
    for r in (0, 1, rows - 2, rows - 1):
        fill(splat, 0, r, u_ref[r : r + 1], nx)
        fill(splat, 1, r, v_ref[r : r + 1], nx)
        fill(splat, 2, r, breaking_ref[r : r + 1], nx)
    fill(splat, 1, -1, vb_ref[2 * rows - 1 : 2 * rows], nx)
    fill(splat, 2, -1, below_ref[rows - 1 : rows], nx)
    fill(splat, 1, rows, va_ref[rows : rows + 1], nx)
    fill(splat, 2, rows, above_ref[0:1], nx)

    def energy(r, sl, h):
        if r == -1:
            return hb_ref[sl, half(h)]
        if r == rows:
            return ha_ref[sl, half(h)]
        if r == 0:
            return lo_ref[sl, half(h)]
        if r == rows - 1:
            return hi_ref[sl, half(h)]
        return mid_ref[r - 1, sl, half(h)]

    def store(r, sl, h, value):
        (newlo_ref if r == 0 else newhi_ref)[sl, half(h)] = value

    advance([[0], [rows - 1]], fd, nx, s, table_ref, energy, lambda r, sl, h: growth_ref[r, sl, half(h)], store, splat, acc, sums)
    zero = jnp.zeros((rows - 2, nx), jnp.float32)
    kinds = []
    for kind in range(acc.shape[0]):
        low, high = folded(acc, kind, (0, rows - 1))
        kinds.append(part_ref[kind] + jnp.concatenate([low, zero, high], axis=0))
    if not sums:
        total_ref[...] = kinds[0]
    if begin:
        ny = level_ref.shape[1]

        @pl.when(lax.axis_index("grp") == 1)
        def _():
            for k in range(2):
                for ref, at in ((newlo_ref, k), (newhi_ref, cols - 2 + k)):
                    for c in range(6):
                        ref[k * SUB + c : k * SUB + c + 1, 0:ny] = level_ref[c * cols + at : c * cols + at + 1, :]

    if sums:
        wet = jnp.where(s == 0, rim_ref[0:rows], 0.0)
        shift = jnp.broadcast_to(cross_ref[:, 0:1], (rows, nx))
        moved = barrel(kinds + [wet], shift, nx, False)
        lane = lanes_of((rows, nx))
        size = cols + 8
        for t in range(t_n):
            chunk = jnp.zeros((rows, nx), jnp.float32)
            for q, value in enumerate(moved):
                amount = (q * size - (cols * t - 4)) % nx
                piece = pltpu.roll(value, amount, 1) if amount else value
                chunk = jnp.where((lane >= q * size) & (lane < (q + 1) * size), piece, chunk)
            for q in range(s_n):
                send_ref[(t_n + t) * s_n + q] = chunk
        mine = lax.axis_index("tile")
        for q in range(s_n):
            send_ref[mine * s_n + q] = kinds[0]


def last_kernel(n, table_ref, level_ref, got_ref, rim_ref, depth_ref, mid_ref, lo_ref, hi_ref, ocean_ref, sea_ref,
                hb_ref, ha_ref, cb_ref, ca_ref, lev_ref, waves_ref, next_ref,
                raw, brk, turn, field, mix, out, sem, osem):
    rows, fd, nx, t_n, s_n, cols, own, ny, chunks = n
    s = lax.axis_index("spec")
    g = lax.axis_index("grp")
    tile = lax.axis_index("tile")
    part = fd * rows // chunks
    count = fd // chunks
    pad = turn.shape[0]
    size = cols + 8

    halves = nx // LANES

    def writes(c, source):
        return [
            pltpu.make_async_copy(
                raw.at[h, pl.ds(source * part, part)], waves_ref.at[pl.ds(c * part, part), half(h)], sem.at[c, h])
            for h in range(halves)
        ]

    ocean_copy = pltpu.make_async_copy(out, next_ref, osem)

    @pl.when(g == 0)
    def _():
        total = got_ref[tile * s_n]
        for q in range(1, s_n):
            total = total + got_ref[tile * s_n + q]
        breaking = rim_ref[0:rows] / (1.0 + total * depth_ref[...])
        for r in range(rows):
            brk[r] = jnp.broadcast_to(breaking[r : r + 1], (SUB, nx))
        for c in range(chunks):

            def finish(i, carry):
                at = pl.multiple_of(c * count + i * SUB, SUB)
                sl = pl.ds(at, SUB)
                inv = wide(table_ref[s, sl, INV : INV + 1])
                for r in range(rows):
                    for h in range(nx // LANES):
                        if r == 0:
                            value = lo_ref[sl, half(h)]
                        elif r == rows - 1:
                            value = hi_ref[sl, half(h)]
                        else:
                            value = mid_ref[r - 1, sl, half(h)]
                        raw[h, pl.ds(at * rows + r, SUB, stride=rows), :] = value * brk[r, :, half(h)] * inv
                return carry

            lax.fori_loop(0, count // SUB, finish, 0)
            for copy in writes(c, c):
                copy.start()
        out[...] = jnp.zeros((3, own, cols, ny), jnp.float32)
        ocean_copy.start()
        ocean_copy.wait()
        for c in range(chunks):
            for copy in writes(c, c):
                copy.wait()

    @pl.when(g == 1)
    def _():
        def clear(i, carry):
            for h in range(halves):
                raw[h, pl.ds(pl.multiple_of(i * 64, 64), 64), :] = jnp.zeros((64, LANES), jnp.float32)
            return carry

        lax.fori_loop(0, part // 64, clear, 0)
        for c in range(chunks):
            for copy in writes(c, 0):
                copy.start()

        if pad > ny:
            turn[ny:pad] = jnp.zeros((pad - ny, nx), jnp.float32)
        for t in range(t_n):
            tilev = got_ref[t * s_n]
            for q in range(1, s_n):
                tilev = tilev + got_ref[t * s_n + q]
            turn[t * rows : (t + 1) * rows] = tilev
        turned = jnp.transpose(turn[...])
        total, sx, sy, dx, dy, wet = [turned[q * size : (q + 1) * size] for q in range(6)]
        row = lax.broadcasted_iota(jnp.int32, (size, pad), 0)
        column = row + (tile * cols - 4)
        wet = jnp.where((column >= 0) & (column < t_n * cols), wet, 0.0)
        stack = 3 * own
        mix[0] = jnp.zeros((size, pad), jnp.float32)
        mix[0, 4 : 4 + cols, 0:ny] = sea_ref[...]
        mix[0, 2:4, 0:ny] = hb_ref[2 * stack : 2 * stack + 2, 0:ny]
        mix[0, 4 + cols : 6 + cols, 0:ny] = ha_ref[2 * stack : 2 * stack + 2, 0:ny]
        depth = 10.0 + 4.0 * mix[0]
        breaking = 1.0 / (1.0 + 25.0 * total / (depth * depth))
        swept = wet * breaking
        sx, sy, dx, dy = sx * breaking, sy * breaking, dx * swept, dy * swept

        field[...] = jnp.zeros(field.shape, jnp.float32)
        ext = own + 4
        for c in range(3):
            for k in range(own):
                l = c * ext + 2 + k
                field[l, 4 : 4 + cols, 0:ny] = ocean_ref[c, k]
                for m in range(2):
                    at = m * stack + c * own + k
                    field[l, 2 + m : 3 + m, 0:ny] = hb_ref[at : at + 1, 0:ny]
                    field[l, 4 + cols + m : 5 + cols + m, 0:ny] = ha_ref[at : at + 1, 0:ny]
        for upper in range(2):
            @pl.when(s == 1 - upper)
            def _():
                for c in range(3):
                    for k in range(2):
                        l = c * ext + (own + 2 if upper else 0) + k
                        at = (c * 2 + k) * cols
                        field[l, 4 : 4 + cols, 0:ny] = lev_ref[at : at + cols, :]
                        for m in range(2):
                            at = m * SUB + c * 2 + k
                            field[l, 2 + m : 3 + m, 0:ny] = cb_ref[at : at + 1, 0:ny]
                            field[l, 4 + cols + m : 5 + cols + m, 0:ny] = ca_ref[at : at + 1, 0:ny]

        lane = lanes_of((size, pad))

        def new_fields(source, k):
            values = []
            for c in range(3):
                q = source[c * ext + k]
                lateral = (
                    pltpu.roll(q, size - 1, 0)
                    + pltpu.roll(q, 1, 0)
                    + jnp.where(lane == ny - 1, 0.0, pltpu.roll(q, pad - 1, 1))
                    + jnp.where(lane == 0, 0.0, pltpu.roll(q, 1, 1))
                    - 4.0 * q
                )
                vertical = source[c * ext + k + 1] + source[c * ext + k - 1] - 2.0 * q
                values.append((q, q + 0.1 * lateral + 0.2 * vertical))
            (u, du), (v, dv), (_, dt) = values
            shaped = level_ref[s, 1, k]
            top = jnp.where((s == 0) & (k == 2), 1.0, 0.0)
            east = du + 0.1 * (v + shaped * dy) + top * sx
            north = dv - 0.1 * (u + shaped * dx) + top * sy
            keep = wet * level_ref[s, 2, k]
            return keep * east, keep * north, keep * dt

        for k in range(1, ext - 1):
            for c, value in enumerate(new_fields(field, k)):
                mix[c * ext + k] = value
        for k in range(2, ext - 2):
            for c, value in enumerate(new_fields(mix, k)):
                out[c, k - 2] = value[4 : 4 + cols, 0:ny]
        ocean_copy.start()
        ocean_copy.wait()
        for c in range(chunks):
            for copy in writes(c, 0):
                copy.wait()


def body(spectrum, wind, land_mask, intersection, ocean_state, sea_level, *, mesh_shape):
    g_n, t_n, s_n = (mesh_shape[a] for a in AXES)
    _, freqs, dirs, rows, nx = spectrum.shape
    _, _, own, cols, ny = ocean_state.shape
    fd = freqs * dirs
    devices = g_n * t_n * s_n
    table = jnp.asarray(wave_table(freqs, dirs * s_n, s_n))
    levels = jnp.asarray(level_table(own * s_n, s_n, own))
    ocean = ocean_state[0]
    sea = sea_level[0]
    natural = spectrum.reshape(fd * rows, nx)
    flat = ocean_state.reshape(3 * own * cols, ny)
    chunks = 8
    params = pltpu.CompilerParams(vmem_limit_bytes=24 << 20)

    def up(x):
        return lax.ppermute(x, "tile", [(i, i + 1) for i in range(t_n - 1)])

    def down(x):
        return lax.ppermute(x, "tile", [(i + 1, i) for i in range(t_n - 1)])

    def others(x):
        result = None
        for k in range(1, s_n):
            got = lax.ppermute(x, "spec", [(i, (i + k) % s_n) for i in range(s_n)])
            result = got if result is None else result + got
        return result

    send, level_rim = pl.pallas_call(
        functools.partial(send_kernel, (t_n, s_n, rows, cols, own, ny)),
        out_shape=(f32(devices, rows, 4 * cols), f32(3, 2, cols, ny)),
        in_specs=[SM, VM, VM], out_specs=(VM, VM), compiler_params=params, name="send",
    )(levels, ocean, sea)
    arrived = lax.all_to_all(send, AXES, 0, 0, tiled=True)

    mid, lo, hi, growth = pl.pallas_call(
        functools.partial(load_kernel, (rows, fd, nx, cols, own, chunks)),
        out_shape=(f32(rows - 2, fd, nx), f32(fd, nx), f32(fd, nx), f32(rows, fd, nx)),
        in_specs=[VM, HB, VM, VM, VM], out_specs=(VM,) * 4,
        scratch_shapes=[pltpu.VMEM((nx // LANES, fd * rows, LANES), jnp.float32), pltpu.VMEM((2, rows, SUB, nx), jnp.float32),
                        pltpu.SemaphoreType.DMA((chunks, nx // LANES))],
        compiler_params=params, name="load",
    )(table, natural, wind, flat, sea)
    hb, ha = up(hi), down(lo)
    level_got = others(level_rim).reshape(6 * cols, ny)
    hb0, ha0 = hb, ha

    u, v, depth, rim = pl.pallas_call(
        functools.partial(pick_kernel, (t_n, s_n, rows, cols, nx)),
        out_shape=(f32(rows, nx), f32(rows, nx), f32(rows, nx), f32(2 * rows, nx)),
        in_specs=[VM] * 3, out_specs=(VM,) * 4, compiler_params=params, name="pick",
    )(arrived, land_mask, intersection)
    vb, va = up(rim), down(rim)

    breaking, below, above = rim, vb, va
    total = got = None
    for step in range(WSTEPS):
        begin, sums = step == 0, step == WSTEPS - 1
        kinds = 5 if sums else 1
        scratch = [pltpu.VMEM((3, rows + 2, SUB, nx), jnp.float32), pltpu.VMEM((kinds, rows, SUB, nx), jnp.float32)]
        shape = (f32(rows - 2, fd, nx), f32(kinds, rows, nx))
        args = (table, u, v, rim)
        if not begin:
            shape += (f32(rows, nx),)
            args += (depth, total, got)
        args += (mid, lo, hi, growth)
        outs = pl.pallas_call(
            functools.partial(middle_kernel, (rows, fd, nx), begin, sums),
            out_shape=shape, in_specs=[VM] * len(args), out_specs=(VM,) * len(shape),
            scratch_shapes=scratch, compiler_params=params, name=f"middle{step}",
        )(*args)
        if begin:
            newmid, partial = outs
        else:
            newmid, partial, breaking = outs
            below, above = up(breaking), down(breaking)
        args = (table, u, v, breaking, below, above, vb, va, rim, mid, lo, hi, hb, ha, growth, partial)
        if begin:
            args += (level_got,)
        if sums:
            args += (intersection,)
            shape = (f32(fd, nx), f32(fd, nx), f32(devices, rows, nx))
        else:
            shape = (f32(fd, nx), f32(fd, nx), f32(rows, nx))
        newlo, newhi, total = pl.pallas_call(
            functools.partial(edge_kernel, (rows, fd, nx, t_n, s_n, cols, own), begin, sums),
            out_shape=shape, in_specs=[VM] * len(args), out_specs=(VM,) * 3,
            scratch_shapes=scratch, compiler_params=params, name=f"edge{step}",
        )(*args)
        mid, lo, hi = newmid, newlo, newhi
        if not sums:
            got = others(total)
            hb, ha = up(hi), down(lo)
        if begin:
            hb1, ha1 = hb, ha

    landed = lax.all_to_all(total, AXES, 0, 0, tiled=True)
    pad = -(-ny // LANES) * LANES
    size = cols + 8
    ins = (table, levels, landed, rim, depth, mid, lo, hi, ocean, sea, hb0, ha0, hb1, ha1, level_got)
    waves, fields = pl.pallas_call(
        functools.partial(last_kernel, (rows, fd, nx, t_n, s_n, cols, own, ny, chunks)),
        out_shape=(f32(fd * rows, nx), f32(3, own, cols, ny)),
        in_specs=[VM, SM] + [VM] * (len(ins) - 2), out_specs=(HB, HB),
        scratch_shapes=[
            pltpu.VMEM((nx // LANES, fd * rows, LANES), jnp.float32),
            pltpu.VMEM((rows, SUB, nx), jnp.float32),
            pltpu.VMEM((pad, nx), jnp.float32),
            pltpu.VMEM((3 * (own + 4), size, pad), jnp.float32),
            pltpu.VMEM((3 * (own + 4), size, pad), jnp.float32),
            pltpu.VMEM((3, own, cols, ny), jnp.float32),
            pltpu.SemaphoreType.DMA((chunks, nx // LANES)),
            pltpu.SemaphoreType.DMA,
        ],
        compiler_params=params, name="last",
    )(*ins)
    return waves.reshape(spectrum.shape), fields.reshape(ocean_state.shape)


def solution(mesh):
    return jax.shard_map(
        functools.partial(body, mesh_shape=dict(mesh.shape)),
        mesh=mesh,
        in_specs=(
            P("grp", None, "spec", "tile", None),
            P(None, "tile", None),
            P("tile", None),
            P("tile", None),
            P("grp", None, "spec", "tile", None),
            P("grp", "tile", None),
        ),
        out_specs=(P("grp", None, "spec", "tile", None), P("grp", None, "spec", "tile", None)),
        check_vma=False,
    )
```

profile of v0, /device:TPU:0, one launch (start us, length us, event | category | flops | bytes accessed | tf_op | source)
XLA Modules:
  0.0 168.7 jit_solution(3493316947096767794)
XLA Ops:
  0.7 1.1 copy-done.2
  1.7 2.3 %copy-done.6 = f32[1,32,18,8,256]{4,3,2,1,0:T(8,128)S(1)} copy-done((f32[1,32,18,8,256]{4,3,2,1,0:T(8,128)S(1)}, f32[1,32,18,8,256]{4,3,2,1,0:T(8,128)}, u32[]{:S(2)}) %copy-start.6) | copy-done | bytes 4718616
  4.1 1.0 copy-done.7
  5.1 0.7 copy-done.9
  5.8 0.7 copy-done.13
  6.5 9.5 %load.1 = (f32[6,576,256]{2,1,0:T(8,128)S(1)}, f32[576,256]{1,0:T(8,128)S(1)}, f32[576,256]{1,0:T(8,128)S(1)}, f32[8,576,256]{2,1,0:T(8,128)S(1)}) custom-call(f32[2,576,16]{2,1,0:T(8,128)S(1)} %copy-done.2, f32[4608,256]{1,0:T(8,128)S(1)} %bitcast.9, f32[2,8,256]{2,1,0:T(8,128)S(1)} %copy-done.13, f32[768,64]{1,0:T(8,128)S(1)} %bitcast.10, ...), custom_call_target="tpu_custom_call" | custom-call | tf_op jit(solution)/shard_map/load/pallas_call | solution.py:561
  16.0 2.2 %copy-done = f32[8,576,256]{2,1,0:T(8,128)} copy-done((f32[8,576,256]{2,1,0:T(8,128)}, f32[8,576,256]{2,1,0:T(8,128)S(1)}, u32[]{:S(2)}) %copy-start) | copy-done | bytes 4718616
  18.2 1.7 %copy-done.4 = f32[6,576,256]{2,1,0:T(8,128)} copy-done((f32[6,576,256]{2,1,0:T(8,128)}, f32[6,576,256]{2,1,0:T(8,128)S(1)}, u32[]{:S(2)}) %copy-start.4) | copy-done | bytes 3538968
  19.9 1.3 collective-permute-start.3
  21.2 3.1 %collective-permute-start.2 = (f32[576,256]{1,0:T(8,128)S(1)}, f32[576,256]{1,0:T(8,128)S(1)}, u32[]{:S(2)}, u32[]{:S(2)}) collective-permute-start(f32[576,256]{1,0:T(8,128)S(1)} %get-tuple-element.44.refs_6_.refs_11_), channel_id=1, source_target_pairs={{0,2},{2,4},{4,6},{6,8},{8,10},{10,12},{12,14},{1,3},{3,5},{5,7},{... | collective-permute-start | bytes 1769480 | tf_op jit(solution)/shard_map/ppermute | solution.py:542
  24.3 0.7 send.1
  25.0 0.7 copy-done.11
  26.3 7.9 %all-to-all-start = ((f32[32,8,128]{2,1,0:T(8,128)}), f32[32,8,128]{2,1,0:T(8,128)S(1)}, u32[]{:S(2)}, u32[]{:S(2)}) async-start(f32[32,8,128]{2,1,0:T(8,128)} %copy-done.11), calls=%async_computation | async-start | bytes 262144 | tf_op jit(solution)/shard_map/all_to_all | solution.py:559
  34.3 1.8 %collective-permute-start.4 = (f32[3,2,32,64]{3,2,1,0:T(8,128)}, f32[3,2,32,64]{3,2,1,0:T(8,128)}, u32[]{:S(2)}, u32[]{:S(2)}) collective-permute-start(f32[3,2,32,64]{3,2,1,0:T(8,128)} %copy-done.16), channel_id=1, source_target_pairs={{0,1},{1,0},{2,3},{3,2},{4,5},{5,4},{6,7},{7,6},{8,9},{9,8},{10,11... | collective-permute-start | bytes 147464 | tf_op jit(solution)/shard_map/ppermute | solution.py:550
  36.1 7.3 %all-to-all-done.got_ref = f32[32,8,128]{2,1,0:T(8,128)S(1)} async-done(((f32[32,8,128]{2,1,0:T(8,128)}), f32[32,8,128]{2,1,0:T(8,128)S(1)}, u32[]{:S(2)}, u32[]{:S(2)}) %all-to-all-start) | async-done | bytes 131104 | tf_op jit(solution)/shard_map/all_to_all | solution.py:559
  44.0 1.3 collective-permute-start.1
  45.3 3.0 %collective-permute-start = (f32[16,256]{1,0:T(8,128)S(1)}, f32[16,256]{1,0:T(8,128)S(1)}, u32[]{:S(2)}, u32[]{:S(2)}) collective-permute-start(f32[16,256]{1,0:T(8,128)S(1)} %get-tuple-element.40.refs_3_.refs_8_.rim_ref), channel_id=1, source_target_pairs={{0,2},{2,4},{4,6},{6,8},{8,10},{10,12},{12,14},{1,3},{3,5},{5,7},{... | collective-permute-start | bytes 49160 | tf_op jit(solution)/shard_map/ppermute | solution.py:542
  48.3 2.3 %copy-done.1 = f32[8,576,256]{2,1,0:T(8,128)S(1)} copy-done((f32[8,576,256]{2,1,0:T(8,128)S(1)}, f32[8,576,256]{2,1,0:T(8,128)}, u32[]{:S(2)}) %copy-start.1) | copy-done | bytes 4718616
  50.7 2.0 %copy-done.5 = f32[6,576,256]{2,1,0:T(8,128)S(1)} copy-done((f32[6,576,256]{2,1,0:T(8,128)S(1)}, f32[6,576,256]{2,1,0:T(8,128)}, u32[]{:S(2)}) %copy-start.5) | copy-done | bytes 3538968
  52.7 5.0 %middle0.1 = (f32[6,576,256]{2,1,0:T(8,128)S(1)}, f32[1,8,256]{2,1,0:T(8,128)S(1)}) custom-call(f32[2,576,16]{2,1,0:T(8,128)S(1)} %copy-done.3, f32[8,256]{1,0:T(8,128)S(1)} %get-tuple-element.38.refs_1_, f32[8,256]{1,0:T(8,128)S(1)} %get-tuple-element.39.refs_2_, f32[16,256]{1,0:T(8,128)S(1)} %get-tuple-element.40.refs_3_.refs_8_.rim_ref, ...), custom_call_target="tpu_custom_call" | custom-call | tf_op jit(solution)/shard_map/middle0/pallas_call | solution.py:592
  57.7 5.2 %edge0.1 = (f32[576,256]{1,0:T(8,128)S(1)}, f32[576,256]{1,0:T(8,128)S(1)}, f32[8,256]{1,0:T(8,128)S(1)}) custom-call(f32[2,576,16]{2,1,0:T(8,128)S(1)} %copy-done.3, f32[8,256]{1,0:T(8,128)S(1)} %get-tuple-element.38.refs_1_, f32[8,256]{1,0:T(8,128)S(1)} %get-tuple-element.39.refs_2_, f32[16,256]{1,0:T(8,128)S(1)} %get-tuple-element.40.refs_3_.refs_8_.rim_ref, ...), custom_call_target="tpu_custom_call" | custom-call | tf_op jit(solution)/shard_map/edge0/pallas_call | solution.py:610
  63.0 1.3 collective-permute-start.9
  64.3 3.1 %collective-permute-start.8 = (f32[576,256]{1,0:T(8,128)S(1)}, f32[576,256]{1,0:T(8,128)S(1)}, u32[]{:S(2)}, u32[]{:S(2)}) collective-permute-start(f32[576,256]{1,0:T(8,128)S(1)} %get-tuple-element.51.refs_9_.refs_11_), channel_id=1, source_target_pairs={{0,2},{2,4},{4,6},{6,8},{8,10},{10,12},{12,14},{1,3},{3,5},{5,7},{... | collective-permute-start | bytes 1769480 | tf_op jit(solution)/shard_map/ppermute | solution.py:542
  67.5 3.6 %collective-permute-done.5.refs_6_ = f32[8,256]{1,0:T(8,128)S(1)} collective-permute-done((f32[8,256]{1,0:T(8,128)S(1)}, f32[8,256]{1,0:T(8,128)S(1)}, u32[]{:S(2)}, u32[]{:S(2)}) %collective-permute-start.5) | collective-permute-done | bytes 8224 | tf_op jit(solution)/shard_map/ppermute | solution.py:550
  71.1 5.1 %middle1.1 = (f32[6,576,256]{2,1,0:T(8,128)S(1)}, f32[1,8,256]{2,1,0:T(8,128)S(1)}, f32[8,256]{1,0:T(8,128)S(1)}) custom-call(f32[2,576,16]{2,1,0:T(8,128)S(1)} %copy-done.3, f32[8,256]{1,0:T(8,128)S(1)} %get-tuple-element.38.refs_1_, f32[8,256]{1,0:T(8,128)S(1)} %get-tuple-element.39.refs_2_, f32[16,256]{1,0:T(8,128)S(1)} %get-tuple-element.40.refs_3_.refs_8_.rim_ref, ...), custom_call_target="tpu_custom_call" | custom-call | tf_op jit(solution)/shard_map/middle1/pallas_call | solution.py:592
  76.2 1.3 collective-permute-start.7
  77.5 3.1 %collective-permute-start.6 = (f32[8,256]{1,0:T(8,128)S(1)}, f32[8,256]{1,0:T(8,128)S(1)}, u32[]{:S(2)}, u32[]{:S(2)}) collective-permute-start(f32[8,256]{1,0:T(8,128)S(1)} %get-tuple-element.52.refs_3_), channel_id=1, source_target_pairs={{0,2},{2,4},{4,6},{6,8},{8,10},{10,12},{12,14},{1,3},{3,5},{5,7},{... | collective-permute-start | bytes 24584 | tf_op jit(solution)/shard_map/ppermute | solution.py:542
  80.6 0.8 collective-permute-done.6.refs_4_
  81.4 4.3 %edge1.1 = (f32[576,256]{1,0:T(8,128)S(1)}, f32[576,256]{1,0:T(8,128)S(1)}, f32[8,256]{1,0:T(8,128)S(1)}) custom-call(f32[2,576,16]{2,1,0:T(8,128)S(1)} %copy-done.3, f32[8,256]{1,0:T(8,128)S(1)} %get-tuple-element.38.refs_1_, f32[8,256]{1,0:T(8,128)S(1)} %get-tuple-element.39.refs_2_, f32[8,256]{1,0:T(8,128)S(1)} %get-tuple-element.52.refs_3_, ...), custom_call_target="tpu_custom_call" | custom-call | tf_op jit(solution)/shard_map/edge1/pallas_call | solution.py:610
  85.7 1.3 collective-permute-start.14
  87.0 4.3 %collective-permute-start.13 = (f32[576,256]{1,0:T(8,128)S(1)}, f32[576,256]{1,0:T(8,128)S(1)}, u32[]{:S(2)}, u32[]{:S(2)}) collective-permute-start(f32[576,256]{1,0:T(8,128)S(1)} %get-tuple-element.57.refs_9_.refs_11_), channel_id=1, source_target_pairs={{0,2},{2,4},{4,6},{6,8},{8,10},{10,12},{12,14},{1,3},{3,5},{5,7},{... | collective-permute-start | bytes 1769480 | tf_op jit(solution)/shard_map/ppermute | solution.py:542
  91.7 3.3 %collective-permute-done.10.refs_6_ = f32[8,256]{1,0:T(8,128)S(1)} collective-permute-done((f32[8,256]{1,0:T(8,128)S(1)}, f32[8,256]{1,0:T(8,128)S(1)}, u32[]{:S(2)}, u32[]{:S(2)}) %collective-permute-start.10) | collective-permute-done | bytes 8224 | tf_op jit(solution)/shard_map/ppermute | solution.py:550
  95.0 5.1 %middle2.1 = (f32[6,576,256]{2,1,0:T(8,128)S(1)}, f32[1,8,256]{2,1,0:T(8,128)S(1)}, f32[8,256]{1,0:T(8,128)S(1)}) custom-call(f32[2,576,16]{2,1,0:T(8,128)S(1)} %copy-done.3, f32[8,256]{1,0:T(8,128)S(1)} %get-tuple-element.38.refs_1_, f32[8,256]{1,0:T(8,128)S(1)} %get-tuple-element.39.refs_2_, f32[16,256]{1,0:T(8,128)S(1)} %get-tuple-element.40.refs_3_.refs_8_.rim_ref, ...), custom_call_target="tpu_custom_call" | custom-call | tf_op jit(solution)/shard_map/middle2/pallas_call | solution.py:592
  100.0 1.3 collective-permute-start.12
  101.3 3.6 %collective-permute-start.11 = (f32[8,256]{1,0:T(8,128)S(1)}, f32[8,256]{1,0:T(8,128)S(1)}, u32[]{:S(2)}, u32[]{:S(2)}) collective-permute-start(f32[8,256]{1,0:T(8,128)S(1)} %get-tuple-element.58.refs_3_), channel_id=1, source_target_pairs={{0,2},{2,4},{4,6},{6,8},{8,10},{10,12},{12,14},{1,3},{3,5},{5,7},{... | collective-permute-start | bytes 24584 | tf_op jit(solution)/shard_map/ppermute | solution.py:542
  105.0 0.8 collective-permute-done.11.refs_4_
  105.8 4.3 %edge2.1 = (f32[576,256]{1,0:T(8,128)S(1)}, f32[576,256]{1,0:T(8,128)S(1)}, f32[8,256]{1,0:T(8,128)S(1)}) custom-call(f32[2,576,16]{2,1,0:T(8,128)S(1)} %copy-done.3, f32[8,256]{1,0:T(8,128)S(1)} %get-tuple-element.38.refs_1_, f32[8,256]{1,0:T(8,128)S(1)} %get-tuple-element.39.refs_2_, f32[8,256]{1,0:T(8,128)S(1)} %get-tuple-element.58.refs_3_, ...), custom_call_target="tpu_custom_call" | custom-call | tf_op jit(solution)/shard_map/edge2/pallas_call | solution.py:610
  110.1 1.3 collective-permute-start.19
  111.4 5.3 %collective-permute-start.18 = (f32[576,256]{1,0:T(8,128)S(1)}, f32[576,256]{1,0:T(8,128)S(1)}, u32[]{:S(2)}, u32[]{:S(2)}) collective-permute-start(f32[576,256]{1,0:T(8,128)S(1)} %get-tuple-element.63.refs_9_.refs_11_), channel_id=1, source_target_pairs={{0,2},{2,4},{4,6},{6,8},{8,10},{10,12},{12,14},{1,3},{3,5},{5,7},{... | collective-permute-start | bytes 1769480 | tf_op jit(solution)/shard_map/ppermute | solution.py:542
  116.7 0.9 collective-permute-start.15
  117.7 2.8 %collective-permute-done.15.refs_6_ = f32[8,256]{1,0:T(8,128)S(1)} collective-permute-done((f32[8,256]{1,0:T(8,128)S(1)}, f32[8,256]{1,0:T(8,128)S(1)}, u32[]{:S(2)}, u32[]{:S(2)}) %collective-permute-start.15) | collective-permute-done | bytes 8224 | tf_op jit(solution)/shard_map/ppermute | solution.py:550
  120.4 6.3 %middle3.1 = (f32[6,576,256]{2,1,0:T(8,128)S(1)}, f32[5,8,256]{2,1,0:T(8,128)S(1)}, f32[8,256]{1,0:T(8,128)S(1)}) custom-call(f32[2,576,16]{2,1,0:T(8,128)S(1)} %copy-done.3, f32[8,256]{1,0:T(8,128)S(1)} %get-tuple-element.38.refs_1_, f32[8,256]{1,0:T(8,128)S(1)} %get-tuple-element.39.refs_2_, f32[16,256]{1,0:T(8,128)S(1)} %get-tuple-element.40.refs_3_.refs_8_.rim_ref, ...), custom_call_target="tpu_custom_call" | custom-call | tf_op jit(solution)/shard_map/middle3/pallas_call | solution.py:592
  126.7 1.3 collective-permute-start.17
  128.0 3.7 %collective-permute-start.16 = (f32[8,256]{1,0:T(8,128)S(1)}, f32[8,256]{1,0:T(8,128)S(1)}, u32[]{:S(2)}, u32[]{:S(2)}) collective-permute-start(f32[8,256]{1,0:T(8,128)S(1)} %get-tuple-element.64.refs_3_), channel_id=1, source_target_pairs={{0,2},{2,4},{4,6},{6,8},{8,10},{10,12},{12,14},{1,3},{3,5},{5,7},{... | collective-permute-start | bytes 24584 | tf_op jit(solution)/shard_map/ppermute | solution.py:542
  131.7 0.8 collective-permute-done.16.refs_4_
  132.6 5.2 %edge3.1 = (f32[576,256]{1,0:T(8,128)S(1)}, f32[576,256]{1,0:T(8,128)S(1)}, f32[32,8,256]{2,1,0:T(8,128)S(1)}) custom-call(f32[2,576,16]{2,1,0:T(8,128)S(1)} %copy-done.3, f32[8,256]{1,0:T(8,128)S(1)} %get-tuple-element.38.refs_1_, f32[8,256]{1,0:T(8,128)S(1)} %get-tuple-element.39.refs_2_, f32[8,256]{1,0:T(8,128)S(1)} %get-tuple-element.64.refs_3_, ...), custom_call_target="tpu_custom_call" | custom-call | tf_op jit(solution)/shard_map/edge3/pallas_call | solution.py:610
  137.7 23.1 %all_to_all.10.got_ref = f32[32,8,256]{2,1,0:T(8,128)S(1)} all-to-all(f32[32,8,256]{2,1,0:T(8,128)S(1)} %get-tuple-element.66), channel_id=1, replica_groups=mesh['grp'=2,'tile'=8,'spec'=2] {'grp','tile','spec'}, dimensions={0} | all-to-all | bytes 524288 | tf_op jit(solution)/shard_map/all_to_all | solution.py:622
  160.8 7.8 %last.1 = (f32[4608,256]{1,0:T(8,128)}, f32[3,8,32,64]{3,2,1,0:T(8,128)}) custom-call(f32[2,576,16]{2,1,0:T(8,128)S(1)} %copy-done.3, f32[2,3,12]{2,1,0:T(4,128)S(1)} %copy-done.14, f32[32,8,256]{2,1,0:T(8,128)S(1)} %all_to_all.10.got_ref, f32[16,256]{1,0:T(8,128)S(1)} %get-tuple-element.40.refs_3_.refs_8_.rim_ref, ...), custom_call_target="tpu_custom_call" | custom-call | tf_op jit(solution)/shard_map/last/pallas_call | solution.py:626
  (46 shorter events, 1.9 us)
Async XLA Ops:
  0.6 23.7 %copy-start.14 = (f32[2,3,12]{2,1,0:T(4,128)S(1)}, f32[2,3,12]{2,1,0:T(4,128)}, u32[]{:S(2)}) copy-start(f32[2,3,12]{2,1,0:T(4,128)} %constant.5.clone.level_ref) | copy-start | bytes 868
  0.6 1.1 copy-start.2
  1.7 2.3 %copy-start.6 = (f32[1,32,18,8,256]{4,3,2,1,0:T(8,128)S(1)}, f32[1,32,18,8,256]{4,3,2,1,0:T(8,128)}, u32[]{:S(2)}) copy-start(f32[1,32,18,8,256]{4,3,2,1,0:T(8,128)} %param.8) | copy-start | bytes 14155780
  4.1 1.0 copy-start.7
  5.0 0.7 copy-start.9
  5.8 0.7 copy-start.13
  6.5 17.8 %copy-start.8 = (f32[1,3,8,32,64]{4,3,2,1,0:T(8,128)S(1)}, f32[1,3,8,32,64]{4,3,2,1,0:T(8,128)}, u32[]{:S(2)}) copy-start(f32[1,3,8,32,64]{4,3,2,1,0:T(8,128)} %param.12) | copy-start | bytes 589828
  6.5 36.9 %copy-start.12 = (s32[8,256]{1,0:T(8,128)S(1)}, s32[8,256]{1,0:T(8,128)}, u32[]{:S(2)}) copy-start(s32[8,256]{1,0:T(8,128)} %refs_16_.1) | copy-start | bytes 24580
  6.5 36.9 %copy-start.15 = (s32[8,256]{1,0:T(8,128)S(1)}, s32[8,256]{1,0:T(8,128)}, u32[]{:S(2)}) copy-start(s32[8,256]{1,0:T(8,128)} %mask_ref.1) | copy-start | bytes 24580
  6.5 41.8 %copy-start.3 = (f32[2,576,16]{2,1,0:T(8,128)S(1)}, f32[2,576,16]{2,1,0:T(8,128)}, u32[]{:S(2)}) copy-start(f32[2,576,16]{2,1,0:T(8,128)} %constant.4.clone.table_ref.refs_0_) | copy-start | bytes 221188
  16.0 2.2 %copy-start = (f32[8,576,256]{2,1,0:T(8,128)}, f32[8,576,256]{2,1,0:T(8,128)S(1)}, u32[]{:S(2)}) copy-start(f32[8,576,256]{2,1,0:T(8,128)S(1)} %get-tuple-element.45.refs_7_.refs_14_.refs_10_) | copy-start | bytes 14155780
  18.2 1.8 %copy-start.4 = (f32[6,576,256]{2,1,0:T(8,128)}, f32[6,576,256]{2,1,0:T(8,128)S(1)}, u32[]{:S(2)}) copy-start(f32[6,576,256]{2,1,0:T(8,128)S(1)} %get-tuple-element.42.refs_4_.refs_9_) | copy-start | bytes 10616836
  19.9 37.8 %collective-permute-start.3 = (f32[576,256]{1,0:T(8,128)S(1)}, f32[576,256]{1,0:T(8,128)S(1)}, u32[]{:S(2)}, u32[]{:S(2)}) collective-permute-start(f32[576,256]{1,0:T(8,128)S(1)} %get-tuple-element.43.refs_5_.refs_10_), channel_id=1, source_target_pairs={{2,0},{4,2},{6,4},{8,6},{10,8},{12,10},{14,12},{3,1},{5,3},{7,5},{... | collective-permute-start | bytes 1769480 | tf_op jit(solution)/shard_map/ppermute | solution.py:545
  21.2 36.5 %collective-permute-start.2 = (f32[576,256]{1,0:T(8,128)S(1)}, f32[576,256]{1,0:T(8,128)S(1)}, u32[]{:S(2)}, u32[]{:S(2)}) collective-permute-start(f32[576,256]{1,0:T(8,128)S(1)} %get-tuple-element.44.refs_6_.refs_11_), channel_id=1, source_target_pairs={{0,2},{2,4},{4,6},{6,8},{8,10},{10,12},{12,14},{1,3},{3,5},{5,7},{... | collective-permute-start | bytes 1769480 | tf_op jit(solution)/shard_map/ppermute | solution.py:542
  25.0 0.7 copy-start.11
  25.7 0.6 copy-start.16
  26.3 17.1 %all-to-all-start = ((f32[32,8,128]{2,1,0:T(8,128)}), f32[32,8,128]{2,1,0:T(8,128)S(1)}, u32[]{:S(2)}, u32[]{:S(2)}) async-start(f32[32,8,128]{2,1,0:T(8,128)} %copy-done.11), calls=%async_computation | async-start | bytes 262144 | tf_op jit(solution)/shard_map/all_to_all | solution.py:559
  34.3 23.4 %collective-permute-start.4 = (f32[3,2,32,64]{3,2,1,0:T(8,128)}, f32[3,2,32,64]{3,2,1,0:T(8,128)}, u32[]{:S(2)}, u32[]{:S(2)}) collective-permute-start(f32[3,2,32,64]{3,2,1,0:T(8,128)} %copy-done.16), channel_id=1, source_target_pairs={{0,1},{1,0},{2,3},{3,2},{4,5},{5,4},{6,7},{7,6},{8,9},{9,8},{10,11... | collective-permute-start | bytes 147464 | tf_op jit(solution)/shard_map/ppermute | solution.py:550
  44.0 13.7 %collective-permute-start.1 = (f32[16,256]{1,0:T(8,128)S(1)}, f32[16,256]{1,0:T(8,128)S(1)}, u32[]{:S(2)}, u32[]{:S(2)}) collective-permute-start(f32[16,256]{1,0:T(8,128)S(1)} %get-tuple-element.40.refs_3_.refs_8_.rim_ref), channel_id=1, source_target_pairs={{2,0},{4,2},{6,4},{8,6},{10,8},{12,10},{14,12},{3,1},{5,3},{7,5},{... | collective-permute-start | bytes 49160 | tf_op jit(solution)/shard_map/ppermute | solution.py:545
  45.3 12.4 %collective-permute-start = (f32[16,256]{1,0:T(8,128)S(1)}, f32[16,256]{1,0:T(8,128)S(1)}, u32[]{:S(2)}, u32[]{:S(2)}) collective-permute-start(f32[16,256]{1,0:T(8,128)S(1)} %get-tuple-element.40.refs_3_.refs_8_.rim_ref), channel_id=1, source_target_pairs={{0,2},{2,4},{4,6},{6,8},{8,10},{10,12},{12,14},{1,3},{3,5},{5,7},{... | collective-permute-start | bytes 49160 | tf_op jit(solution)/shard_map/ppermute | solution.py:542
  48.3 2.3 %copy-start.1 = (f32[8,576,256]{2,1,0:T(8,128)S(1)}, f32[8,576,256]{2,1,0:T(8,128)}, u32[]{:S(2)}) copy-start(f32[8,576,256]{2,1,0:T(8,128)} %copy-done) | copy-start | bytes 14155780
  50.7 2.0 %copy-start.5 = (f32[6,576,256]{2,1,0:T(8,128)S(1)}, f32[6,576,256]{2,1,0:T(8,128)}, u32[]{:S(2)}) copy-start(f32[6,576,256]{2,1,0:T(8,128)} %copy-done.4) | copy-start | bytes 10616836
  52.7 18.4 %slice-start = ((s8[4718592]{0:T(1024)(128)(4,1)}), s8[4194304]{0:T(1024)(128)(4,1)S(1)}, s32[]{:S(2)}) async-start(s8[4718592]{0:T(1024)(128)(4,1)} %bitcast.7), calls=%async_computation.2 | async-start | bytes 8388608
  57.7 13.4 %slice-start.1 = ((s8[4718592]{0:T(1024)(128)(4,1)}), s8[524288]{0:T(1024)(128)(4,1)S(1)}, s32[]{:S(2)}) async-start(s8[4718592]{0:T(1024)(128)(4,1)} %bitcast.7), calls=%async_computation.3 | async-start | bytes 1048576
  63.0 18.4 %collective-permute-start.9 = (f32[576,256]{1,0:T(8,128)S(1)}, f32[576,256]{1,0:T(8,128)S(1)}, u32[]{:S(2)}, u32[]{:S(2)}) collective-permute-start(f32[576,256]{1,0:T(8,128)S(1)} %get-tuple-element.50.refs_8_.refs_10_), channel_id=1, source_target_pairs={{2,0},{4,2},{6,4},{8,6},{10,8},{12,10},{14,12},{3,1},{5,3},{7,5},{... | collective-permute-start | bytes 1769480 | tf_op jit(solution)/shard_map/ppermute | solution.py:545
  64.3 17.1 %collective-permute-start.8 = (f32[576,256]{1,0:T(8,128)S(1)}, f32[576,256]{1,0:T(8,128)S(1)}, u32[]{:S(2)}, u32[]{:S(2)}) collective-permute-start(f32[576,256]{1,0:T(8,128)S(1)} %get-tuple-element.51.refs_9_.refs_11_), channel_id=1, source_target_pairs={{0,2},{2,4},{4,6},{6,8},{8,10},{10,12},{12,14},{1,3},{3,5},{5,7},{... | collective-permute-start | bytes 1769480 | tf_op jit(solution)/shard_map/ppermute | solution.py:542
  67.4 3.7 %collective-permute-start.5 = (f32[8,256]{1,0:T(8,128)S(1)}, f32[8,256]{1,0:T(8,128)S(1)}, u32[]{:S(2)}, u32[]{:S(2)}) collective-permute-start(f32[8,256]{1,0:T(8,128)S(1)} %get-tuple-element.48.refs_5_), channel_id=1, source_target_pairs={{0,1},{1,0},{2,3},{3,2},{4,5},{5,4},{6,7},{7,6},{8,9},{9,8},{10,11... | collective-permute-start | bytes 24584 | tf_op jit(solution)/shard_map/ppermute | solution.py:550
  76.2 4.4 %collective-permute-start.7 = (f32[8,256]{1,0:T(8,128)S(1)}, f32[8,256]{1,0:T(8,128)S(1)}, u32[]{:S(2)}, u32[]{:S(2)}) collective-permute-start(f32[8,256]{1,0:T(8,128)S(1)} %get-tuple-element.52.refs_3_), channel_id=1, source_target_pairs={{2,0},{4,2},{6,4},{8,6},{10,8},{12,10},{14,12},{3,1},{5,3},{7,5},{... | collective-permute-start | bytes 24584 | tf_op jit(solution)/shard_map/ppermute | solution.py:545
  77.5 3.9 %collective-permute-start.6 = (f32[8,256]{1,0:T(8,128)S(1)}, f32[8,256]{1,0:T(8,128)S(1)}, u32[]{:S(2)}, u32[]{:S(2)}) collective-permute-start(f32[8,256]{1,0:T(8,128)S(1)} %get-tuple-element.52.refs_3_), channel_id=1, source_target_pairs={{0,2},{2,4},{4,6},{6,8},{8,10},{10,12},{12,14},{1,3},{3,5},{5,7},{... | collective-permute-start | bytes 24584 | tf_op jit(solution)/shard_map/ppermute | solution.py:542
  85.7 20.1 %collective-permute-start.14 = (f32[576,256]{1,0:T(8,128)S(1)}, f32[576,256]{1,0:T(8,128)S(1)}, u32[]{:S(2)}, u32[]{:S(2)}) collective-permute-start(f32[576,256]{1,0:T(8,128)S(1)} %get-tuple-element.56.refs_8_.refs_10_), channel_id=1, source_target_pairs={{2,0},{4,2},{6,4},{8,6},{10,8},{12,10},{14,12},{3,1},{5,3},{7,5},{... | collective-permute-start | bytes 1769480 | tf_op jit(solution)/shard_map/ppermute | solution.py:545
  87.0 18.8 %collective-permute-start.13 = (f32[576,256]{1,0:T(8,128)S(1)}, f32[576,256]{1,0:T(8,128)S(1)}, u32[]{:S(2)}, u32[]{:S(2)}) collective-permute-start(f32[576,256]{1,0:T(8,128)S(1)} %get-tuple-element.57.refs_9_.refs_11_), channel_id=1, source_target_pairs={{0,2},{2,4},{4,6},{6,8},{8,10},{10,12},{12,14},{1,3},{3,5},{5,7},{... | collective-permute-start | bytes 1769480 | tf_op jit(solution)/shard_map/ppermute | solution.py:542
  91.3 3.7 %collective-permute-start.10 = (f32[8,256]{1,0:T(8,128)S(1)}, f32[8,256]{1,0:T(8,128)S(1)}, u32[]{:S(2)}, u32[]{:S(2)}) collective-permute-start(f32[8,256]{1,0:T(8,128)S(1)} %get-tuple-element.54.refs_5_), channel_id=1, source_target_pairs={{0,1},{1,0},{2,3},{3,2},{4,5},{5,4},{6,7},{7,6},{8,9},{9,8},{10,11... | collective-permute-start | bytes 24584 | tf_op jit(solution)/shard_map/ppermute | solution.py:550
  100.0 4.9 %collective-permute-start.12 = (f32[8,256]{1,0:T(8,128)S(1)}, f32[8,256]{1,0:T(8,128)S(1)}, u32[]{:S(2)}, u32[]{:S(2)}) collective-permute-start(f32[8,256]{1,0:T(8,128)S(1)} %get-tuple-element.58.refs_3_), channel_id=1, source_target_pairs={{2,0},{4,2},{6,4},{8,6},{10,8},{12,10},{14,12},{3,1},{5,3},{7,5},{... | collective-permute-start | bytes 24584 | tf_op jit(solution)/shard_map/ppermute | solution.py:545
  101.3 4.5 %collective-permute-start.11 = (f32[8,256]{1,0:T(8,128)S(1)}, f32[8,256]{1,0:T(8,128)S(1)}, u32[]{:S(2)}, u32[]{:S(2)}) collective-permute-start(f32[8,256]{1,0:T(8,128)S(1)} %get-tuple-element.58.refs_3_), channel_id=1, source_target_pairs={{0,2},{2,4},{4,6},{6,8},{8,10},{10,12},{12,14},{1,3},{3,5},{5,7},{... | collective-permute-start | bytes 24584 | tf_op jit(solution)/shard_map/ppermute | solution.py:542
  110.1 22.5 %collective-permute-start.19 = (f32[576,256]{1,0:T(8,128)S(1)}, f32[576,256]{1,0:T(8,128)S(1)}, u32[]{:S(2)}, u32[]{:S(2)}) collective-permute-start(f32[576,256]{1,0:T(8,128)S(1)} %get-tuple-element.62.refs_8_.refs_10_), channel_id=1, source_target_pairs={{2,0},{4,2},{6,4},{8,6},{10,8},{12,10},{14,12},{3,1},{5,3},{7,5},{... | collective-permute-start | bytes 1769480 | tf_op jit(solution)/shard_map/ppermute | solution.py:545
  111.4 21.2 %collective-permute-start.18 = (f32[576,256]{1,0:T(8,128)S(1)}, f32[576,256]{1,0:T(8,128)S(1)}, u32[]{:S(2)}, u32[]{:S(2)}) collective-permute-start(f32[576,256]{1,0:T(8,128)S(1)} %get-tuple-element.63.refs_9_.refs_11_), channel_id=1, source_target_pairs={{0,2},{2,4},{4,6},{6,8},{8,10},{10,12},{12,14},{1,3},{3,5},{5,7},{... | collective-permute-start | bytes 1769480 | tf_op jit(solution)/shard_map/ppermute | solution.py:542
  116.7 3.7 %collective-permute-start.15 = (f32[8,256]{1,0:T(8,128)S(1)}, f32[8,256]{1,0:T(8,128)S(1)}, u32[]{:S(2)}, u32[]{:S(2)}) collective-permute-start(f32[8,256]{1,0:T(8,128)S(1)} %get-tuple-element.60.refs_5_), channel_id=1, source_target_pairs={{0,1},{1,0},{2,3},{3,2},{4,5},{5,4},{6,7},{7,6},{8,9},{9,8},{10,11... | collective-permute-start | bytes 24584 | tf_op jit(solution)/shard_map/ppermute | solution.py:550
  126.7 5.0 %collective-permute-start.17 = (f32[8,256]{1,0:T(8,128)S(1)}, f32[8,256]{1,0:T(8,128)S(1)}, u32[]{:S(2)}, u32[]{:S(2)}) collective-permute-start(f32[8,256]{1,0:T(8,128)S(1)} %get-tuple-element.64.refs_3_), channel_id=1, source_target_pairs={{2,0},{4,2},{6,4},{8,6},{10,8},{12,10},{14,12},{3,1},{5,3},{7,5},{... | collective-permute-start | bytes 24584 | tf_op jit(solution)/shard_map/ppermute | solution.py:545
  128.0 4.5 %collective-permute-start.16 = (f32[8,256]{1,0:T(8,128)S(1)}, f32[8,256]{1,0:T(8,128)S(1)}, u32[]{:S(2)}, u32[]{:S(2)}) collective-permute-start(f32[8,256]{1,0:T(8,128)S(1)} %get-tuple-element.64.refs_3_), channel_id=1, source_target_pairs={{0,2},{2,4},{4,6},{6,8},{8,10},{10,12},{12,14},{1,3},{3,5},{5,7},{... | collective-permute-start | bytes 24584 | tf_op jit(solution)/shard_map/ppermute | solution.py:542
  132.5 28.3 %copy-start.10 = (f32[1,32,64]{2,1,0:T(8,128)S(1)}, f32[1,32,64]{2,1,0:T(8,128)}, u32[]{:S(2)}) copy-start(f32[1,32,64]{2,1,0:T(8,128)} %param.13) | copy-start | bytes 24580
where the time goes:
time: 170 us; the launch traced here: 169 us
  Pallas kernels  59 us (35%)
  starting transfers between devices  50.8 us (30%)
  blocking collectives  23.1 us (14%)
  waiting for transfers between devices  19.4 us (11%)
  local copies, waits for them, and re-layouts  15.4 us (9%)
    ppermute x8, starting transfers between devices, up(): return lax.ppermute(x, 'tile', [(i, i + 1) for i in range(t_n - 1)])  29.2 us
    all_to_all x1, blocking collectives, body(): landed = lax.all_to_all(total, AXES, 0, 0, tiled=True)  23.1 us
    pallas_call x4, Pallas kernels, body(): pl.pallas_call(functools.partial(middle_kernel, (rows, fd, nx), begin, su...  21.4 us
    pallas_call x4, Pallas kernels, body(): pl.pallas_call(functools.partial(edge_kernel, (rows, fd, nx, t_n, s_n, co...  19 us
    unnamed x38, local copies, waits for them, and re-layouts  15.4 us
    ppermute x8, starting transfers between devices, down(): return lax.ppermute(x, 'tile', [(i + 1, i) for i in range(t_n - 1)])  10.3 us
    ppermute x4, waiting for transfers between devices, others(): got = lax.ppermute(x, 'spec', [(i, (i + k) % s_n) for i in range(s_n)])  9.65 us
    pallas_call x1, Pallas kernels, body(): pl.pallas_call(functools.partial(load_kernel, (rows, fd, nx, cols, own, c...  9.49 us
  transfers between devices with their start and end apart: 21, of which 7 were waited for; matrix products, arithmetic and copies ran while one was open for 0% of the time, Pallas kernels for 13%

commit v1 on v0

--- a/solution.py
+++ b/solution.py
@@ -20,7 +20,7 @@
 
 VM = pl.BlockSpec(memory_space=pltpu.VMEM)
 SM = pl.BlockSpec(memory_space=pltpu.SMEM)
-HB = pl.BlockSpec(memory_space=pl.ANY)
+HB = pl.BlockSpec(memory_space=pltpu.HBM)
 
 
 def f32(*shape):
@@ -90,20 +90,34 @@
     return values
 
 
-def send_kernel(n, level_ref, ocean_ref, sea_ref, out_ref, rim_ref):
-    t_n, s_n, rows, cols, own, ny = n
+def start_kernel(n, level_ref, spectrum_ref, ocean_hbm, sea_hbm, out_ref, rim_ref, lo_ref, hi_ref, raw, ocean, sea, sem):
+    t_n, s_n, rows, cols, own, ny, fd, nx, chunks = n
     s = lax.axis_index("spec")
     pad = -(-ny // LANES) * LANES
+    part = fd // chunks
+    first = [
+        pltpu.make_async_copy(ocean_hbm, ocean, sem.at[chunks]),
+        pltpu.make_async_copy(sea_hbm, sea, sem.at[chunks + 1]),
+    ]
+    copies = [
+        pltpu.make_async_copy(spectrum_ref.at[pl.ds(c * part, part)], raw.at[pl.ds(c * part, part)], sem.at[c])
+        for c in range(chunks)
+    ]
+    for copy in first + copies:
+        copy.start()
+    for copy in first:
+        copy.wait()
     parts = []
     for c in range(2):
         total = None
         for k in range(own):
-            term = level_ref[s, 0, k] * ocean_ref[c, k]
+            term = level_ref[s, 0, k] * ocean[c * own + k]
             total = term if total is None else total + term
         parts.append(total)
-    parts.append(jnp.where(s == 0, sea_ref[...], 0.0))
+    parts.append(jnp.where(s == 0, sea[...], 0.0))
     for c in range(3):
-        rim_ref[c] = jnp.where(s == 0, ocean_ref[c, own - 2 : own], ocean_ref[c, 0:2])
+        for k in range(2):
+            rim_ref[c, k] = jnp.where(s == 0, ocean[c * own + own - 2 + k], ocean[c * own + k])
     stack = jnp.concatenate(parts, axis=0)
     stack = jnp.pad(stack, ((0, LANES - 3 * cols), (0, pad - ny)))
     turned = jnp.transpose(stack)
@@ -111,57 +125,18 @@
         for q in range(s_n):
             out_ref[t * s_n + q] = turned[t * rows : (t + 1) * rows, : 4 * cols]
 
-
-def load_kernel(n, table_ref, spectrum_ref, wind_ref, ocean_ref, sea_ref, mid_ref, lo_ref, hi_ref, growth_ref, raw, windb, sem):
-    rows, fd, nx, cols, own, chunks = n
-    s = lax.axis_index("spec")
-    part = fd * rows // chunks
-    copies = []
-    halves = nx // LANES
     for c in range(chunks):
-        span = pl.ds(c * part, part)
-        for h in range(halves):
-            copy = pltpu.make_async_copy(spectrum_ref.at[span, half(h)], raw.at[h, span], sem.at[c, h])
-            copy.start()
-            copies.append(copy)
-    for c in range(2):
-        for r in range(rows):
-            windb[c, r] = jnp.broadcast_to(wind_ref[c, r : r + 1], (SUB, nx))
-
-    def grow(i, carry):
-        for k in range(2):
-            sl = pl.ds(pl.multiple_of(i * 2 * SUB + k * SUB, SUB), SUB)
-            we, wn = wide(table_ref[s, sl, WE : WE + 1]), wide(table_ref[s, sl, WN : WN + 1])
-            for r in range(rows):
-                for h in range(nx // LANES):
-                    drive = we * windb[0, r, :, half(h)] + wn * windb[1, r, :, half(h)]
-                    growth_ref[r, sl, half(h)] = 1.0 + jnp.maximum(drive - 0.05, 0.0)
-        return carry
-
-    lax.fori_loop(0, fd // (2 * SUB), grow, 0)
-    for c in range(chunks):
-        for h in range(halves):
-            copies[c * halves + h].wait()
-        count = fd // chunks
+        copies[c].wait()
 
         def turn(i, carry):
-            at = pl.multiple_of(c * count + i * SUB, SUB)
-            sl = pl.ds(at, SUB)
-            bw = wide(table_ref[s, sl, BW : BW + 1])
-            for r in range(rows):
-                for h in range(nx // LANES):
-                    value = bw * raw[h, pl.ds(at * rows + r, SUB, stride=rows), :]
-                    if r == 0:
-                        lo_ref[sl, half(h)] = value
-                    elif r == rows - 1:
-                        hi_ref[sl, half(h)] = value
-                    else:
-                        mid_ref[r - 1, sl, half(h)] = value
+            sl = pl.ds(pl.multiple_of(c * part + i * SUB, SUB), SUB)
+            for h in range(nx // LANES):
+                planes = jnp.swapaxes(raw[sl, :, half(h)], 0, 1)
+                lo_ref[sl, half(h)] = planes[0]
+                hi_ref[sl, half(h)] = planes[rows - 1]
             return carry
 
-        lax.fori_loop(0, count // SUB, turn, 0)
-
-    ny = ocean_ref.shape[1]
+        lax.fori_loop(0, part // SUB, turn, 0)
 
     @pl.when(lax.axis_index("grp") == 1)
     def _():
@@ -169,8 +144,8 @@
         for k in range(2):
             for ref, at in ((lo_ref, k), (hi_ref, cols - 2 + k)):
                 for m in range(stack):
-                    ref[k * stack + m : k * stack + m + 1, 0:ny] = ocean_ref[m * cols + at : m * cols + at + 1, :]
-                ref[2 * stack + k : 2 * stack + k + 1, 0:ny] = sea_ref[at : at + 1, :]
+                    ref[k * stack + m : k * stack + m + 1, 0:ny] = ocean[m, at : at + 1, :]
+                ref[2 * stack + k : 2 * stack + k + 1, 0:ny] = sea[at : at + 1, :]
 
 
 def pick_kernel(n, got_ref, mask_ref, cross_ref, u_ref, v_ref, depth_ref, rim_ref):
@@ -198,15 +173,18 @@
     depth_ref[...] = 25.0 / (depth * depth)
     rim_ref[0:rows] = mask_ref[...].astype(jnp.float32)
     rim_ref[rows : 2 * rows] = 0.1 * v
-
-
-def advance(segments, fd, nx, s, table_ref, energy, growth, store, splat, acc, sums):
+    rim_ref[2 * rows : 3 * rows] = 25.0 / (depth * depth)
+
+
+def advance(segments, fd, nx, s, table_ref, planes, store, splat, acc, sums, before=None):
     halves = nx // LANES
     lane = lanes_of((SUB, LANES))
     first, last = lane == 0, lane == LANES - 1
     acc[...] = jnp.zeros(acc.shape, jnp.float32)
 
     def body(i, carry):
+        if before is not None:
+            before(i)
         totals = {}
 
         def add(key, value):
@@ -216,9 +194,10 @@
             sl = pl.ds(pl.multiple_of((i * UNROLL + k) * SUB, SUB), SUB)
             ge, gn = wide(table_ref[s, sl, GE : GE + 1]), wide(table_ref[s, sl, GN : GN + 1])
             bands = [wide(table_ref[s, sl, b : b + 1]) for b in (SX, SY, DX, DY)] if sums else None
+            energy, growth = planes(sl)
             for segment in segments:
                 def state(r):
-                    e = [energy(r, sl, h) * splat[2, r + 1, :, half(h)] for h in range(halves)]
+                    e = [energy(r, h) * splat[2, r + 1, :, half(h)] for h in range(halves)]
                     north = [(gn + splat[1, r + 1, :, half(h)]) * e[h] for h in range(halves)]
                     return e, north
 
@@ -239,7 +218,7 @@
                     for h in range(halves):
                         behind = jnp.where(first, right[h - 1] if h else jnp.minimum(east[0], 0.0), right[h])
                         advected = (e[h] - (flux[h] - behind)) - (upper[h] - flow[h])
-                        g = growth(r, sl, h)
+                        g = growth(r, h)
                         add((0, r, h), advected)
                         if sums:
                             pushed = (g - 1.0) * advected
@@ -266,76 +245,137 @@
     splat[kind, row + 1] = jnp.broadcast_to(value, (SUB, nx))
 
 
-def middle_kernel(n, begin, sums, *refs):
+def first_middle_kernel(n, table_ref, u_ref, v_ref, rim_ref, wind_ref, spectrum_ref,
+                        out_ref, total_ref, growth_ref, inner_ref, raw, windb, splat, acc, sem):
+    rows, fd, nx, chunks = n
+    s = lax.axis_index("spec")
+    part = fd // chunks
+    turns = part // (SUB * UNROLL)
+
+    def copy(c):
+        span = pl.ds(pl.multiple_of(c * part, SUB), part)
+        return pltpu.make_async_copy(spectrum_ref.at[span], raw.at[span], sem.at[c])
+
+    for c in range(chunks):
+        copy(c).start()
+    for c in range(2):
+        for r in range(rows):
+            windb[c, r] = jnp.broadcast_to(wind_ref[c, r : r + 1], (SUB, nx))
+    for r in range(rows):
+        fill(splat, 0, r, u_ref[r : r + 1], nx)
+        fill(splat, 1, r, v_ref[r : r + 1], nx)
+        fill(splat, 2, r, rim_ref[r : r + 1], nx)
+
+    def before(i):
+        @pl.when(i % turns == 0)
+        def _():
+            copy(i // turns).wait()
+
+    def planes(sl):
+        bw, we, wn = [wide(table_ref[s, sl, b : b + 1]) for b in (BW, WE, WN)]
+        natural, grown = {}, {}
+        for h in range(nx // LANES):
+            natural[h] = jnp.swapaxes(raw[sl, :, half(h)], 0, 1)
+            inner_ref[0, sl, half(h)] = natural[h][1]
+            inner_ref[1, sl, half(h)] = natural[h][rows - 2]
+            for r in range(rows):
+                drive = we * windb[0, r, :, half(h)] + wn * windb[1, r, :, half(h)]
+                grown[r, h] = 1.0 + jnp.maximum(drive - 0.05, 0.0)
+                growth_ref[r, sl, half(h)] = grown[r, h]
+        return lambda r, h: bw * natural[h][r], lambda r, h: grown[r, h]
+
+    def store(r, sl, h, value):
+        out_ref[r - 1, sl, half(h)] = value
+
+    inner = list(range(1, rows - 1))
+    advance([inner], fd, nx, s, table_ref, planes, store, splat, acc, False, before)
+    finish_middle(inner, nx, acc, total_ref)
+
+
+def finish_middle(inner, nx, acc, total_ref):
+    zero = jnp.zeros((1, nx), jnp.float32)
+    for kind in range(acc.shape[0]):
+        total_ref[kind] = jnp.concatenate([zero] + folded(acc, kind, inner) + [zero], axis=0)
+
+
+def middle_kernel(n, sums, table_ref, u_ref, v_ref, rim_ref, depth_ref, own_ref, got_ref, mid_ref, lo_ref, hi_ref,
+                  growth_ref, out_ref, total_ref, breaking_ref, splat, acc):
     rows, fd, nx = n
-    table_ref, u_ref, v_ref, *refs = refs
     s = lax.axis_index("spec")
-    if begin:
-        rim_ref, mid_ref, lo_ref, hi_ref, growth_ref, out_ref, total_ref, splat, acc = refs
-        breaking = rim_ref[0:rows]
-    else:
-        (rim_ref, depth_ref, own_ref, got_ref, mid_ref, lo_ref, hi_ref, growth_ref,
-         out_ref, total_ref, breaking_ref, splat, acc) = refs
-        wet = rim_ref[0:rows]
-        breaking = wet / (1.0 + (own_ref[...] + got_ref[...]) * depth_ref[...])
-        breaking_ref[...] = breaking
+    breaking = rim_ref[0:rows] / (1.0 + (own_ref[...] + got_ref[...]) * depth_ref[...])
+    breaking_ref[...] = breaking
     for r in range(rows):
         fill(splat, 0, r, u_ref[r : r + 1], nx)
         fill(splat, 1, r, v_ref[r : r + 1], nx)
         fill(splat, 2, r, breaking[r : r + 1], nx)
 
-    def energy(r, sl, h):
-        if r == 0:
-            return lo_ref[sl, half(h)]
-        if r == rows - 1:
-            return hi_ref[sl, half(h)]
-        return mid_ref[r - 1, sl, half(h)]
+    def planes(sl):
+        def energy(r, h):
+            if r == 0:
+                return lo_ref[sl, half(h)]
+            if r == rows - 1:
+                return hi_ref[sl, half(h)]
+            return mid_ref[r - 1, sl, half(h)]
+
+        return energy, lambda r, h: growth_ref[r, sl, half(h)]
 
     def store(r, sl, h, value):
         out_ref[r - 1, sl, half(h)] = value
 
     inner = list(range(1, rows - 1))
-    advance([inner], fd, nx, s, table_ref, energy, lambda r, sl, h: growth_ref[r, sl, half(h)], store, splat, acc, sums)
-    zero = jnp.zeros((1, nx), jnp.float32)
-    for kind in range(acc.shape[0]):
-        total_ref[kind] = jnp.concatenate([zero] + folded(acc, kind, inner) + [zero], axis=0)
+    advance([inner], fd, nx, s, table_ref, planes, store, splat, acc, sums)
+    finish_middle(inner, nx, acc, total_ref)
 
 
 def edge_kernel(n, begin, sums, *refs):
     rows, fd, nx, t_n, s_n, cols, own = n
-    (table_ref, u_ref, v_ref, breaking_ref, below_ref, above_ref, vb_ref, va_ref, rim_ref, mid_ref, lo_ref, hi_ref,
+    (table_ref, u_ref, v_ref, breaking_ref, vb_ref, va_ref, rim_ref, mid_ref, lo_ref, hi_ref,
      hb_ref, ha_ref, growth_ref, part_ref, *refs) = refs
     s = lax.axis_index("spec")
     if begin:
         level_ref, newlo_ref, newhi_ref, total_ref, splat, acc = refs
     elif sums:
-        cross_ref, newlo_ref, newhi_ref, send_ref, splat, acc = refs
+        cb_ref, ca_ref, cross_ref, newlo_ref, newhi_ref, send_ref, splat, acc = refs
     else:
-        newlo_ref, newhi_ref, total_ref, splat, acc = refs
+        cb_ref, ca_ref, newlo_ref, newhi_ref, total_ref, splat, acc = refs
     for r in (0, 1, rows - 2, rows - 1):
         fill(splat, 0, r, u_ref[r : r + 1], nx)
         fill(splat, 1, r, v_ref[r : r + 1], nx)
         fill(splat, 2, r, breaking_ref[r : r + 1], nx)
+    below, above = vb_ref[rows - 1 : rows], va_ref[0:1]
+    if not begin:
+        low = hb_ref[fd : fd + 1] + cb_ref[rows - 1 : rows]
+        high = ha_ref[fd : fd + 1] + ca_ref[0:1]
+        below = below / (1.0 + low * vb_ref[3 * rows - 1 : 3 * rows])
+        above = above / (1.0 + high * va_ref[2 * rows : 2 * rows + 1])
     fill(splat, 1, -1, vb_ref[2 * rows - 1 : 2 * rows], nx)
-    fill(splat, 2, -1, below_ref[rows - 1 : rows], nx)
+    fill(splat, 2, -1, below, nx)
     fill(splat, 1, rows, va_ref[rows : rows + 1], nx)
-    fill(splat, 2, rows, above_ref[0:1], nx)
-
-    def energy(r, sl, h):
-        if r == -1:
-            return hb_ref[sl, half(h)]
-        if r == rows:
-            return ha_ref[sl, half(h)]
-        if r == 0:
-            return lo_ref[sl, half(h)]
-        if r == rows - 1:
-            return hi_ref[sl, half(h)]
-        return mid_ref[r - 1, sl, half(h)]
+    fill(splat, 2, rows, above, nx)
+
+    def planes(sl):
+        bw = wide(table_ref[s, sl, BW : BW + 1]) if begin else None
+
+        def plane(r, h):
+            if r == -1:
+                return hb_ref[sl, half(h)]
+            if r == rows:
+                return ha_ref[sl, half(h)]
+            if r == 0:
+                return lo_ref[sl, half(h)]
+            if r == rows - 1:
+                return hi_ref[sl, half(h)]
+            return mid_ref[(0 if r == 1 else 1) if begin else r - 1, sl, half(h)]
+
+        def energy(r, h):
+            return bw * plane(r, h) if begin else plane(r, h)
+
+        return energy, lambda r, h: growth_ref[r, sl, half(h)]
 
     def store(r, sl, h, value):
         (newlo_ref if r == 0 else newhi_ref)[sl, half(h)] = value
 
-    advance([[0], [rows - 1]], fd, nx, s, table_ref, energy, lambda r, sl, h: growth_ref[r, sl, half(h)], store, splat, acc, sums)
+    advance([[0], [rows - 1]], fd, nx, s, table_ref, planes, store, splat, acc, sums)
     zero = jnp.zeros((rows - 2, nx), jnp.float32)
     kinds = []
     for kind in range(acc.shape[0]):
@@ -343,6 +383,8 @@
         kinds.append(part_ref[kind] + jnp.concatenate([low, zero, high], axis=0))
     if not sums:
         total_ref[...] = kinds[0]
+        newlo_ref[fd : fd + SUB] = jnp.broadcast_to(kinds[0][0:1], (SUB, nx))
+        newhi_ref[fd : fd + SUB] = jnp.broadcast_to(kinds[0][rows - 1 : rows], (SUB, nx))
     if begin:
         ny = level_ref.shape[1]
 
@@ -379,19 +421,12 @@
     s = lax.axis_index("spec")
     g = lax.axis_index("grp")
     tile = lax.axis_index("tile")
-    part = fd * rows // chunks
-    count = fd // chunks
+    part = fd // chunks
     pad = turn.shape[0]
     size = cols + 8
 
-    halves = nx // LANES
-
-    def writes(c, source):
-        return [
-            pltpu.make_async_copy(
-                raw.at[h, pl.ds(source * part, part)], waves_ref.at[pl.ds(c * part, part), half(h)], sem.at[c, h])
-            for h in range(halves)
-        ]
+    def write(c, source):
+        return pltpu.make_async_copy(raw.at[pl.ds(source * part, part)], waves_ref.at[pl.ds(c * part, part)], sem.at[c])
 
     ocean_copy = pltpu.make_async_copy(out, next_ref, osem)
 
@@ -406,41 +441,33 @@
         for c in range(chunks):
 
             def finish(i, carry):
-                at = pl.multiple_of(c * count + i * SUB, SUB)
-                sl = pl.ds(at, SUB)
+                sl = pl.ds(pl.multiple_of(c * part + i * SUB, SUB), SUB)
                 inv = wide(table_ref[s, sl, INV : INV + 1])
-                for r in range(rows):
-                    for h in range(nx // LANES):
-                        if r == 0:
-                            value = lo_ref[sl, half(h)]
-                        elif r == rows - 1:
-                            value = hi_ref[sl, half(h)]
-                        else:
-                            value = mid_ref[r - 1, sl, half(h)]
-                        raw[h, pl.ds(at * rows + r, SUB, stride=rows), :] = value * brk[r, :, half(h)] * inv
+                for h in range(nx // LANES):
+                    values = [lo_ref[sl, half(h)]]
+                    values += [mid_ref[r, sl, half(h)] for r in range(rows - 2)]
+                    values += [hi_ref[sl, half(h)]]
+                    values = [value * brk[r, :, half(h)] * inv for r, value in enumerate(values)]
+                    raw[sl, :, half(h)] = jnp.swapaxes(jnp.stack(values), 0, 1)
                 return carry
 
-            lax.fori_loop(0, count // SUB, finish, 0)
-            for copy in writes(c, c):
-                copy.start()
+            lax.fori_loop(0, part // SUB, finish, 0)
+            write(c, c).start()
         out[...] = jnp.zeros((3, own, cols, ny), jnp.float32)
         ocean_copy.start()
         ocean_copy.wait()
         for c in range(chunks):
-            for copy in writes(c, c):
-                copy.wait()
+            write(c, c).wait()
 
     @pl.when(g == 1)
     def _():
         def clear(i, carry):
-            for h in range(halves):
-                raw[h, pl.ds(pl.multiple_of(i * 64, 64), 64), :] = jnp.zeros((64, LANES), jnp.float32)
+            raw[pl.ds(pl.multiple_of(i * SUB, SUB), SUB)] = jnp.zeros((SUB, rows, nx), jnp.float32)
             return carry
 
-        lax.fori_loop(0, part // 64, clear, 0)
+        lax.fori_loop(0, part // SUB, clear, 0)
         for c in range(chunks):
-            for copy in writes(c, 0):
-                copy.start()
+            write(c, 0).start()
 
         if pad > ny:
             turn[ny:pad] = jnp.zeros((pad - ny, nx), jnp.float32)
@@ -519,8 +546,7 @@
         ocean_copy.start()
         ocean_copy.wait()
         for c in range(chunks):
-            for copy in writes(c, 0):
-                copy.wait()
+            write(c, 0).wait()
 
 
 def body(spectrum, wind, land_mask, intersection, ocean_state, sea_level, *, mesh_shape):
@@ -533,9 +559,13 @@
     levels = jnp.asarray(level_table(own * s_n, s_n, own))
     ocean = ocean_state[0]
     sea = sea_level[0]
-    natural = spectrum.reshape(fd * rows, nx)
-    flat = ocean_state.reshape(3 * own * cols, ny)
-    chunks = 8
+
+    def in_hbm(x):
+        return pltpu.with_memory_space_constraint(x, pltpu.HBM)
+
+    natural = in_hbm(spectrum.reshape(fd, rows, nx))
+    chunks = 6
+    vm = pltpu.VMEM
     params = pltpu.CompilerParams(vmem_limit_bytes=24 << 20)
 
     def up(x):
@@ -545,77 +575,78 @@
         return lax.ppermute(x, "tile", [(i + 1, i) for i in range(t_n - 1)])
 
     def others(x):
-        result = None
-        for k in range(1, s_n):
-            got = lax.ppermute(x, "spec", [(i, (i + k) % s_n) for i in range(s_n)])
-            result = got if result is None else result + got
-        return result
-
-    send, level_rim = pl.pallas_call(
-        functools.partial(send_kernel, (t_n, s_n, rows, cols, own, ny)),
-        out_shape=(f32(devices, rows, 4 * cols), f32(3, 2, cols, ny)),
-        in_specs=[SM, VM, VM], out_specs=(VM, VM), compiler_params=params, name="send",
-    )(levels, ocean, sea)
+        return added(lax.ppermute(x, "spec", [(i, (i + k) % s_n) for i in range(s_n)]) for k in range(1, s_n))
+
+    def crossed(x, step):
+        tiles = [(i, i + step) for i in range(t_n) if 0 <= i + step < t_n]
+        return added(
+            lax.ppermute(x, ("tile", "spec"), [(a * s_n + q, b * s_n + (q + k) % s_n) for a, b in tiles for q in range(s_n)])
+            for k in range(1, s_n)
+        )
+
+    def added(values):
+        return functools.reduce(lambda a, b: a + b, values)
+
+    def call(kernel, name, args, specs, shapes, out_specs, scratch):
+        return pl.pallas_call(
+            kernel, out_shape=shapes, in_specs=specs, out_specs=out_specs,
+            scratch_shapes=scratch, compiler_params=params, name=name,
+        )(*args)
+
+    send, level_rim, lo, hi = call(
+        functools.partial(start_kernel, (t_n, s_n, rows, cols, own, ny, fd, nx, chunks)), "start",
+        (levels, natural, in_hbm(ocean.reshape(3 * own, cols, ny)), in_hbm(sea)), [SM, HB, HB, HB],
+        (f32(devices, rows, 4 * cols), f32(3, 2, cols, ny), f32(fd, nx), f32(fd, nx)), (VM,) * 4,
+        [vm((fd, rows, nx), jnp.float32), vm((3 * own, cols, ny), jnp.float32), vm((cols, ny), jnp.float32),
+         pltpu.SemaphoreType.DMA((chunks + 2,))],
+    )
     arrived = lax.all_to_all(send, AXES, 0, 0, tiled=True)
-
-    mid, lo, hi, growth = pl.pallas_call(
-        functools.partial(load_kernel, (rows, fd, nx, cols, own, chunks)),
-        out_shape=(f32(rows - 2, fd, nx), f32(fd, nx), f32(fd, nx), f32(rows, fd, nx)),
-        in_specs=[VM, HB, VM, VM, VM], out_specs=(VM,) * 4,
-        scratch_shapes=[pltpu.VMEM((nx // LANES, fd * rows, LANES), jnp.float32), pltpu.VMEM((2, rows, SUB, nx), jnp.float32),
-                        pltpu.SemaphoreType.DMA((chunks, nx // LANES))],
-        compiler_params=params, name="load",
-    )(table, natural, wind, flat, sea)
     hb, ha = up(hi), down(lo)
     level_got = others(level_rim).reshape(6 * cols, ny)
     hb0, ha0 = hb, ha
 
-    u, v, depth, rim = pl.pallas_call(
-        functools.partial(pick_kernel, (t_n, s_n, rows, cols, nx)),
-        out_shape=(f32(rows, nx), f32(rows, nx), f32(rows, nx), f32(2 * rows, nx)),
-        in_specs=[VM] * 3, out_specs=(VM,) * 4, compiler_params=params, name="pick",
-    )(arrived, land_mask, intersection)
+    u, v, depth, rim = call(
+        functools.partial(pick_kernel, (t_n, s_n, rows, cols, nx)), "pick",
+        (arrived, land_mask, intersection), [VM] * 3,
+        (f32(rows, nx), f32(rows, nx), f32(rows, nx), f32(3 * rows, nx)), (VM,) * 4, [],
+    )
     vb, va = up(rim), down(rim)
 
-    breaking, below, above = rim, vb, va
-    total = got = None
+    breaking = rim
     for step in range(WSTEPS):
         begin, sums = step == 0, step == WSTEPS - 1
         kinds = 5 if sums else 1
-        scratch = [pltpu.VMEM((3, rows + 2, SUB, nx), jnp.float32), pltpu.VMEM((kinds, rows, SUB, nx), jnp.float32)]
-        shape = (f32(rows - 2, fd, nx), f32(kinds, rows, nx))
-        args = (table, u, v, rim)
-        if not begin:
-            shape += (f32(rows, nx),)
-            args += (depth, total, got)
-        args += (mid, lo, hi, growth)
-        outs = pl.pallas_call(
-            functools.partial(middle_kernel, (rows, fd, nx), begin, sums),
-            out_shape=shape, in_specs=[VM] * len(args), out_specs=(VM,) * len(shape),
-            scratch_shapes=scratch, compiler_params=params, name=f"middle{step}",
-        )(*args)
+        scratch = [vm((3, rows + 2, SUB, nx), jnp.float32), vm((kinds, rows, SUB, nx), jnp.float32)]
         if begin:
-            newmid, partial = outs
+            newmid, partial, growth, mid = call(
+                functools.partial(first_middle_kernel, (rows, fd, nx, chunks)), "middle0",
+                (table, u, v, rim, wind, natural), [VM] * 5 + [HB],
+                (f32(rows - 2, fd, nx), f32(1, rows, nx), f32(rows, fd, nx), f32(2, fd, nx)), (VM,) * 4,
+                [vm((fd, rows, nx), jnp.float32), vm((2, rows, SUB, nx), jnp.float32)] + scratch
+                + [pltpu.SemaphoreType.DMA((chunks,))],
+            )
         else:
-            newmid, partial, breaking = outs
-            below, above = up(breaking), down(breaking)
-        args = (table, u, v, breaking, below, above, vb, va, rim, mid, lo, hi, hb, ha, growth, partial)
-        if begin:
-            args += (level_got,)
+            newmid, partial, breaking = call(
+                functools.partial(middle_kernel, (rows, fd, nx), sums), f"middle{step}",
+                (table, u, v, rim, depth, total, got, mid, lo, hi, growth), [VM] * 11,
+                (f32(rows - 2, fd, nx), f32(kinds, rows, nx), f32(rows, nx)), (VM,) * 3, scratch,
+            )
+        args = (table, u, v, breaking, vb, va, rim, mid, lo, hi, hb, ha, growth, partial)
+        args += (level_got,) if begin else (cb, ca)
         if sums:
             args += (intersection,)
-            shape = (f32(fd, nx), f32(fd, nx), f32(devices, rows, nx))
+            shapes = (f32(fd, nx), f32(fd, nx), f32(devices, rows, nx))
         else:
-            shape = (f32(fd, nx), f32(fd, nx), f32(rows, nx))
-        newlo, newhi, total = pl.pallas_call(
-            functools.partial(edge_kernel, (rows, fd, nx, t_n, s_n, cols, own), begin, sums),
-            out_shape=shape, in_specs=[VM] * len(args), out_specs=(VM,) * 3,
-            scratch_shapes=scratch, compiler_params=params, name=f"edge{step}",
-        )(*args)
+            shapes = (f32(fd + SUB, nx), f32(fd + SUB, nx), f32(rows, nx))
+        newlo, newhi, total = call(
+            functools.partial(edge_kernel, (rows, fd, nx, t_n, s_n, cols, own), begin, sums), f"edge{step}",
+            args, [VM] * len(args), shapes, (VM,) * 3, scratch,
+        )
         mid, lo, hi = newmid, newlo, newhi
         if not sums:
             got = others(total)
             hb, ha = up(hi), down(lo)
+            cb, ca = crossed(total, 1), crossed(total, -1)
         if begin:
             hb1, ha1 = hb, ha
 
@@ -623,22 +654,20 @@
     pad = -(-ny // LANES) * LANES
     size = cols + 8
     ins = (table, levels, landed, rim, depth, mid, lo, hi, ocean, sea, hb0, ha0, hb1, ha1, level_got)
-    waves, fields = pl.pallas_call(
-        functools.partial(last_kernel, (rows, fd, nx, t_n, s_n, cols, own, ny, chunks)),
-        out_shape=(f32(fd * rows, nx), f32(3, own, cols, ny)),
-        in_specs=[VM, SM] + [VM] * (len(ins) - 2), out_specs=(HB, HB),
-        scratch_shapes=[
-            pltpu.VMEM((nx // LANES, fd * rows, LANES), jnp.float32),
-            pltpu.VMEM((rows, SUB, nx), jnp.float32),
-            pltpu.VMEM((pad, nx), jnp.float32),
-            pltpu.VMEM((3 * (own + 4), size, pad), jnp.float32),
-            pltpu.VMEM((3 * (own + 4), size, pad), jnp.float32),
-            pltpu.VMEM((3, own, cols, ny), jnp.float32),
-            pltpu.SemaphoreType.DMA((chunks, nx // LANES)),
+    waves, fields = call(
+        functools.partial(last_kernel, (rows, fd, nx, t_n, s_n, cols, own, ny, chunks)), "last",
+        ins, [VM, SM] + [VM] * (len(ins) - 2), (f32(fd, rows, nx), f32(3, own, cols, ny)), (HB, HB),
+        [
+            vm((fd, rows, nx), jnp.float32),
+            vm((rows, SUB, nx), jnp.float32),
+            vm((pad, nx), jnp.float32),
+            vm((3 * (own + 4), size, pad), jnp.float32),
+            vm((3 * (own + 4), size, pad), jnp.float32),
+            vm((3, own, cols, ny), jnp.float32),
+            pltpu.SemaphoreType.DMA((chunks,)),
             pltpu.SemaphoreType.DMA,
         ],
-        compiler_params=params, name="last",
-    )(*ins)
+    )
     return waves.reshape(spectrum.shape), fields.reshape(ocean_state.shape)
 
 

time: 170 us -> 142 us (0.84)
  local copies, waits for them, and re-layouts: 15.4 us -> 0.78 us
  waiting for transfers between devices: 19.4 us -> 7.34 us
  starting transfers between devices: 50.8 us -> 57.8 us
  Pallas kernels: 59 us -> 53.5 us
  blocking collectives: 23.1 us -> 20.9 us
    ppermute x4 -> x10, starting transfers between devices: 3.34 us -> 23.7 us  [the longest x6 19.2 us: crossed(): lax.ppermute(x, ('tile', 'spec'), [(a * s_n + q, b * s_n + (q + k) % s_n)...]
    unnamed x38 -> x16, local copies, waits for them, and re-layouts: 15.4 us -> 0.78 us
    ppermute x4 -> x10, waiting for transfers between devices: 9.65 us -> 0.03 us  [the longest x6 0.02 us: crossed(): lax.ppermute(x, ('tile', 'spec'), [(a * s_n + q, b * s_n + (q + k) % s_n)...]
    ppermute x8 -> x5, starting transfers between devices: 29.2 us -> 19.7 us  [up(): return lax.ppermute(x, 'tile', [(i, i + 1) for i in range(t_n - 1)])]
    pallas_call x12 -> x11, Pallas kernels: 59 us -> 53.5 us  [call(): pl.pallas_call(kernel, out_shape=shapes, in_specs=specs, out_specs=out_sp...]
    ppermute x8 -> x5, starting transfers between devices: 10.3 us -> 6.46 us  [down(): return lax.ppermute(x, 'tile', [(i + 1, i) for i in range(t_n - 1)])]
    ppermute x8 -> x5, waiting for transfers between devices: 2.41 us -> 0.01 us  [up(): return lax.ppermute(x, 'tile', [(i, i + 1) for i in range(t_n - 1)])]
    all_to_all x1, blocking collectives: 23.1 us -> 20.9 us  [body(): landed = lax.all_to_all(total, AXES, 0, 0, tiled=True)]
  transfers between devices with their start and end apart: 21 -> 21, of which waited for: 7 -> 1; matrix products, arithmetic and copies ran while one was open for 0% -> 0% of each run, Pallas kernels for 13% -> 17%
where the time goes in v1:
time: 142 us; the launch traced here: 141 us
  starting transfers between devices  57.8 us (41%)
  Pallas kernels  53.5 us (38%)
  blocking collectives  20.9 us (15%)
  waiting for transfers between devices  7.34 us (5%)
    pallas_call x11, Pallas kernels, call(): pl.pallas_call(kernel, out_shape=shapes, in_specs=specs, out_specs=out_sp...  53.5 us
    all_to_all x1, blocking collectives, body(): landed = lax.all_to_all(total, AXES, 0, 0, tiled=True)  20.9 us
    ppermute x5, starting transfers between devices, up(): return lax.ppermute(x, 'tile', [(i, i + 1) for i in range(t_n - 1)])  19.7 us
    ppermute x6, starting transfers between devices, crossed(): lax.ppermute(x, ('tile', 'spec'), [(a * s_n + q, b * s_n + (q + k) % s_n)...  19.2 us
    all_to_all x1, starting transfers between devices, body(): arrived = lax.all_to_all(send, AXES, 0, 0, tiled=True)  7.95 us
    all_to_all x1, waiting for transfers between devices, body(): arrived = lax.all_to_all(send, AXES, 0, 0, tiled=True)  7.28 us
    ppermute x5, starting transfers between devices, down(): return lax.ppermute(x, 'tile', [(i + 1, i) for i in range(t_n - 1)])  6.46 us
    ppermute x4, starting transfers between devices, others(): lax.ppermute(x, 'spec', [(i, (i + k) % s_n) for i in range(s_n)])  4.51 us
  transfers between devices with their start and end apart: 21, of which 1 were waited for; matrix products, arithmetic and copies ran while one was open for 0% of the time, Pallas kernels for 17%

profile of v1, /device:TPU:0, one launch (start us, length us, event | category | flops | bytes accessed | tf_op | source)
XLA Modules:
  0.0 141.3 jit_solution(16679584948378853537)
XLA Ops:
  0.6 0.0 copy-start
  0.7 0.0 copy-start.5
  0.7 0.7 copy-done.5
  1.4 3.9 %start.1 = (f32[32,8,128]{2,1,0:T(8,128)}, f32[3,2,32,64]{3,2,1,0:T(8,128)S(1)}, f32[576,256]{1,0:T(8,128)S(1)}, f32[576,256]{1,0:T(8,128)S(1)}) custom-call(f32[2,3,12]{2,1,0:T(4,128)S(1)} %copy-done.5, f32[576,8,256]{2,1,0:T(8,128)} %bitcast.13, f32[24,32,64]{2,1,0:T(8,128)} %bitcast.7, f32[32,64]{1,0:T(8,128)} %bitcast.11), custom_call_target="tpu_custom_call" | custom-call | tf_op jit(solution)/shard_map/start/pallas_call | solution.py:591
  5.4 1.3 collective-permute-start.3
  6.7 3.1 %collective-permute-start.2 = (f32[576,256]{1,0:T(8,128)S(1)}, f32[576,256]{1,0:T(8,128)S(1)}, u32[]{:S(2)}, u32[]{:S(2)}) collective-permute-start(f32[576,256]{1,0:T(8,128)S(1)} %get-tuple-element.44.refs_9_), channel_id=1, source_target_pairs={{0,2},{2,4},{4,6},{6,8},{8,10},{10,12},{12,14},{1,3},{3,5},{5,7},{... | collective-permute-start | bytes 1769480 | tf_op jit(solution)/shard_map/ppermute | solution.py:572
  9.7 8.0 %all-to-all-start = ((f32[32,8,128]{2,1,0:T(8,128)}), f32[32,8,128]{2,1,0:T(8,128)S(1)}, u32[]{:S(2)}, u32[]{:S(2)}) async-start(f32[32,8,128]{2,1,0:T(8,128)} %get-tuple-element.37), calls=%async_computation | async-start | bytes 262144 | tf_op jit(solution)/shard_map/all_to_all | solution.py:603
  17.7 1.8 %collective-permute-start.4 = (f32[3,2,32,64]{3,2,1,0:T(8,128)S(1)}, f32[3,2,32,64]{3,2,1,0:T(8,128)S(1)}, u32[]{:S(2)}, u32[]{:S(2)}) collective-permute-start(f32[3,2,32,64]{3,2,1,0:T(8,128)S(1)} %get-tuple-element.47), channel_id=1, source_target_pairs={{0,1},{1,0},{2,3},{3,2},{4,5},{5,4},{6,7},{7,6},{8,9},{9,8},{10,11... | collective-permute-start | bytes 147464 | tf_op jit(solution)/shard_map/ppermute | solution.py:578
  19.5 7.3 %all-to-all-done.got_ref = f32[32,8,128]{2,1,0:T(8,128)S(1)} async-done(((f32[32,8,128]{2,1,0:T(8,128)}), f32[32,8,128]{2,1,0:T(8,128)S(1)}, u32[]{:S(2)}, u32[]{:S(2)}) %all-to-all-start) | async-done | bytes 131104 | tf_op jit(solution)/shard_map/all_to_all | solution.py:603
  26.8 0.6 pick.1
  27.4 1.3 collective-permute-start.1
  28.7 3.0 %collective-permute-start = (f32[24,256]{1,0:T(8,128)S(1)}, f32[24,256]{1,0:T(8,128)S(1)}, u32[]{:S(2)}, u32[]{:S(2)}) collective-permute-start(f32[24,256]{1,0:T(8,128)S(1)} %get-tuple-element.40.rim_ref.refs_3_.refs_6_), channel_id=1, source_target_pairs={{0,2},{2,4},{4,6},{6,8},{8,10},{10,12},{12,14},{1,3},{3,5},{5,7},{... | collective-permute-start | bytes 73736 | tf_op jit(solution)/shard_map/ppermute | solution.py:572
  31.7 6.6 %middle0.1 = (f32[6,576,256]{2,1,0:T(8,128)S(1)}, f32[1,8,256]{2,1,0:T(8,128)S(1)}, f32[8,576,256]{2,1,0:T(8,128)S(1)}, f32[2,576,256]{2,1,0:T(8,128)S(1)}) custom-call(f32[2,576,16]{2,1,0:T(8,128)S(1)} %copy-done, f32[8,256]{1,0:T(8,128)S(1)} %get-tuple-element.38.u_ref.refs_1_, f32[8,256]{1,0:T(8,128)S(1)} %get-tuple-element.39.v_ref.refs_2_, ...), custom_call_target="tpu_custom_call" | custom-call | tf_op jit(solution)/shard_map/middle0/pallas_call | solution.py:591
  38.4 0.0 collective-permute-done.4
  38.4 0.0 collective-permute-done.1.refs_5_
  38.4 0.0 collective-permute-done.2.refs_10_.hb_ref
  38.4 4.3 %edge0.1 = (f32[584,256]{1,0:T(8,128)S(1)}, f32[584,256]{1,0:T(8,128)S(1)}, f32[8,256]{1,0:T(8,128)S(1)}) custom-call(f32[2,576,16]{2,1,0:T(8,128)S(1)} %copy-done, f32[8,256]{1,0:T(8,128)S(1)} %get-tuple-element.38.u_ref.refs_1_, f32[8,256]{1,0:T(8,128)S(1)} %get-tuple-element.39.v_ref.refs_2_, f32[24,256]{1,0:T(8,128)S(1)} %get-tuple-element.40.rim_ref.refs_3_.refs_6_, ...), custom_call_target="tpu_custom_call" | custom-call | tf_op jit(solution)/shard_map/edge0/pallas_call | solution.py:591
  42.7 1.3 collective-permute-start.7
  44.0 3.5 %collective-permute-start.6 = (f32[584,256]{1,0:T(8,128)S(1)}, f32[584,256]{1,0:T(8,128)S(1)}, u32[]{:S(2)}, u32[]{:S(2)}) collective-permute-start(f32[584,256]{1,0:T(8,128)S(1)} %get-tuple-element.51.hi_ref.refs_9_), channel_id=1, source_target_pairs={{0,2},{2,4},{4,6},{6,8},{8,10},{10,12},{12,14},{1,3},{3,5},{5,7},{... | collective-permute-start | bytes 1794056 | tf_op jit(solution)/shard_map/ppermute | solution.py:572
  47.6 1.6 %collective-permute-start.5 = (f32[8,256]{1,0:T(8,128)S(1)}, f32[8,256]{1,0:T(8,128)S(1)}, u32[]{:S(2)}, u32[]{:S(2)}) collective-permute-start(f32[8,256]{1,0:T(8,128)S(1)} %get-tuple-element.48.own_ref), channel_id=1, source_target_pairs={{0,1},{1,0},{2,3},{3,2},{4,5},{5,4},{6,7},{7,6},{8,9},{9,8},{10,11... | collective-permute-start | bytes 24584 | tf_op jit(solution)/shard_map/ppermute | solution.py:578
  49.2 1.3 collective-permute-start.9
  50.5 4.3 %collective-permute-start.8 = (f32[8,256]{1,0:T(8,128)S(1)}, f32[8,256]{1,0:T(8,128)S(1)}, u32[]{:S(2)}, u32[]{:S(2)}) collective-permute-start(f32[8,256]{1,0:T(8,128)S(1)} %get-tuple-element.48.own_ref), channel_id=1, source_target_pairs={{0,3},{1,2},{2,5},{3,4},{4,7},{5,6},{6,9},{7,8},{8,11},{9,10},{10,... | collective-permute-start | bytes 24584 | tf_op jit(solution)/shard_map/ppermute | solution.py:583
  54.8 0.0 collective-permute-done.5.got_ref
  54.8 5.0 %middle1.1 = (f32[6,576,256]{2,1,0:T(8,128)S(1)}, f32[1,8,256]{2,1,0:T(8,128)S(1)}, f32[8,256]{1,0:T(8,128)S(1)}) custom-call(f32[2,576,16]{2,1,0:T(8,128)S(1)} %copy-done, f32[8,256]{1,0:T(8,128)S(1)} %get-tuple-element.38.u_ref.refs_1_, f32[8,256]{1,0:T(8,128)S(1)} %get-tuple-element.39.v_ref.refs_2_, ...), custom_call_target="tpu_custom_call" | custom-call | tf_op jit(solution)/shard_map/middle1/pallas_call | solution.py:591
  59.8 0.0 collective-permute-done.9.refs_15_
  59.8 0.0 collective-permute-done.7.refs_11_.ca_ref
  59.8 0.0 collective-permute-done.6.refs_10_.cb_ref
  59.8 4.3 %edge1.1 = (f32[584,256]{1,0:T(8,128)S(1)}, f32[584,256]{1,0:T(8,128)S(1)}, f32[8,256]{1,0:T(8,128)S(1)}) custom-call(f32[2,576,16]{2,1,0:T(8,128)S(1)} %copy-done, f32[8,256]{1,0:T(8,128)S(1)} %get-tuple-element.38.u_ref.refs_1_, f32[8,256]{1,0:T(8,128)S(1)} %get-tuple-element.39.v_ref.refs_2_, f32[8,256]{1,0:T(8,128)S(1)} %get-tuple-element.52.refs_3_, ...), custom_call_target="tpu_custom_call" | custom-call | tf_op jit(solution)/shard_map/edge1/pallas_call | solution.py:591
  64.1 1.3 collective-permute-start.12
  65.4 4.9 %collective-permute-start.11 = (f32[584,256]{1,0:T(8,128)S(1)}, f32[584,256]{1,0:T(8,128)S(1)}, u32[]{:S(2)}, u32[]{:S(2)}) collective-permute-start(f32[584,256]{1,0:T(8,128)S(1)} %get-tuple-element.57.hi_ref.refs_9_), channel_id=1, source_target_pairs={{0,2},{2,4},{4,6},{6,8},{8,10},{10,12},{12,14},{1,3},{3,5},{5,7},{... | collective-permute-start | bytes 1794056 | tf_op jit(solution)/shard_map/ppermute | solution.py:572
  70.3 0.5 collective-permute-start.10
  70.8 1.3 collective-permute-start.14
  72.1 5.1 %collective-permute-start.13 = (f32[8,256]{1,0:T(8,128)S(1)}, f32[8,256]{1,0:T(8,128)S(1)}, u32[]{:S(2)}, u32[]{:S(2)}) collective-permute-start(f32[8,256]{1,0:T(8,128)S(1)} %get-tuple-element.54.own_ref), channel_id=1, source_target_pairs={{0,3},{1,2},{2,5},{3,4},{4,7},{5,6},{6,9},{7,8},{8,11},{9,10},{10,... | collective-permute-start | bytes 24584 | tf_op jit(solution)/shard_map/ppermute | solution.py:583
  77.3 5.0 %middle2.1 = (f32[6,576,256]{2,1,0:T(8,128)S(1)}, f32[1,8,256]{2,1,0:T(8,128)S(1)}, f32[8,256]{1,0:T(8,128)S(1)}) custom-call(f32[2,576,16]{2,1,0:T(8,128)S(1)} %copy-done, f32[8,256]{1,0:T(8,128)S(1)} %get-tuple-element.38.u_ref.refs_1_, f32[8,256]{1,0:T(8,128)S(1)} %get-tuple-element.39.v_ref.refs_2_, ...), custom_call_target="tpu_custom_call" | custom-call | tf_op jit(solution)/shard_map/middle2/pallas_call | solution.py:591
  82.3 0.0 collective-permute-done.13.refs_14_
  82.4 4.3 %edge2.1 = (f32[584,256]{1,0:T(8,128)S(1)}, f32[584,256]{1,0:T(8,128)S(1)}, f32[8,256]{1,0:T(8,128)S(1)}) custom-call(f32[2,576,16]{2,1,0:T(8,128)S(1)} %copy-done, f32[8,256]{1,0:T(8,128)S(1)} %get-tuple-element.38.u_ref.refs_1_, f32[8,256]{1,0:T(8,128)S(1)} %get-tuple-element.39.v_ref.refs_2_, f32[8,256]{1,0:T(8,128)S(1)} %get-tuple-element.58.refs_3_, ...), custom_call_target="tpu_custom_call" | custom-call | tf_op jit(solution)/shard_map/edge2/pallas_call | solution.py:591
  86.6 1.3 collective-permute-start.17
  87.9 5.2 %collective-permute-start.16 = (f32[584,256]{1,0:T(8,128)S(1)}, f32[584,256]{1,0:T(8,128)S(1)}, u32[]{:S(2)}, u32[]{:S(2)}) collective-permute-start(f32[584,256]{1,0:T(8,128)S(1)} %get-tuple-element.63.hi_ref.refs_9_), channel_id=1, source_target_pairs={{0,2},{2,4},{4,6},{6,8},{8,10},{10,12},{12,14},{1,3},{3,5},{5,7},{... | collective-permute-start | bytes 1794056 | tf_op jit(solution)/shard_map/ppermute | solution.py:572
  93.1 0.5 collective-permute-start.15
  93.6 1.3 collective-permute-start.19
  94.9 5.9 %collective-permute-start.18 = (f32[8,256]{1,0:T(8,128)S(1)}, f32[8,256]{1,0:T(8,128)S(1)}, u32[]{:S(2)}, u32[]{:S(2)}) collective-permute-start(f32[8,256]{1,0:T(8,128)S(1)} %get-tuple-element.60.own_ref), channel_id=1, source_target_pairs={{0,3},{1,2},{2,5},{3,4},{4,7},{5,6},{6,9},{7,8},{8,11},{9,10},{10,... | collective-permute-start | bytes 24584 | tf_op jit(solution)/shard_map/ppermute | solution.py:583
  100.9 6.3 %middle3.1 = (f32[6,576,256]{2,1,0:T(8,128)S(1)}, f32[5,8,256]{2,1,0:T(8,128)S(1)}, f32[8,256]{1,0:T(8,128)S(1)}) custom-call(f32[2,576,16]{2,1,0:T(8,128)S(1)} %copy-done, f32[8,256]{1,0:T(8,128)S(1)} %get-tuple-element.38.u_ref.refs_1_, f32[8,256]{1,0:T(8,128)S(1)} %get-tuple-element.39.v_ref.refs_2_, ...), custom_call_target="tpu_custom_call" | custom-call | tf_op jit(solution)/shard_map/middle3/pallas_call | solution.py:591
  107.2 0.0 copy-start.1
  107.2 0.0 copy-start.2
  107.2 0.0 copy-start.6
  107.2 5.2 %edge3.1 = (f32[576,256]{1,0:T(8,128)S(1)}, f32[576,256]{1,0:T(8,128)S(1)}, f32[32,8,256]{2,1,0:T(8,128)S(1)}) custom-call(f32[2,576,16]{2,1,0:T(8,128)S(1)} %copy-done, f32[8,256]{1,0:T(8,128)S(1)} %get-tuple-element.38.u_ref.refs_1_, f32[8,256]{1,0:T(8,128)S(1)} %get-tuple-element.39.v_ref.refs_2_, f32[8,256]{1,0:T(8,128)S(1)} %get-tuple-element.64.refs_3_, ...), custom_call_target="tpu_custom_call" | custom-call | tf_op jit(solution)/shard_map/edge3/pallas_call | solution.py:591
  112.4 20.9 %all_to_all.10.got_ref = f32[32,8,256]{2,1,0:T(8,128)S(1)} all-to-all(f32[32,8,256]{2,1,0:T(8,128)S(1)} %get-tuple-element.66), channel_id=1, replica_groups=mesh['grp'=2,'tile'=8,'spec'=2] {'grp','tile','spec'}, dimensions={0} | all-to-all | bytes 524288 | tf_op jit(solution)/shard_map/all_to_all | solution.py:653
  133.3 8.0 %last.1 = (f32[576,8,256]{2,1,0:T(8,128)}, f32[3,8,32,64]{3,2,1,0:T(8,128)}) custom-call(f32[2,576,16]{2,1,0:T(8,128)S(1)} %copy-done, f32[2,3,12]{2,1,0:T(4,128)S(1)} %copy-done.6, f32[32,8,256]{2,1,0:T(8,128)S(1)} %all_to_all.10.got_ref, f32[24,256]{1,0:T(8,128)S(1)} %get-tuple-element.40.rim_ref.refs_3_.refs_6_, ...), custom_call_target="tpu_custom_call" | custom-call | tf_op jit(solution)/shard_map/last/pallas_call | solution.py:591
  (22 shorter events, 0.1 us)
Async XLA Ops:
  0.6 31.1 %copy-start = (f32[2,576,16]{2,1,0:T(8,128)S(1)}, f32[2,576,16]{2,1,0:T(8,128)}, u32[]{:S(2)}) copy-start(f32[2,576,16]{2,1,0:T(8,128)} %constant.4.clone.table_ref.refs_0_) | copy-start | bytes 221188
  0.6 26.2 %copy-start.3 = (s32[8,256]{1,0:T(8,128)S(1)}, s32[8,256]{1,0:T(8,128)}, u32[]{:S(2)}) copy-start(s32[8,256]{1,0:T(8,128)} %refs_16_.1) | copy-start | bytes 24580
  0.7 31.1 %copy-start.4 = (f32[2,8,256]{2,1,0:T(8,128)S(1)}, f32[2,8,256]{2,1,0:T(8,128)}, u32[]{:S(2)}) copy-start(f32[2,8,256]{2,1,0:T(8,128)} %wind_ref.1) | copy-start | bytes 49156
  0.7 0.7 copy-start.5
  1.4 25.4 %copy-start.7 = (s32[8,256]{1,0:T(8,128)S(1)}, s32[8,256]{1,0:T(8,128)}, u32[]{:S(2)}) copy-start(s32[8,256]{1,0:T(8,128)} %mask_ref.1) | copy-start | bytes 24580
  5.4 33.0 %collective-permute-start.3 = (f32[576,256]{1,0:T(8,128)S(1)}, f32[576,256]{1,0:T(8,128)S(1)}, u32[]{:S(2)}, u32[]{:S(2)}) collective-permute-start(f32[576,256]{1,0:T(8,128)S(1)} %get-tuple-element.43.refs_8_), channel_id=1, source_target_pairs={{2,0},{4,2},{6,4},{8,6},{10,8},{12,10},{14,12},{3,1},{5,3},{7,5},{... | collective-permute-start | bytes 1769480 | tf_op jit(solution)/shard_map/ppermute | solution.py:575
  6.7 31.7 %collective-permute-start.2 = (f32[576,256]{1,0:T(8,128)S(1)}, f32[576,256]{1,0:T(8,128)S(1)}, u32[]{:S(2)}, u32[]{:S(2)}) collective-permute-start(f32[576,256]{1,0:T(8,128)S(1)} %get-tuple-element.44.refs_9_), channel_id=1, source_target_pairs={{0,2},{2,4},{4,6},{6,8},{8,10},{10,12},{12,14},{1,3},{3,5},{5,7},{... | collective-permute-start | bytes 1769480 | tf_op jit(solution)/shard_map/ppermute | solution.py:572
  9.7 17.1 %all-to-all-start = ((f32[32,8,128]{2,1,0:T(8,128)}), f32[32,8,128]{2,1,0:T(8,128)S(1)}, u32[]{:S(2)}, u32[]{:S(2)}) async-start(f32[32,8,128]{2,1,0:T(8,128)} %get-tuple-element.37), calls=%async_computation | async-start | bytes 262144 | tf_op jit(solution)/shard_map/all_to_all | solution.py:603
  17.7 20.7 %collective-permute-start.4 = (f32[3,2,32,64]{3,2,1,0:T(8,128)S(1)}, f32[3,2,32,64]{3,2,1,0:T(8,128)S(1)}, u32[]{:S(2)}, u32[]{:S(2)}) collective-permute-start(f32[3,2,32,64]{3,2,1,0:T(8,128)S(1)} %get-tuple-element.47), channel_id=1, source_target_pairs={{0,1},{1,0},{2,3},{3,2},{4,5},{5,4},{6,7},{7,6},{8,9},{9,8},{10,11... | collective-permute-start | bytes 147464 | tf_op jit(solution)/shard_map/ppermute | solution.py:578
  27.4 11.0 %collective-permute-start.1 = (f32[24,256]{1,0:T(8,128)S(1)}, f32[24,256]{1,0:T(8,128)S(1)}, u32[]{:S(2)}, u32[]{:S(2)}) collective-permute-start(f32[24,256]{1,0:T(8,128)S(1)} %get-tuple-element.40.rim_ref.refs_3_.refs_6_), channel_id=1, source_target_pairs={{2,0},{4,2},{6,4},{8,6},{10,8},{12,10},{14,12},{3,1},{5,3},{7,5},{... | collective-permute-start | bytes 73736 | tf_op jit(solution)/shard_map/ppermute | solution.py:575
  28.7 9.7 %collective-permute-start = (f32[24,256]{1,0:T(8,128)S(1)}, f32[24,256]{1,0:T(8,128)S(1)}, u32[]{:S(2)}, u32[]{:S(2)}) collective-permute-start(f32[24,256]{1,0:T(8,128)S(1)} %get-tuple-element.40.rim_ref.refs_3_.refs_6_), channel_id=1, source_target_pairs={{0,2},{2,4},{4,6},{6,8},{8,10},{10,12},{12,14},{1,3},{3,5},{5,7},{... | collective-permute-start | bytes 73736 | tf_op jit(solution)/shard_map/ppermute | solution.py:572
  42.7 17.1 %collective-permute-start.7 = (f32[584,256]{1,0:T(8,128)S(1)}, f32[584,256]{1,0:T(8,128)S(1)}, u32[]{:S(2)}, u32[]{:S(2)}) collective-permute-start(f32[584,256]{1,0:T(8,128)S(1)} %get-tuple-element.50.lo_ref.refs_8_), channel_id=1, source_target_pairs={{2,0},{4,2},{6,4},{8,6},{10,8},{12,10},{14,12},{3,1},{5,3},{7,5},{... | collective-permute-start | bytes 1794056 | tf_op jit(solution)/shard_map/ppermute | solution.py:575
  44.0 15.8 %collective-permute-start.6 = (f32[584,256]{1,0:T(8,128)S(1)}, f32[584,256]{1,0:T(8,128)S(1)}, u32[]{:S(2)}, u32[]{:S(2)}) collective-permute-start(f32[584,256]{1,0:T(8,128)S(1)} %get-tuple-element.51.hi_ref.refs_9_), channel_id=1, source_target_pairs={{0,2},{2,4},{4,6},{6,8},{8,10},{10,12},{12,14},{1,3},{3,5},{5,7},{... | collective-permute-start | bytes 1794056 | tf_op jit(solution)/shard_map/ppermute | solution.py:572
  47.6 7.2 %collective-permute-start.5 = (f32[8,256]{1,0:T(8,128)S(1)}, f32[8,256]{1,0:T(8,128)S(1)}, u32[]{:S(2)}, u32[]{:S(2)}) collective-permute-start(f32[8,256]{1,0:T(8,128)S(1)} %get-tuple-element.48.own_ref), channel_id=1, source_target_pairs={{0,1},{1,0},{2,3},{3,2},{4,5},{5,4},{6,7},{7,6},{8,9},{9,8},{10,11... | collective-permute-start | bytes 24584 | tf_op jit(solution)/shard_map/ppermute | solution.py:578
  49.2 10.6 %collective-permute-start.9 = (f32[8,256]{1,0:T(8,128)S(1)}, f32[8,256]{1,0:T(8,128)S(1)}, u32[]{:S(2)}, u32[]{:S(2)}) collective-permute-start(f32[8,256]{1,0:T(8,128)S(1)} %get-tuple-element.48.own_ref), channel_id=1, source_target_pairs={{2,1},{3,0},{4,3},{5,2},{6,5},{7,4},{8,7},{9,6},{10,9},{11,8},{12,... | collective-permute-start | bytes 24584 | tf_op jit(solution)/shard_map/ppermute | solution.py:583
  50.5 9.3 %collective-permute-start.8 = (f32[8,256]{1,0:T(8,128)S(1)}, f32[8,256]{1,0:T(8,128)S(1)}, u32[]{:S(2)}, u32[]{:S(2)}) collective-permute-start(f32[8,256]{1,0:T(8,128)S(1)} %get-tuple-element.48.own_ref), channel_id=1, source_target_pairs={{0,3},{1,2},{2,5},{3,4},{4,7},{5,6},{6,9},{7,8},{8,11},{9,10},{10,... | collective-permute-start | bytes 24584 | tf_op jit(solution)/shard_map/ppermute | solution.py:583
  64.1 18.2 %collective-permute-start.12 = (f32[584,256]{1,0:T(8,128)S(1)}, f32[584,256]{1,0:T(8,128)S(1)}, u32[]{:S(2)}, u32[]{:S(2)}) collective-permute-start(f32[584,256]{1,0:T(8,128)S(1)} %get-tuple-element.56.lo_ref.refs_8_), channel_id=1, source_target_pairs={{2,0},{4,2},{6,4},{8,6},{10,8},{12,10},{14,12},{3,1},{5,3},{7,5},{... | collective-permute-start | bytes 1794056 | tf_op jit(solution)/shard_map/ppermute | solution.py:575
  65.4 16.9 %collective-permute-start.11 = (f32[584,256]{1,0:T(8,128)S(1)}, f32[584,256]{1,0:T(8,128)S(1)}, u32[]{:S(2)}, u32[]{:S(2)}) collective-permute-start(f32[584,256]{1,0:T(8,128)S(1)} %get-tuple-element.57.hi_ref.refs_9_), channel_id=1, source_target_pairs={{0,2},{2,4},{4,6},{6,8},{8,10},{10,12},{12,14},{1,3},{3,5},{5,7},{... | collective-permute-start | bytes 1794056 | tf_op jit(solution)/shard_map/ppermute | solution.py:572
  70.3 6.9 %collective-permute-start.10 = (f32[8,256]{1,0:T(8,128)S(1)}, f32[8,256]{1,0:T(8,128)S(1)}, u32[]{:S(2)}, u32[]{:S(2)}) collective-permute-start(f32[8,256]{1,0:T(8,128)S(1)} %get-tuple-element.54.own_ref), channel_id=1, source_target_pairs={{0,1},{1,0},{2,3},{3,2},{4,5},{5,4},{6,7},{7,6},{8,9},{9,8},{10,11... | collective-permute-start | bytes 24584 | tf_op jit(solution)/shard_map/ppermute | solution.py:578
  70.8 11.5 %collective-permute-start.14 = (f32[8,256]{1,0:T(8,128)S(1)}, f32[8,256]{1,0:T(8,128)S(1)}, u32[]{:S(2)}, u32[]{:S(2)}) collective-permute-start(f32[8,256]{1,0:T(8,128)S(1)} %get-tuple-element.54.own_ref), channel_id=1, source_target_pairs={{2,1},{3,0},{4,3},{5,2},{6,5},{7,4},{8,7},{9,6},{10,9},{11,8},{12,... | collective-permute-start | bytes 24584 | tf_op jit(solution)/shard_map/ppermute | solution.py:583
  72.1 10.2 %collective-permute-start.13 = (f32[8,256]{1,0:T(8,128)S(1)}, f32[8,256]{1,0:T(8,128)S(1)}, u32[]{:S(2)}, u32[]{:S(2)}) collective-permute-start(f32[8,256]{1,0:T(8,128)S(1)} %get-tuple-element.54.own_ref), channel_id=1, source_target_pairs={{0,3},{1,2},{2,5},{3,4},{4,7},{5,6},{6,9},{7,8},{8,11},{9,10},{10,... | collective-permute-start | bytes 24584 | tf_op jit(solution)/shard_map/ppermute | solution.py:583
  86.6 20.5 %collective-permute-start.17 = (f32[584,256]{1,0:T(8,128)S(1)}, f32[584,256]{1,0:T(8,128)S(1)}, u32[]{:S(2)}, u32[]{:S(2)}) collective-permute-start(f32[584,256]{1,0:T(8,128)S(1)} %get-tuple-element.62.lo_ref.refs_8_), channel_id=1, source_target_pairs={{2,0},{4,2},{6,4},{8,6},{10,8},{12,10},{14,12},{3,1},{5,3},{7,5},{... | collective-permute-start | bytes 1794056 | tf_op jit(solution)/shard_map/ppermute | solution.py:575
  87.9 19.2 %collective-permute-start.16 = (f32[584,256]{1,0:T(8,128)S(1)}, f32[584,256]{1,0:T(8,128)S(1)}, u32[]{:S(2)}, u32[]{:S(2)}) collective-permute-start(f32[584,256]{1,0:T(8,128)S(1)} %get-tuple-element.63.hi_ref.refs_9_), channel_id=1, source_target_pairs={{0,2},{2,4},{4,6},{6,8},{8,10},{10,12},{12,14},{1,3},{3,5},{5,7},{... | collective-permute-start | bytes 1794056 | tf_op jit(solution)/shard_map/ppermute | solution.py:572
  93.1 7.7 %collective-permute-start.15 = (f32[8,256]{1,0:T(8,128)S(1)}, f32[8,256]{1,0:T(8,128)S(1)}, u32[]{:S(2)}, u32[]{:S(2)}) collective-permute-start(f32[8,256]{1,0:T(8,128)S(1)} %get-tuple-element.60.own_ref), channel_id=1, source_target_pairs={{0,1},{1,0},{2,3},{3,2},{4,5},{5,4},{6,7},{7,6},{8,9},{9,8},{10,11... | collective-permute-start | bytes 24584 | tf_op jit(solution)/shard_map/ppermute | solution.py:578
  93.6 13.5 %collective-permute-start.19 = (f32[8,256]{1,0:T(8,128)S(1)}, f32[8,256]{1,0:T(8,128)S(1)}, u32[]{:S(2)}, u32[]{:S(2)}) collective-permute-start(f32[8,256]{1,0:T(8,128)S(1)} %get-tuple-element.60.own_ref), channel_id=1, source_target_pairs={{2,1},{3,0},{4,3},{5,2},{6,5},{7,4},{8,7},{9,6},{10,9},{11,8},{12,... | collective-permute-start | bytes 24584 | tf_op jit(solution)/shard_map/ppermute | solution.py:583
  94.9 12.2 %collective-permute-start.18 = (f32[8,256]{1,0:T(8,128)S(1)}, f32[8,256]{1,0:T(8,128)S(1)}, u32[]{:S(2)}, u32[]{:S(2)}) collective-permute-start(f32[8,256]{1,0:T(8,128)S(1)} %get-tuple-element.60.own_ref), channel_id=1, source_target_pairs={{0,3},{1,2},{2,5},{3,4},{4,7},{5,6},{6,9},{7,8},{8,11},{9,10},{10,... | collective-permute-start | bytes 24584 | tf_op jit(solution)/shard_map/ppermute | solution.py:583
  107.2 26.1 %copy-start.1 = (f32[1,3,8,32,64]{4,3,2,1,0:T(8,128)S(1)}, f32[1,3,8,32,64]{4,3,2,1,0:T(8,128)}, u32[]{:S(2)}) copy-start(f32[1,3,8,32,64]{4,3,2,1,0:T(8,128)} %param.12) | copy-start | bytes 589828
  107.2 26.1 %copy-start.2 = (f32[1,32,64]{2,1,0:T(8,128)S(1)}, f32[1,32,64]{2,1,0:T(8,128)}, u32[]{:S(2)}) copy-start(f32[1,32,64]{2,1,0:T(8,128)} %param.13) | copy-start | bytes 24580
  107.2 26.1 %copy-start.6 = (f32[2,3,12]{2,1,0:T(4,128)S(1)}, f32[2,3,12]{2,1,0:T(4,128)}, u32[]{:S(2)}) copy-start(f32[2,3,12]{2,1,0:T(4,128)} %constant.5.clone.level_ref) | copy-start | bytes 868

commit v2 on v1

v2 whole, which is shorter than its diff:
```python
import functools
import math

import jax
import jax.numpy as jnp
import numpy as np
from jax import lax
from jax.experimental import pallas as pl
from jax.experimental.pallas import tpu as pltpu
from jax.sharding import PartitionSpec as P


WSTEPS = 4
HALO = WSTEPS
NEAR = 2
LANES = 128
SUB = 8
UNROLL = 4
AXES = ("grp", "tile", "spec")

BW, GE, GN, WE, WN, SX, SY, DX, DY, INV = range(10)

VM = pl.BlockSpec(memory_space=pltpu.VMEM)
SM = pl.BlockSpec(memory_space=pltpu.SMEM)
HB = pl.BlockSpec(memory_space=pltpu.HBM)


def f32(*shape):
    return jax.ShapeDtypeStruct(shape, jnp.float32)


def wave_table(freqs, dirs, parts):
    frequency = 0.04 * 1.1 ** np.arange(freqs)
    celerity = 1.56 / frequency
    group = 0.4 * 1.1 ** (-np.arange(freqs, dtype=np.float64))
    width = 0.1 * frequency * (2.0 * math.pi / dirs)
    angle = 2.0 * math.pi * (np.arange(dirs) + 0.5) / dirs
    cos, sin, one = np.cos(angle), np.sin(angle), np.ones(dirs)
    columns = [
        np.outer(width, one),
        np.outer(group, cos),
        np.outer(group, sin),
        np.outer(0.05 / celerity, cos),
        np.outer(0.05 / celerity, sin),
        np.outer(5.0 / celerity, cos),
        np.outer(5.0 / celerity, sin),
        np.outer(20.0 * frequency**3, cos),
        np.outer(20.0 * frequency**3, sin),
        np.outer(1.0 / width, one),
    ]
    table = np.zeros((parts, freqs * dirs // parts, 16), np.float32)
    for k, column in enumerate(columns):
        split = column.reshape(freqs, parts, dirs // parts).transpose(1, 0, 2)
        table[:, :, k] = split.reshape(parts, -1)
    return table


def level_table(levels, parts, own):
    depth = (np.arange(levels) + 0.5) / levels
    profile = np.exp(-2.0 * depth)
    weights = profile / profile.sum()
    table = np.zeros((parts, 3, own + 4), np.float32)
    for s in range(parts):
        table[s, 0, :own] = weights[s * own : (s + 1) * own]
        for l in range(own + 4):
            g = s * own + l - 2
            if 0 <= g < levels:
                table[s, 1, l] = profile[g]
                table[s, 2, l] = 1.0
    return table


def lanes_of(shape):
    return lax.broadcasted_iota(jnp.int32, shape, len(shape) - 1)


def wide(column):
    return jnp.broadcast_to(column, (SUB, LANES))


def half(h):
    return slice(h * LANES, (h + 1) * LANES)


def barrel(values, shift, size, left):
    bit = 1
    while bit < size:
        taken = (shift & bit) != 0
        amount = size - bit if left else bit
        values = [jnp.where(taken, pltpu.roll(v, amount, 1), v) for v in values]
        bit *= 2
    return values


def start_kernel(n, level_ref, spectrum_ref, ocean_hbm, sea_hbm, mask_hbm, wind_hbm, cross_hbm,
                 out_ref, rim_ref, near_lo_hbm, near_hi_hbm, far_lo_hbm, far_hi_hbm,
                 raw, ocean, sea, mask_ref, wind_ref, cross_ref, near_lo, near_hi, far_lo, far_hi, sem, out_sem):
    t_n, s_n, rows, cols, own, ny, fd, nx, chunks = n
    s = lax.axis_index("spec")
    pad = -(-ny // LANES) * LANES
    part = fd // chunks
    small = ((ocean_hbm, ocean), (sea_hbm, sea), (mask_hbm, mask_ref), (wind_hbm, wind_ref), (cross_hbm, cross_ref))
    first = [pltpu.make_async_copy(a, b, sem.at[chunks + k]) for k, (a, b) in enumerate(small)]
    copies = [
        pltpu.make_async_copy(spectrum_ref.at[pl.ds(c * part, part)], raw.at[pl.ds(c * part, part)], sem.at[c])
        for c in range(chunks)
    ]
    for copy in first + copies:
        copy.start()
    for copy in first:
        copy.wait()
    parts = []
    for c in range(2):
        total = None
        for k in range(own):
            term = level_ref[s, 0, k] * ocean[c * own + k]
            total = term if total is None else total + term
        parts.append(total)
    parts.append(jnp.where(s == 0, sea[...], 0.0))
    for c in range(3):
        for k in range(2):
            rim_ref[c, k] = jnp.where(s == 0, ocean[c * own + own - 2 + k], ocean[c * own + k])
    stack = jnp.concatenate(parts, axis=0)
    stack = jnp.pad(stack, ((0, LANES - 3 * cols), (0, pad - ny)))
    edge = jnp.zeros((HALO, LANES), jnp.float32)
    turned = jnp.concatenate([edge, jnp.transpose(stack)[:ny], edge], axis=0)
    for t in range(t_n):
        for q in range(s_n):
            out_ref[t * s_n + q] = turned[t * rows : (t + 1) * rows + 2 * HALO, : 4 * cols]
    aux = [mask_ref[...].astype(jnp.float32), wind_ref[0], wind_ref[1], cross_ref[...].astype(jnp.float32)]
    for k, value in enumerate(aux):
        at = NEAR * fd + k * HALO
        near_hi[at : at + HALO] = value[rows - HALO : rows]
        near_lo[at : at + HALO] = value[0:HALO]

    held = ((near_lo, near_lo_hbm), (near_hi, near_hi_hbm), (far_lo, far_lo_hbm), (far_hi, far_hi_hbm))
    outward = []

    def send_out(c):
        spans = [(c * part, part), (fd + c * part, part)]
        for k, (here, there) in enumerate(held):
            for j, (at, size) in enumerate(spans):
                span = pl.ds(at, size)
                outward.append(pltpu.make_async_copy(here.at[span], there.at[span], out_sem.at[c, k, j]))
                outward[-1].start()
            if c == 0 and k < 2:
                span = pl.ds(NEAR * fd, 4 * HALO)
                outward.append(pltpu.make_async_copy(here.at[span], there.at[span], out_sem.at[c, k, 2]))
                outward[-1].start()

    for c in range(chunks):
        copies[c].wait()

        def turn(i, carry):
            for k in range(2):
                at = pl.multiple_of(c * part + (2 * i + k) * SUB, SUB)
                for h in range(nx // LANES):
                    planes = jnp.swapaxes(raw[pl.ds(at, SUB), :, half(h)], 0, 1)
                    for j in range(HALO):
                        lo_ref, hi_ref = (near_lo, near_hi) if j < NEAR else (far_lo, far_hi)
                        sl = pl.ds(pl.multiple_of(at + (j % NEAR) * fd, SUB), SUB)
                        lo_ref[sl, half(h)] = planes[j]
                        hi_ref[sl, half(h)] = planes[rows - 1 - j]
            return carry

        lax.fori_loop(0, part // (2 * SUB), turn, 0)
        if c:
            send_out(c)

    @pl.when(lax.axis_index("grp") == 1)
    def _():
        stack = 3 * own
        for k in range(2):
            for ref, at in ((near_lo, k), (near_hi, cols - 2 + k)):
                for m in range(stack):
                    ref[k * stack + m : k * stack + m + 1, 0:ny] = ocean[m, at : at + 1, :]
                ref[2 * stack + k : 2 * stack + k + 1, 0:ny] = sea[at : at + 1, :]

    send_out(0)
    for copy in outward:
        copy.wait()


def pick_kernel(n, full, got_ref, mask_ref, cross_ref, *refs):
    t_n, s_n, rows, cols, nx, fd = n[:6]
    ext = rows + 2 * HALO
    lane = lanes_of((ext, LANES))
    per = LANES // cols
    fields = [[jnp.zeros((ext, LANES), jnp.float32) for _ in range(nx // LANES)] for _ in range(3)]
    for t in range(t_n):
        tile = got_ref[(t_n + t) * s_n]
        for q in range(1, s_n):
            tile = tile + got_ref[(t_n + t) * s_n + q]
        if tile.shape[1] < LANES:
            tile = jnp.pad(tile, ((0, 0), (0, LANES - tile.shape[1])))
        h, at = t // per, (t % per) * cols
        inside = (lane >= at) & (lane < at + cols)
        for c in range(3):
            moved = pltpu.roll(tile, (at - c * cols) % LANES, 1) if (at - c * cols) % LANES else tile
            fields[c][h] = jnp.where(inside, moved, fields[c][h])
    whole = [jnp.concatenate(f, axis=1) for f in fields]
    wet, shift = mask_ref[...].astype(jnp.float32), cross_ref[...].astype(jnp.float32)
    if full:
        wind_ref, hb_ref, ha_ref, rim_ref, geo_ref, out_ref, edge_ref = refs
        own, ny = n[6], rim_ref.shape[3]
        low = lax.axis_index("spec") == 0
        for c in range(3):
            for k in range(2):
                edge_ref[c * 2 + k] = jnp.zeros((cols + 8, ny), jnp.float32)
                edge_ref[c * 2 + k, 4 : 4 + cols] = rim_ref[c, k]
                for m in range(2):
                    for ref, at in ((hb_ref, 2 + m), (ha_ref, 4 + cols + m)):
                        top, bottom = [m * 3 * own + c * own + j for j in (own - 2 + k, k)]
                        value = jnp.where(low, ref[top : top + 1, 0:ny], ref[bottom : bottom + 1, 0:ny])
                        edge_ref[c * 2 + k, at : at + 1] = value

        def joined(k, own):
            span = slice(NEAR * fd + k * HALO, NEAR * fd + (k + 1) * HALO)
            return jnp.concatenate([hb_ref[span], own, ha_ref[span]], axis=0)

        wet, shift = joined(0, wet), joined(3, shift)
        for c in range(2):
            out_ref[c * ext : (c + 1) * ext] = joined(1 + c, wind_ref[c])
    else:
        (geo_ref,) = refs
        edge = jnp.zeros((HALO, nx), jnp.float32)
        wet, shift = [jnp.concatenate([edge, x, edge], axis=0) for x in (wet, shift)]
    shift = jnp.broadcast_to(shift[:, 0:1].astype(jnp.int32), (ext, nx))
    u, v, sea = barrel(whole, shift, nx, True)
    depth = 10.0 + 4.0 * sea
    for k, value in enumerate((0.1 * u, 0.1 * v, 25.0 / (depth * depth), wet)):
        geo_ref[k * ext : (k + 1) * ext] = value


def advance(segments, fd, nx, s, table_ref, planes, store, splat, acc, sums, before=None):
    halves = nx // LANES
    lane = lanes_of((SUB, LANES))
    first, last = lane == 0, lane == LANES - 1
    acc[...] = jnp.zeros(acc.shape, jnp.float32)

    def body(i, carry):
        if before is not None:
            before(i)
        totals = {}

        def add(key, value):
            totals[key] = totals[key] + value if key in totals else value

        for k in range(UNROLL):
            at = pl.multiple_of((i * UNROLL + k) * SUB, SUB)
            sl = pl.ds(at, SUB)
            ge, gn = wide(table_ref[s, sl, GE : GE + 1]), wide(table_ref[s, sl, GN : GN + 1])
            bands = [wide(table_ref[s, sl, b : b + 1]) for b in (SX, SY, DX, DY)] if sums else None
            energy, growth = planes(at)
            for segment in segments:
                def state(r):
                    e = [energy(r, h) * splat[2, r + HALO, :, half(h)] for h in range(halves)]
                    north = [(gn + splat[1, r + HALO, :, half(h)]) * e[h] for h in range(halves)]
                    return e, north

                here, below = state(segment[0]), state(segment[0] - 1)
                flow = [jnp.maximum(below[1][h], 0.0) + jnp.minimum(here[1][h], 0.0) for h in range(halves)]
                for r in segment:
                    above = state(r + 1)
                    e, north = here
                    upper = [jnp.maximum(north[h], 0.0) + jnp.minimum(above[1][h], 0.0) for h in range(halves)]
                    east = [(ge + splat[0, r + HALO, :, half(h)]) * e[h] for h in range(halves)]
                    left = [pltpu.roll(x, LANES - 1, 1) for x in east]
                    flux = [
                        jnp.maximum(east[h], 0.0)
                        + jnp.minimum(jnp.where(last, left[h + 1] if h + 1 < halves else 0.0, left[h]), 0.0)
                        for h in range(halves)
                    ]
                    right = [pltpu.roll(x, 1, 1) for x in flux]
                    for h in range(halves):
                        behind = jnp.where(first, right[h - 1] if h else jnp.minimum(east[0], 0.0), right[h])
                        advected = (e[h] - (flux[h] - behind)) - (upper[h] - flow[h])
                        g = growth(r, h)
                        add((0, r, h), advected)
                        if sums:
                            pushed = (g - 1.0) * advected
                            grown = advected + pushed
                            for b in range(2):
                                add((1 + b, r, h), bands[b] * pushed)
                                add((3 + b, r, h), bands[2 + b] * grown)
                        else:
                            grown = g * advected
                        store(r, at, h, grown)
                    here, flow = above, upper
        for (kind, r, h), value in totals.items():
            acc[kind, r + HALO, :, half(h)] += value
        return carry

    lax.fori_loop(0, fd // (SUB * UNROLL), body, 0)


def folded(acc, kind, rows):
    return [jnp.sum(acc[kind, r + HALO], axis=0, keepdims=True) for r in rows]


def fill(splat, kind, row, value, nx):
    splat[kind, row + HALO] = jnp.broadcast_to(value, (SUB, nx))


def geometry(geo_ref, ext, kind, r):
    at = kind * ext + r + HALO
    return geo_ref[at : at + 1]


def write_totals(total_ref, acc, rows, previous, ext, nx):
    total_ref[...] = jnp.zeros((ext, nx), jnp.float32) if previous is None else previous[...]
    for r, value in zip(rows, folded(acc, 0, rows)):
        total_ref[r + HALO : r + HALO + 1] = value


def first_middle_kernel(n, table_ref, geo_ref, wind_ref, spectrum_ref,
                        out_ref, total_ref, growth_ref, raw, windb, splat, acc, sem):
    rows, fd, nx, chunks = n
    ext = rows + 2 * HALO
    s = lax.axis_index("spec")
    part = fd // chunks
    turns = part // (SUB * UNROLL)

    def copy(c):
        span = pl.ds(pl.multiple_of(c * part, SUB), part)
        return pltpu.make_async_copy(spectrum_ref.at[span], raw.at[span], sem.at[c])

    for c in range(chunks):
        copy(c).start()
    for c in range(2):
        for r in range(rows):
            windb[c, r] = jnp.broadcast_to(wind_ref[c, r : r + 1], (SUB, nx))
    for r in range(rows):
        for kind, source in ((0, 0), (1, 1), (2, 3)):
            fill(splat, kind, r, geometry(geo_ref, ext, source, r), nx)

    def before(i):
        @pl.when(i % turns == 0)
        def _():
            copy(i // turns).wait()

    def planes(at):
        sl = pl.ds(at, SUB)
        bw, we, wn = [wide(table_ref[s, sl, b : b + 1]) for b in (BW, WE, WN)]
        natural, grown = {}, {}
        for h in range(nx // LANES):
            natural[h] = jnp.swapaxes(raw[sl, :, half(h)], 0, 1)
            for r in range(rows):
                drive = we * windb[0, r, :, half(h)] + wn * windb[1, r, :, half(h)]
                grown[r, h] = 1.0 + jnp.maximum(drive - 0.05, 0.0)
                growth_ref[pl.ds(pl.multiple_of(r * fd + at, SUB), SUB), half(h)] = grown[r, h]
        return lambda r, h: bw * natural[h][r], lambda r, h: grown[r, h]

    def store(r, at, h, value):
        out_ref[pl.ds(pl.multiple_of((r - 1) * fd + at, SUB), SUB), half(h)] = value

    inner = list(range(1, rows - 1))
    advance([inner], fd, nx, s, table_ref, planes, store, splat, acc, False, before)
    write_totals(total_ref, acc, inner, None, ext, nx)


def step_kernel(n, cfg, *refs):
    rows, fd, nx, t_n, s_n, cols = n
    segments, source, growth, grow, raw, sums, joined, count = cfg
    ext = rows + 2 * HALO
    refs = list(refs)
    table_ref, geo_ref = refs.pop(0), refs.pop(0)
    wind_ref = refs.pop(0) if grow else None
    own_ref, got_ref = (None, None) if raw else (refs.pop(0), refs.pop(0))
    previous = refs.pop(0) if joined else None
    cross_ref = refs.pop(0) if sums else None
    operands, refs = refs[:count], refs[count:]
    out_ref, total_ref = refs.pop(0), refs.pop(0)
    growth_ref = refs.pop(0) if grow else None
    splat, acc = refs.pop(0), refs.pop(0)
    windb = refs.pop(0) if grow else None
    s = lax.axis_index("spec")
    order = [r for segment in segments for r in segment]
    needed = sorted({r + d for r in order for d in (-1, 0, 1)})
    breaking = geo_ref[3 * ext : 4 * ext]
    if not raw:
        breaking = breaking / (1.0 + (own_ref[...] + got_ref[...]) * geo_ref[2 * ext : 3 * ext])
    for r in needed:
        fill(splat, 0, r, geometry(geo_ref, ext, 0, r), nx)
        fill(splat, 1, r, geometry(geo_ref, ext, 1, r), nx)
        fill(splat, 2, r, breaking[r + HALO : r + HALO + 1], nx)
    for c in range(2):
        for k, r in enumerate(grow):
            at = c * ext + r + HALO
            windb[c, k] = jnp.broadcast_to(wind_ref[at : at + 1], (SUB, nx))

    def planes(at):
        sl = pl.ds(at, SUB)
        bw = wide(table_ref[s, sl, BW : BW + 1]) if raw else None
        we, wn = [wide(table_ref[s, sl, b : b + 1]) for b in (WE, WN)] if grow else (None, None)

        def energy(r, h):
            operand, first = source[r]
            value = operands[operand][pl.ds(pl.multiple_of(first + at, SUB), SUB), half(h)]
            return bw * value if raw else value

        def factor(r, h):
            if r in grow:
                k = grow.index(r)
                drive = we * windb[0, k, :, half(h)] + wn * windb[1, k, :, half(h)]
                value = 1.0 + jnp.maximum(drive - 0.05, 0.0)
                growth_ref[pl.ds(pl.multiple_of(k * fd + at, SUB), SUB), half(h)] = value
                return value
            operand, first = growth[r]
            return operands[operand][pl.ds(pl.multiple_of(first + at, SUB), SUB), half(h)]

        return energy, factor

    def store(r, at, h, value):
        out_ref[pl.ds(pl.multiple_of(order.index(r) * fd + at, SUB), SUB), half(h)] = value

    advance(segments, fd, nx, s, table_ref, planes, store, splat, acc, sums)
    if not sums:
        write_totals(total_ref, acc, order, previous, ext, nx)
        return
    kinds = [jnp.concatenate(folded(acc, kind, order), axis=0) for kind in range(acc.shape[0])]
    wet = jnp.where(s == 0, geo_ref[3 * ext + HALO : 3 * ext + HALO + rows], 0.0)
    shift = jnp.broadcast_to(cross_ref[:, 0:1], (rows, nx))
    moved = barrel(kinds + [wet], shift, nx, False)
    lane = lanes_of((rows, nx))
    size = cols + 8
    for t in range(t_n):
        chunk = jnp.zeros((rows, nx), jnp.float32)
        for q, value in enumerate(moved):
            amount = (q * size - (cols * t - 4)) % nx
            piece = pltpu.roll(value, amount, 1) if amount else value
            chunk = jnp.where((lane >= q * size) & (lane < (q + 1) * size), piece, chunk)
        for q in range(s_n):
            total_ref[(t_n + t) * s_n + q] = chunk
    mine = lax.axis_index("tile")
    for q in range(s_n):
        total_ref[mine * s_n + q] = kinds[0]


def last_kernel(n, table_ref, level_ref, got_ref, geo_ref, wave_ref, ocean_ref, sea_ref,
                hb_ref, ha_ref, lev_ref, waves_ref, next_ref,
                raw, brk, turn, field, mix, out, sem, osem):
    rows, fd, nx, t_n, s_n, cols, own, ny, chunks = n
    s = lax.axis_index("spec")
    g = lax.axis_index("grp")
    tile = lax.axis_index("tile")
    part = fd // chunks
    pad = turn.shape[0]
    size = cols + 8

    def write(c, source):
        return pltpu.make_async_copy(raw.at[pl.ds(source * part, part)], waves_ref.at[pl.ds(c * part, part)], sem.at[c])

    ocean_copy = pltpu.make_async_copy(out, next_ref, osem)

    @pl.when(g == 0)
    def _():
        total = got_ref[tile * s_n]
        for q in range(1, s_n):
            total = total + got_ref[tile * s_n + q]
        ext = rows + 2 * HALO
        wet = geo_ref[3 * ext + HALO : 3 * ext + HALO + rows]
        breaking = wet / (1.0 + total * geo_ref[2 * ext + HALO : 2 * ext + HALO + rows])
        for r in range(rows):
            brk[r] = jnp.broadcast_to(breaking[r : r + 1], (SUB, nx))
        for c in range(chunks):

            def finish(i, carry):
                for k in range(2):
                    at = pl.multiple_of(c * part + (2 * i + k) * SUB, SUB)
                    sl = pl.ds(at, SUB)
                    inv = wide(table_ref[s, sl, INV : INV + 1])
                    for h in range(nx // LANES):
                        spans = [pl.ds(pl.multiple_of(r * fd + at, SUB), SUB) for r in range(rows)]
                        values = [wave_ref[span, half(h)] for span in spans]
                        values = [value * brk[r, :, half(h)] * inv for r, value in enumerate(values)]
                        raw[sl, :, half(h)] = jnp.swapaxes(jnp.stack(values), 0, 1)
                return carry

            lax.fori_loop(0, part // (2 * SUB), finish, 0)
            write(c, c).start()
        out[...] = jnp.zeros((3, own, cols, ny), jnp.float32)
        ocean_copy.start()
        ocean_copy.wait()
        for c in range(chunks):
            write(c, c).wait()

    @pl.when(g == 1)
    def _():
        def clear(i, carry):
            raw[pl.ds(pl.multiple_of(i * SUB, SUB), SUB)] = jnp.zeros((SUB, rows, nx), jnp.float32)
            return carry

        lax.fori_loop(0, part // SUB, clear, 0)
        for c in range(chunks):
            write(c, 0).start()

        if pad > ny:
            turn[ny:pad] = jnp.zeros((pad - ny, nx), jnp.float32)
        for t in range(t_n):
            tilev = got_ref[t * s_n]
            for q in range(1, s_n):
                tilev = tilev + got_ref[t * s_n + q]
            turn[t * rows : (t + 1) * rows] = tilev
        turned = jnp.transpose(turn[...])
        total, sx, sy, dx, dy, wet = [turned[q * size : (q + 1) * size] for q in range(6)]
        row = lax.broadcasted_iota(jnp.int32, (size, pad), 0)
        column = row + (tile * cols - 4)
        wet = jnp.where((column >= 0) & (column < t_n * cols), wet, 0.0)
        stack = 3 * own
        mix[0] = jnp.zeros((size, pad), jnp.float32)
        mix[0, 4 : 4 + cols, 0:ny] = sea_ref[...]
        mix[0, 2:4, 0:ny] = hb_ref[2 * stack : 2 * stack + 2, 0:ny]
        mix[0, 4 + cols : 6 + cols, 0:ny] = ha_ref[2 * stack : 2 * stack + 2, 0:ny]
        depth = 10.0 + 4.0 * mix[0]
        breaking = 1.0 / (1.0 + 25.0 * total / (depth * depth))
        swept = wet * breaking
        sx, sy, dx, dy = sx * breaking, sy * breaking, dx * swept, dy * swept

        field[...] = jnp.zeros(field.shape, jnp.float32)
        ext = own + 4
        for c in range(3):
            for k in range(own):
                l = c * ext + 2 + k
                field[l, 4 : 4 + cols, 0:ny] = ocean_ref[c, k]
                for m in range(2):
                    at = m * stack + c * own + k
                    field[l, 2 + m : 3 + m, 0:ny] = hb_ref[at : at + 1, 0:ny]
                    field[l, 4 + cols + m : 5 + cols + m, 0:ny] = ha_ref[at : at + 1, 0:ny]
        for upper in range(2):
            @pl.when(s == 1 - upper)
            def _():
                for c in range(3):
                    for k in range(2):
                        l = c * ext + (own + 2 if upper else 0) + k
                        field[l, :, 0:ny] = lev_ref[c * 2 + k]

        lane = lanes_of((size, pad))

        def new_fields(source, k):
            values = []
            for c in range(3):
                q = source[c * ext + k]
                lateral = (
                    pltpu.roll(q, size - 1, 0)
                    + pltpu.roll(q, 1, 0)
                    + jnp.where(lane == ny - 1, 0.0, pltpu.roll(q, pad - 1, 1))
                    + jnp.where(lane == 0, 0.0, pltpu.roll(q, 1, 1))
                    - 4.0 * q
                )
                vertical = source[c * ext + k + 1] + source[c * ext + k - 1] - 2.0 * q
                values.append((q, q + 0.1 * lateral + 0.2 * vertical))
            (u, du), (v, dv), (_, dt) = values
            shaped = level_ref[s, 1, k]
            top = jnp.where((s == 0) & (k == 2), 1.0, 0.0)
            east = du + 0.1 * (v + shaped * dy) + top * sx
            north = dv - 0.1 * (u + shaped * dx) + top * sy
            keep = wet * level_ref[s, 2, k]
            return keep * east, keep * north, keep * dt

        for k in range(1, ext - 1):
            for c, value in enumerate(new_fields(field, k)):
                mix[c * ext + k] = value
        for k in range(2, ext - 2):
            for c, value in enumerate(new_fields(mix, k)):
                out[c, k - 2] = value[4 : 4 + cols, 0:ny]
        ocean_copy.start()
        ocean_copy.wait()
        for c in range(chunks):
            write(c, 0).wait()


def program(spectrum, wind, land_mask, intersection, ocean_state, sea_level, *, mesh_shape):
    g_n, t_n, s_n = (mesh_shape[a] for a in AXES)
    _, freqs, dirs, rows, nx = spectrum.shape
    _, _, own, cols, ny = ocean_state.shape
    fd = freqs * dirs
    devices = g_n * t_n * s_n
    table = jnp.asarray(wave_table(freqs, dirs * s_n, s_n))
    levels = jnp.asarray(level_table(own * s_n, s_n, own))
    ocean = ocean_state[0]
    sea = sea_level[0]

    def in_hbm(x):
        return pltpu.with_memory_space_constraint(x, pltpu.HBM)

    natural = in_hbm(spectrum.reshape(fd, rows, nx))
    chunks = 6
    vm = pltpu.VMEM
    params = pltpu.CompilerParams(vmem_limit_bytes=24 << 20)

    def up(x):
        return lax.ppermute(x, "tile", [(i, i + 1) for i in range(t_n - 1)])

    def down(x):
        return lax.ppermute(x, "tile", [(i + 1, i) for i in range(t_n - 1)])

    def others(x):
        return added(lax.ppermute(x, "spec", [(i, (i + k) % s_n) for i in range(s_n)]) for k in range(1, s_n))

    def added(values):
        return functools.reduce(lambda a, b: a + b, values)

    def call(kernel, args, specs, shapes, out_specs, scratch):
        return pl.pallas_call(
            kernel, out_shape=shapes, in_specs=specs, out_specs=out_specs,
            scratch_shapes=scratch, compiler_params=params,
        )(*args)

    ext = rows + 2 * HALO
    near, far = f32(NEAR * fd + 4 * HALO, nx), f32((HALO - NEAR) * fd, nx)

    def hbm(shape):
        return pltpu.HBM(shape.shape, shape.dtype)

    send, level_rim, near_lo, near_hi, far_lo, far_hi = call(
        functools.partial(start_kernel, (t_n, s_n, rows, cols, own, ny, fd, nx, chunks)),
        (levels, natural, in_hbm(ocean.reshape(3 * own, cols, ny)), in_hbm(sea), in_hbm(land_mask), in_hbm(wind), in_hbm(intersection)),
        [SM] + [HB] * 6,
        (f32(devices, ext, 4 * cols), f32(3, 2, cols, ny), hbm(near), hbm(near), hbm(far), hbm(far)),
        (VM,) * 2 + (HB,) * 4,
        [vm((fd, rows, nx), jnp.float32), vm((3 * own, cols, ny), jnp.float32), vm((cols, ny), jnp.float32),
         vm((rows, nx), jnp.int32), vm((2, rows, nx), jnp.float32), vm((rows, nx), jnp.int32),
         vm(near.shape, jnp.float32), vm(near.shape, jnp.float32), vm(far.shape, jnp.float32), vm(far.shape, jnp.float32),
         pltpu.SemaphoreType.DMA((chunks + 5,)), pltpu.SemaphoreType.DMA((chunks, 4, 3))],
    )
    hb, ha = up(near_hi), down(near_lo)
    arrived = lax.all_to_all(send, AXES, 0, 0, tiled=True)
    hbf, haf = up(far_hi), down(far_lo)

    geo = call(
        functools.partial(pick_kernel, (t_n, s_n, rows, cols, nx, fd), False),
        (arrived, land_mask, intersection), [VM] * 3, f32(4 * ext, nx), VM, [],
    )

    def scratch(kinds, grow):
        result = [vm((3, ext, SUB, nx), jnp.float32), vm((kinds, ext, SUB, nx), jnp.float32)]
        return result + [vm((2, grow, SUB, nx), jnp.float32)] if grow else result

    mid, total, growth0 = call(
        functools.partial(first_middle_kernel, (rows, fd, nx, chunks)),
        (table, geo, wind, natural), [VM] * 3 + [HB],
        (f32((rows - 2) * fd, nx), f32(ext, nx), f32(rows * fd, nx)), (VM,) * 3,
        [vm((fd, rows, nx), jnp.float32), vm((2, rows, SUB, nx), jnp.float32)] + scratch(1, 0)
        + [pltpu.SemaphoreType.DMA((chunks,))],
    )
    geo, winds, level_rim = call(
        functools.partial(pick_kernel, (t_n, s_n, rows, cols, nx, fd, own), True),
        (arrived, land_mask, intersection, wind, hb, ha, level_rim), [VM] * 7,
        (f32(4 * ext, nx), f32(2 * ext, nx), f32(6, cols + 8, ny)), (VM,) * 3, [],
    )

    planes = {k: {} for k in range(WSTEPS + 1)}
    for j in range(HALO):
        for base, sign, (a, b) in ((-1, -1, (hb, hbf)), (rows, 1, (ha, haf))):
            planes[0][base + sign * j] = (a if j < NEAR else b, (j % NEAR) * fd)
    for j in range(NEAR):
        planes[0][j] = (near_lo, j * fd)
        planes[0][rows - 1 - j] = (near_hi, j * fd)
    for k, r in enumerate(range(1, rows - 1)):
        planes[1][r] = (mid, k * fd)
    grown = {r: (growth0, r * fd) for r in range(rows)}
    totals, gots = {1: total}, {}

    def advanced(step, segments, exchange=True):
        raw, sums = step == 1, step == WSTEPS
        order = [r for segment in segments for r in segment]
        grow = [r for r in order if r not in grown]
        operands = []

        def place(pair):
            for k, array in enumerate(operands):
                if array is pair[0]:
                    return k, pair[1]
            operands.append(pair[0])
            return len(operands) - 1, pair[1]

        source = {r: place(planes[step - 1][r]) for r in sorted({r + d for r in order for d in (-1, 0, 1)})}
        growth = {r: place(grown[r]) for r in order if r in grown}
        args = [table, geo]
        if grow:
            args.append(winds)
        if not raw:
            args += [totals[step - 1], gots[step - 1]]
        joined = step in totals
        if joined:
            args.append(totals[step])
        if sums:
            args.append(intersection)
        args += operands
        shapes = [f32(len(order) * fd, nx), f32(devices, rows, nx) if sums else f32(ext, nx)]
        if grow:
            shapes.append(f32(len(grow) * fd, nx))
        cfg = (segments, source, growth, grow, raw, sums, joined, len(operands))
        outs = call(
            functools.partial(step_kernel, (rows, fd, nx, t_n, s_n, cols), cfg),
            args, [VM] * len(args), tuple(shapes), (VM,) * len(shapes), scratch(5 if sums else 1, len(grow)),
        )
        for k, r in enumerate(order):
            planes[step][r] = (outs[0], k * fd)
        for k, r in enumerate(grow):
            grown[r] = (outs[2], k * fd)
        totals[step] = outs[1]
        if exchange and not sums:
            gots[step] = others(outs[1])

    def pair(first, last):
        return [list(range(first, last + 1)), list(range(rows - 1 - last, rows - first))]

    advanced(1, pair(-1, 0))
    advanced(2, [list(range(rows))])
    advanced(3, [list(range(1, rows - 1))], exchange=False)
    level_got = others(level_rim)
    advanced(1, pair(-3, -2))
    advanced(2, pair(-2, -1))
    advanced(3, pair(-1, 0))
    totals[3], level_got = lax.optimization_barrier((totals[3], level_got))
    advanced(4, [list(range(rows))])

    landed = lax.all_to_all(totals[WSTEPS], AXES, 0, 0, tiled=True)
    pad = -(-ny // LANES) * LANES
    size = cols + 8
    ins = (table, levels, landed, geo, planes[WSTEPS][0][0], ocean, sea, hb, ha, level_got)
    waves, fields = call(
        functools.partial(last_kernel, (rows, fd, nx, t_n, s_n, cols, own, ny, chunks)),
        ins, [VM, SM] + [VM] * (len(ins) - 2), (f32(fd, rows, nx), f32(3, own, cols, ny)), (HB, HB),
        [
            vm((fd, rows, nx), jnp.float32),
            vm((rows, SUB, nx), jnp.float32),
            vm((pad, nx), jnp.float32),
            vm((3 * (own + 4), size, pad), jnp.float32),
            vm((3 * (own + 4), size, pad), jnp.float32),
            vm((3, own, cols, ny), jnp.float32),
            pltpu.SemaphoreType.DMA((chunks,)),
            pltpu.SemaphoreType.DMA,
        ],
    )
    return waves.reshape(spectrum.shape), fields.reshape(ocean_state.shape)


def solution(mesh):
    return jax.shard_map(
        functools.partial(program, mesh_shape=dict(mesh.shape)),
        mesh=mesh,
        in_specs=(
            P("grp", None, "spec", "tile", None),
            P(None, "tile", None),
            P("tile", None),
            P("tile", None),
            P("grp", None, "spec", "tile", None),
            P("grp", "tile", None),
        ),
        out_specs=(P("grp", None, "spec", "tile", None), P("grp", None, "spec", "tile", None)),
        check_vma=False,
    )
```

time: 142 us -> 145 us (1.021)
  blocking collectives: 20.9 us -> 65.4 us
  starting transfers between devices: 57.8 us -> 16.8 us
  waiting for transfers between devices: 7.34 us -> 3.31 us
  Pallas kernels: 53.5 us -> 57.3 us
    all_to_all x1 -> x2, blocking collectives: 20.9 us -> 65.4 us  [the longest x1 51 us: program(): arrived = lax.all_to_all(send, AXES, 0, 0, tiled=True)]
    ppermute x6 -> x0, starting transfers between devices: 19.2 us -> none  [crossed(): lax.ppermute(x, ('tile', 'spec'), [(a * s_n + q, b * s_n + (q + k) % s_n)...]
    ppermute x5 -> x2, starting transfers between devices: 19.7 us -> 7.73 us  [up(): return lax.ppermute(x, 'tile', [(i, i + 1) for i in range(t_n - 1)])]
    all_to_all x1 -> x0, starting transfers between devices: 7.95 us -> none  [body(): arrived = lax.all_to_all(send, AXES, 0, 0, tiled=True)]
    all_to_all x1 -> x0, waiting for transfers between devices: 7.28 us -> none  [body(): arrived = lax.all_to_all(send, AXES, 0, 0, tiled=True)]
    ppermute x5 -> x2, starting transfers between devices: 6.46 us -> 2.58 us  [down(): return lax.ppermute(x, 'tile', [(i + 1, i) for i in range(t_n - 1)])]
    pallas_call x11 -> x12, Pallas kernels: 53.5 us -> 57.3 us  [call(): pl.pallas_call(kernel, out_shape=shapes, in_specs=specs, out_specs=out_sp...]
    ppermute x4 -> x6, waiting for transfers between devices: 0.01 us -> 3.3 us  [others(): lax.ppermute(x, 'spec', [(i, (i + k) % s_n) for i in range(s_n)])]
  transfers between devices with their start and end apart: 21 -> 10, of which waited for: 1 -> 1; matrix products, arithmetic and copies ran while one was open for 0% -> 0% of each run, Pallas kernels for 17% -> 27%
where the time goes in v2:
time: 145 us; the launch traced here: 144 us
  blocking collectives  65.4 us (45%)
  Pallas kernels  57.3 us (40%)
  starting transfers between devices  16.8 us (12%)
  waiting for transfers between devices  3.31 us (2%)
    pallas_call x12, Pallas kernels, call(): pl.pallas_call(kernel, out_shape=shapes, in_specs=specs, out_specs=out_sp...  57.3 us
    all_to_all x1, blocking collectives, program(): arrived = lax.all_to_all(send, AXES, 0, 0, tiled=True)  51 us
    all_to_all x1, blocking collectives, program(): landed = lax.all_to_all(totals[WSTEPS], AXES, 0, 0, tiled=True)  14.4 us
    ppermute x2, starting transfers between devices, up(): return lax.ppermute(x, 'tile', [(i, i + 1) for i in range(t_n - 1)])  7.73 us
    ppermute x6, starting transfers between devices, others(): lax.ppermute(x, 'spec', [(i, (i + k) % s_n) for i in range(s_n)])  6.47 us
    ppermute x6, waiting for transfers between devices, others(): lax.ppermute(x, 'spec', [(i, (i + k) % s_n) for i in range(s_n)])  3.3 us
  transfers between devices with their start and end apart: 10, of which 1 were waited for; matrix products, arithmetic and copies ran while one was open for 0% of the time, Pallas kernels for 27%

profile of v2, /device:TPU:0, one launch (start us, length us, event | category | flops | bytes accessed | tf_op | source)
XLA Modules:
  0.0 144.3 jit_solution(15697065377162515370)
XLA Ops:
  0.6 0.0 copy-start.8
  0.6 0.7 copy-done.8
  1.3 5.2 %shard_map.95 = (f32[32,16,128]{2,1,0:T(8,128)S(1)}, f32[3,2,32,64]{3,2,1,0:T(8,128)S(1)}, f32[1168,256]{1,0:T(8,128)}, f32[1168,256]{1,0:T(8,128)}, f32[1152,256]{1,0:T(8,128)}, /*index=5*/f32[1152,256]{1,0:T(8,128)}) custom-call(f32[2,3,12]{2,1,0:T(4,128)S(1)} %copy-done.8, f32[576,8,256]{2,1,0:T(8,128)} %bitcast.10, f32[24,32,64]{2,1,0:T(8,128)} %bitcast.6, ...), custom_call_target="tpu_custom_call" | custom-call | tf_op jit(solution)/shard_map/pallas_call | solution.py:605
  6.5 0.0 copy-start
  6.5 2.6 %collective-permute-start = (f32[1168,256]{1,0:T(8,128)}, f32[1168,256]{1,0:T(8,128)S(1)}, u32[]{:S(2)}, u32[]{:S(2)}) collective-permute-start(f32[1168,256]{1,0:T(8,128)} %get-tuple-element.35.refs_6_), channel_id=1, source_target_pairs={{0,2},{2,4},{4,6},{6,8},{8,10},{10,12},{12,14},{1,3},{3,5},{5,7},{... | collective-permute-start | bytes 3588104 | tf_op jit(solution)/shard_map/ppermute | solution.py:593
  9.2 1.3 collective-permute-start.1
  10.5 5.1 %collective-permute-start.2 = (f32[1152,256]{1,0:T(8,128)}, f32[1152,256]{1,0:T(8,128)S(1)}, u32[]{:S(2)}, u32[]{:S(2)}) collective-permute-start(f32[1152,256]{1,0:T(8,128)} %get-tuple-element.43), channel_id=1, source_target_pairs={{0,2},{2,4},{4,6},{6,8},{8,10},{10,12},{12,14},{1,3},{3,5},{5,7},{... | collective-permute-start | bytes 3538952 | tf_op jit(solution)/shard_map/ppermute | solution.py:593
  15.6 1.3 collective-permute-start.3
  16.9 51.0 %all_to_all.10.got_ref = f32[32,16,128]{2,1,0:T(8,128)S(1)} all-to-all(f32[32,16,128]{2,1,0:T(8,128)S(1)} %get-tuple-element.34), channel_id=1, replica_groups=mesh['grp'=2,'tile'=8,'spec'=2] {'grp','tile','spec'}, dimensions={0} | all-to-all | bytes 524288 | tf_op jit(solution)/shard_map/all_to_all | solution.py:628
  67.9 0.0 collective-permute-done.refs_1_.refs_4_.refs_5_.hb_ref
  67.9 0.0 collective-permute-done.1.refs_2_.refs_7_.refs_6_.ha_ref
  67.9 0.0 copy-done.4
  67.9 0.0 copy-done.5
  67.9 0.0 copy-done.6
  68.0 0.6 shard_map.96
  68.6 1.6 %collective-permute-start.8 = (f32[6,40,64]{2,1,0:T(8,128)S(1)}, f32[6,40,64]{2,1,0:T(8,128)S(1)}, u32[]{:S(2)}, u32[]{:S(2)}) collective-permute-start(f32[6,40,64]{2,1,0:T(8,128)S(1)} %get-tuple-element.57), channel_id=1, source_target_pairs={{0,1},{1,0},{2,3},{3,2},{4,5},{5,4},{6,7},{7,6},{8,9},{9,8},{10,11... | collective-permute-start | bytes 184328 | tf_op jit(solution)/shard_map/ppermute | solution.py:599
  70.2 0.6 shard_map.97.geo_ref
  70.8 0.0 copy-done
  70.8 0.0 copy-start.2
  70.8 0.0 copy-start.3
  70.8 7.1 %shard_map.98 = (f32[3456,256]{1,0:T(8,128)S(1)}, f32[16,256]{1,0:T(8,128)S(1)}, f32[4608,256]{1,0:T(8,128)S(1)}) custom-call(f32[2,576,16]{2,1,0:T(8,128)S(1)} %copy-done, f32[64,256]{1,0:T(8,128)S(1)} %shard_map.97.geo_ref, f32[2,8,256]{2,1,0:T(8,128)S(1)} %copy-done.4, f32[576,8,256]{2,1,0:T(8,128)} %bitcast.11), custom_call_target="tpu_custom_call" | custom-call | tf_op jit(solution)/shard_map/pallas_call | solution.py:605
  78.0 0.0 copy-done.2
  78.0 0.0 copy-done.3
  78.0 4.8 %shard_map.99 = (f32[2304,256]{1,0:T(8,128)S(1)}, f32[16,256]{1,0:T(8,128)S(1)}, f32[1152,256]{1,0:T(8,128)S(1)}) custom-call(f32[2,576,16]{2,1,0:T(8,128)S(1)} %copy-done, f32[64,256]{1,0:T(8,128)S(1)} %get-tuple-element.38.refs_1_.geo_ref, f32[32,256]{1,0:T(8,128)S(1)} %get-tuple-element.39.refs_2_, f32[16,256]{1,0:T(8,128)S(1)} %get-tuple-element.40.refs_3_, ...), custom_call_target="tpu_custom_call" | custom-call | tf_op jit(solution)/shard_map/pallas_call | solution.py:605
  82.8 0.5 collective-permute-start.5
  83.3 0.0 collective-permute-done.2.refs_4_
  83.3 0.0 collective-permute-done.3.refs_7_
  83.3 4.8 %shard_map.100 = (f32[2304,256]{1,0:T(8,128)S(1)}, f32[16,256]{1,0:T(8,128)S(1)}, f32[2304,256]{1,0:T(8,128)S(1)}) custom-call(f32[2,576,16]{2,1,0:T(8,128)S(1)} %copy-done, f32[64,256]{1,0:T(8,128)S(1)} %get-tuple-element.38.refs_1_.geo_ref, f32[32,256]{1,0:T(8,128)S(1)} %get-tuple-element.39.refs_2_, f32[16,256]{1,0:T(8,128)S(1)} %get-tuple-element.42.refs_3_.refs_2_, ...), custom_call_target="tpu_custom_call" | custom-call | tf_op jit(solution)/shard_map/pallas_call | solution.py:605
  88.1 1.6 %collective-permute-start.4 = (f32[16,256]{1,0:T(8,128)S(1)}, f32[16,256]{1,0:T(8,128)S(1)}, u32[]{:S(2)}, u32[]{:S(2)}) collective-permute-start(f32[16,256]{1,0:T(8,128)S(1)} %get-tuple-element.45.refs_2_), channel_id=1, source_target_pairs={{0,1},{1,0},{2,3},{3,2},{4,5},{5,4},{6,7},{7,6},{8,9},{9,8},{10,11... | collective-permute-start | bytes 49160 | tf_op jit(solution)/shard_map/ppermute | solution.py:599
  89.7 0.0 collective-permute-done.5.refs_3_
  89.7 6.0 %shard_map.101 = (f32[4608,256]{1,0:T(8,128)S(1)}, f32[16,256]{1,0:T(8,128)S(1)}) custom-call(f32[2,576,16]{2,1,0:T(8,128)S(1)} %copy-done, f32[64,256]{1,0:T(8,128)S(1)} %get-tuple-element.38.refs_1_.geo_ref, f32[16,256]{1,0:T(8,128)S(1)} %get-tuple-element.42.refs_3_.refs_2_, f32[16,256]{1,0:T(8,128)S(1)} %collective-permute-done.5.refs_3_, ...), custom_call_target="tpu_custom_call" | custom-call | tf_op jit(solution)/shard_map/pallas_call | solution.py:605
  95.7 0.5 collective-permute-start.7
  96.2 0.0 collective-permute-done.4.refs_3_
  96.2 4.7 %shard_map.102 = (f32[2304,256]{1,0:T(8,128)S(1)}, f32[16,256]{1,0:T(8,128)S(1)}) custom-call(f32[2,576,16]{2,1,0:T(8,128)S(1)} %copy-done, f32[64,256]{1,0:T(8,128)S(1)} %get-tuple-element.38.refs_1_.geo_ref, f32[16,256]{1,0:T(8,128)S(1)} %get-tuple-element.45.refs_2_, f32[16,256]{1,0:T(8,128)S(1)} %collective-permute-done.4.refs_3_, ...), custom_call_target="tpu_custom_call" | custom-call | tf_op jit(solution)/shard_map/pallas_call | solution.py:605
  100.9 1.6 %collective-permute-start.6 = (f32[16,256]{1,0:T(8,128)S(1)}, f32[16,256]{1,0:T(8,128)S(1)}, u32[]{:S(2)}, u32[]{:S(2)}) collective-permute-start(f32[16,256]{1,0:T(8,128)S(1)} %get-tuple-element.52.refs_2_), channel_id=1, source_target_pairs={{0,1},{1,0},{2,3},{3,2},{4,5},{5,4},{6,7},{7,6},{8,9},{9,8},{10,11... | collective-permute-start | bytes 49160 | tf_op jit(solution)/shard_map/ppermute | solution.py:599
  102.6 0.0 collective-permute-done.7.refs_3_
  102.6 5.2 %shard_map.103 = (f32[3456,256]{1,0:T(8,128)S(1)}, f32[16,256]{1,0:T(8,128)S(1)}) custom-call(f32[2,576,16]{2,1,0:T(8,128)S(1)} %copy-done, f32[64,256]{1,0:T(8,128)S(1)} %get-tuple-element.38.refs_1_.geo_ref, f32[16,256]{1,0:T(8,128)S(1)} %get-tuple-element.48.refs_4_.refs_2_, f32[16,256]{1,0:T(8,128)S(1)} %collective-permute-done.7.refs_3_, ...), custom_call_target="tpu_custom_call" | custom-call | tf_op jit(solution)/shard_map/pallas_call | solution.py:605
  107.8 0.0 collective-permute-done.6.refs_3_
  107.8 4.8 %shard_map.104 = (f32[2304,256]{1,0:T(8,128)S(1)}, f32[16,256]{1,0:T(8,128)S(1)}) custom-call(f32[2,576,16]{2,1,0:T(8,128)S(1)} %copy-done, f32[64,256]{1,0:T(8,128)S(1)} %get-tuple-element.38.refs_1_.geo_ref, f32[16,256]{1,0:T(8,128)S(1)} %get-tuple-element.52.refs_2_, f32[16,256]{1,0:T(8,128)S(1)} %collective-permute-done.6.refs_3_, ...), custom_call_target="tpu_custom_call" | custom-call | tf_op jit(solution)/shard_map/pallas_call | solution.py:605
  112.6 0.5 collective-permute-start.9
  113.1 0.0 collective-permute-done.8.lev_ref
  113.1 3.3 %collective-permute-done.9.refs_3_ = f32[16,256]{1,0:T(8,128)S(1)} collective-permute-done((f32[16,256]{1,0:T(8,128)S(1)}, f32[16,256]{1,0:T(8,128)S(1)}, u32[]{:S(2)}, u32[]{:S(2)}) %collective-permute-start.9) | collective-permute-done | bytes 16416 | tf_op jit(solution)/shard_map/ppermute | solution.py:599
  116.4 8.2 %shard_map.105 = (f32[4608,256]{1,0:T(8,128)S(1)}, f32[32,8,256]{2,1,0:T(8,128)S(1)}) custom-call(f32[2,576,16]{2,1,0:T(8,128)S(1)} %copy-done, f32[64,256]{1,0:T(8,128)S(1)} %get-tuple-element.38.refs_1_.geo_ref, f32[16,256]{1,0:T(8,128)S(1)} %get-tuple-element.58.refs_2_, f32[16,256]{1,0:T(8,128)S(1)} %collective-permute-done.9.refs_3_, ...), custom_call_target="tpu_custom_call" | custom-call | tf_op jit(solution)/shard_map/pallas_call | solution.py:605
  124.6 14.4 %all_to_all.11.got_ref = f32[32,8,256]{2,1,0:T(8,128)S(1)} all-to-all(f32[32,8,256]{2,1,0:T(8,128)S(1)} %get-tuple-element.61), channel_id=1, replica_groups=mesh['grp'=2,'tile'=8,'spec'=2] {'grp','tile','spec'}, dimensions={0} | all-to-all | bytes 524288 | tf_op jit(solution)/shard_map/all_to_all | solution.py:720
  139.0 0.0 copy-done.1
  139.0 0.0 copy-done.7
  139.0 0.0 copy-done.9
  139.0 5.3 %shard_map.106 = (f32[576,8,256]{2,1,0:T(8,128)}, f32[3,8,32,64]{3,2,1,0:T(8,128)}) custom-call(f32[2,576,16]{2,1,0:T(8,128)S(1)} %copy-done, f32[2,3,12]{2,1,0:T(4,128)S(1)} %copy-done.9, f32[32,8,256]{2,1,0:T(8,128)S(1)} %all_to_all.11.got_ref, f32[64,256]{1,0:T(8,128)S(1)} %get-tuple-element.38.refs_1_.geo_ref, ...), custom_call_target="tpu_custom_call" | custom-call | tf_op jit(solution)/shard_map/pallas_call | solution.py:605
  (6 shorter events, 0.0 us)
Async XLA Ops:
  0.6 0.7 copy-start.8
  1.3 66.6 %copy-start.4 = (f32[2,8,256]{2,1,0:T(8,128)S(1)}, f32[2,8,256]{2,1,0:T(8,128)}, u32[]{:S(2)}) copy-start(f32[2,8,256]{2,1,0:T(8,128)} %wind_ref.1) | copy-start | bytes 49156
  1.3 66.6 %copy-start.5 = (s32[8,256]{1,0:T(8,128)S(1)}, s32[8,256]{1,0:T(8,128)}, u32[]{:S(2)}) copy-start(s32[8,256]{1,0:T(8,128)} %refs_4_.1) | copy-start | bytes 24580
  1.3 66.6 %copy-start.6 = (s32[8,256]{1,0:T(8,128)S(1)}, s32[8,256]{1,0:T(8,128)}, u32[]{:S(2)}) copy-start(s32[8,256]{1,0:T(8,128)} %mask_ref.3) | copy-start | bytes 24580
  6.5 64.3 %copy-start = (f32[2,576,16]{2,1,0:T(8,128)S(1)}, f32[2,576,16]{2,1,0:T(8,128)}, u32[]{:S(2)}) copy-start(f32[2,576,16]{2,1,0:T(8,128)} %constant.4.clone.table_ref.refs_0_) | copy-start | bytes 221188
  6.5 61.4 %collective-permute-start = (f32[1168,256]{1,0:T(8,128)}, f32[1168,256]{1,0:T(8,128)S(1)}, u32[]{:S(2)}, u32[]{:S(2)}) collective-permute-start(f32[1168,256]{1,0:T(8,128)} %get-tuple-element.35.refs_6_), channel_id=1, source_target_pairs={{0,2},{2,4},{4,6},{6,8},{8,10},{10,12},{12,14},{1,3},{3,5},{5,7},{... | collective-permute-start | bytes 3588104 | tf_op jit(solution)/shard_map/ppermute | solution.py:593
  9.2 58.8 %collective-permute-start.1 = (f32[1168,256]{1,0:T(8,128)}, f32[1168,256]{1,0:T(8,128)S(1)}, u32[]{:S(2)}, u32[]{:S(2)}) collective-permute-start(f32[1168,256]{1,0:T(8,128)} %get-tuple-element.36.refs_5_), channel_id=1, source_target_pairs={{2,0},{4,2},{6,4},{8,6},{10,8},{12,10},{14,12},{3,1},{5,3},{7,5},{... | collective-permute-start | bytes 3588104 | tf_op jit(solution)/shard_map/ppermute | solution.py:596
  10.5 72.8 %collective-permute-start.2 = (f32[1152,256]{1,0:T(8,128)}, f32[1152,256]{1,0:T(8,128)S(1)}, u32[]{:S(2)}, u32[]{:S(2)}) collective-permute-start(f32[1152,256]{1,0:T(8,128)} %get-tuple-element.43), channel_id=1, source_target_pairs={{0,2},{2,4},{4,6},{6,8},{8,10},{10,12},{12,14},{1,3},{3,5},{5,7},{... | collective-permute-start | bytes 3538952 | tf_op jit(solution)/shard_map/ppermute | solution.py:593
  15.6 67.7 %collective-permute-start.3 = (f32[1152,256]{1,0:T(8,128)}, f32[1152,256]{1,0:T(8,128)S(1)}, u32[]{:S(2)}, u32[]{:S(2)}) collective-permute-start(f32[1152,256]{1,0:T(8,128)} %get-tuple-element.44), channel_id=1, source_target_pairs={{2,0},{4,2},{6,4},{8,6},{10,8},{12,10},{14,12},{3,1},{5,3},{7,5},{... | collective-permute-start | bytes 3538952 | tf_op jit(solution)/shard_map/ppermute | solution.py:596
  68.6 44.6 %collective-permute-start.8 = (f32[6,40,64]{2,1,0:T(8,128)S(1)}, f32[6,40,64]{2,1,0:T(8,128)S(1)}, u32[]{:S(2)}, u32[]{:S(2)}) collective-permute-start(f32[6,40,64]{2,1,0:T(8,128)S(1)} %get-tuple-element.57), channel_id=1, source_target_pairs={{0,1},{1,0},{2,3},{3,2},{4,5},{5,4},{6,7},{7,6},{8,9},{9,8},{10,11... | collective-permute-start | bytes 184328 | tf_op jit(solution)/shard_map/ppermute | solution.py:599
  70.8 7.1 %copy-start.2 = (f32[1168,256]{1,0:T(8,128)S(1)}, f32[1168,256]{1,0:T(8,128)}, u32[]{:S(2)}) copy-start(f32[1168,256]{1,0:T(8,128)} %get-tuple-element.36.refs_5_) | copy-start | bytes 3588100
  70.8 7.1 %copy-start.3 = (f32[1168,256]{1,0:T(8,128)S(1)}, f32[1168,256]{1,0:T(8,128)}, u32[]{:S(2)}) copy-start(f32[1168,256]{1,0:T(8,128)} %get-tuple-element.35.refs_6_) | copy-start | bytes 3588100
  82.8 7.0 %collective-permute-start.5 = (f32[16,256]{1,0:T(8,128)S(1)}, f32[16,256]{1,0:T(8,128)S(1)}, u32[]{:S(2)}, u32[]{:S(2)}) collective-permute-start(f32[16,256]{1,0:T(8,128)S(1)} %get-tuple-element.42.refs_3_.refs_2_), channel_id=1, source_target_pairs={{0,1},{1,0},{2,3},{3,2},{4,5},{5,4},{6,7},{7,6},{8,9},{9,8},{10,11... | collective-permute-start | bytes 49160 | tf_op jit(solution)/shard_map/ppermute | solution.py:599
  88.1 8.1 %collective-permute-start.4 = (f32[16,256]{1,0:T(8,128)S(1)}, f32[16,256]{1,0:T(8,128)S(1)}, u32[]{:S(2)}, u32[]{:S(2)}) collective-permute-start(f32[16,256]{1,0:T(8,128)S(1)} %get-tuple-element.45.refs_2_), channel_id=1, source_target_pairs={{0,1},{1,0},{2,3},{3,2},{4,5},{5,4},{6,7},{7,6},{8,9},{9,8},{10,11... | collective-permute-start | bytes 49160 | tf_op jit(solution)/shard_map/ppermute | solution.py:599
  95.7 6.9 %collective-permute-start.7 = (f32[16,256]{1,0:T(8,128)S(1)}, f32[16,256]{1,0:T(8,128)S(1)}, u32[]{:S(2)}, u32[]{:S(2)}) collective-permute-start(f32[16,256]{1,0:T(8,128)S(1)} %get-tuple-element.48.refs_4_.refs_2_), channel_id=1, source_target_pairs={{0,1},{1,0},{2,3},{3,2},{4,5},{5,4},{6,7},{7,6},{8,9},{9,8},{10,11... | collective-permute-start | bytes 49160 | tf_op jit(solution)/shard_map/ppermute | solution.py:599
  100.9 6.8 %collective-permute-start.6 = (f32[16,256]{1,0:T(8,128)S(1)}, f32[16,256]{1,0:T(8,128)S(1)}, u32[]{:S(2)}, u32[]{:S(2)}) collective-permute-start(f32[16,256]{1,0:T(8,128)S(1)} %get-tuple-element.52.refs_2_), channel_id=1, source_target_pairs={{0,1},{1,0},{2,3},{3,2},{4,5},{5,4},{6,7},{7,6},{8,9},{9,8},{10,11... | collective-permute-start | bytes 49160 | tf_op jit(solution)/shard_map/ppermute | solution.py:599
  112.6 3.8 %collective-permute-start.9 = (f32[16,256]{1,0:T(8,128)S(1)}, f32[16,256]{1,0:T(8,128)S(1)}, u32[]{:S(2)}, u32[]{:S(2)}) collective-permute-start(f32[16,256]{1,0:T(8,128)S(1)} %get-tuple-element.58.refs_2_), channel_id=1, source_target_pairs={{0,1},{1,0},{2,3},{3,2},{4,5},{5,4},{6,7},{7,6},{8,9},{9,8},{10,11... | collective-permute-start | bytes 49160 | tf_op jit(solution)/shard_map/ppermute | solution.py:599
  116.4 22.6 %copy-start.1 = (f32[1,3,8,32,64]{4,3,2,1,0:T(8,128)S(1)}, f32[1,3,8,32,64]{4,3,2,1,0:T(8,128)}, u32[]{:S(2)}) copy-start(f32[1,3,8,32,64]{4,3,2,1,0:T(8,128)} %param.12) | copy-start | bytes 589828
  116.4 22.6 %copy-start.7 = (f32[1,32,64]{2,1,0:T(8,128)S(1)}, f32[1,32,64]{2,1,0:T(8,128)}, u32[]{:S(2)}) copy-start(f32[1,32,64]{2,1,0:T(8,128)} %param.13) | copy-start | bytes 24580
  116.4 22.6 %copy-start.9 = (f32[2,3,12]{2,1,0:T(4,128)S(1)}, f32[2,3,12]{2,1,0:T(4,128)}, u32[]{:S(2)}) copy-start(f32[2,3,12]{2,1,0:T(4,128)} %constant.5.clone.level_ref) | copy-start | bytes 868

commit v3 on v2

--- a/solution.py
+++ b/solution.py
@@ -12,7 +12,6 @@
 
 WSTEPS = 4
 HALO = WSTEPS
-NEAR = 2
 LANES = 128
 SUB = 8
 UNROLL = 4
@@ -93,8 +92,8 @@
 
 
 def start_kernel(n, level_ref, spectrum_ref, ocean_hbm, sea_hbm, mask_hbm, wind_hbm, cross_hbm,
-                 out_ref, rim_ref, near_lo_hbm, near_hi_hbm, far_lo_hbm, far_hi_hbm,
-                 raw, ocean, sea, mask_ref, wind_ref, cross_ref, near_lo, near_hi, far_lo, far_hi, sem, out_sem):
+                 out_ref, rim_ref, near_lo_hbm, near_hi_hbm, next_lo_hbm, next_hi_hbm, far_lo_hbm, far_hi_hbm,
+                 raw, ocean, sea, mask_ref, wind_ref, cross_ref, near_lo, near_hi, next_lo, next_hi, far_lo, far_hi, sem, out_sem):
     t_n, s_n, rows, cols, own, ny, fd, nx, chunks = n
     s = lax.axis_index("spec")
     pad = -(-ny // LANES) * LANES
@@ -129,23 +128,23 @@
             out_ref[t * s_n + q] = turned[t * rows : (t + 1) * rows + 2 * HALO, : 4 * cols]
     aux = [mask_ref[...].astype(jnp.float32), wind_ref[0], wind_ref[1], cross_ref[...].astype(jnp.float32)]
     for k, value in enumerate(aux):
-        at = NEAR * fd + k * HALO
+        at = fd + k * HALO
         near_hi[at : at + HALO] = value[rows - HALO : rows]
         near_lo[at : at + HALO] = value[0:HALO]
 
-    held = ((near_lo, near_lo_hbm), (near_hi, near_hi_hbm), (far_lo, far_lo_hbm), (far_hi, far_hi_hbm))
+    held = ((near_lo, near_lo_hbm), (near_hi, near_hi_hbm), (next_lo, next_lo_hbm), (next_hi, next_hi_hbm),
+            (far_lo, far_lo_hbm), (far_hi, far_hi_hbm))
     outward = []
 
     def send_out(c):
-        spans = [(c * part, part), (fd + c * part, part)]
         for k, (here, there) in enumerate(held):
-            for j, (at, size) in enumerate(spans):
-                span = pl.ds(at, size)
+            for j in range(here.shape[0] // fd):
+                span = pl.ds(j * fd + c * part, part)
                 outward.append(pltpu.make_async_copy(here.at[span], there.at[span], out_sem.at[c, k, j]))
                 outward[-1].start()
             if c == 0 and k < 2:
-                span = pl.ds(NEAR * fd, 4 * HALO)
-                outward.append(pltpu.make_async_copy(here.at[span], there.at[span], out_sem.at[c, k, 2]))
+                span = pl.ds(fd, 4 * HALO)
+                outward.append(pltpu.make_async_copy(here.at[span], there.at[span], out_sem.at[c, k, HALO]))
                 outward[-1].start()
 
     for c in range(chunks):
@@ -157,8 +156,8 @@
                 for h in range(nx // LANES):
                     planes = jnp.swapaxes(raw[pl.ds(at, SUB), :, half(h)], 0, 1)
                     for j in range(HALO):
-                        lo_ref, hi_ref = (near_lo, near_hi) if j < NEAR else (far_lo, far_hi)
-                        sl = pl.ds(pl.multiple_of(at + (j % NEAR) * fd, SUB), SUB)
+                        lo_ref, hi_ref = ((near_lo, near_hi), (next_lo, next_hi), (far_lo, far_hi))[min(j, 2)]
+                        sl = pl.ds(pl.multiple_of(at + max(j - 2, 0) * fd, SUB), SUB)
                         lo_ref[sl, half(h)] = planes[j]
                         hi_ref[sl, half(h)] = planes[rows - 1 - j]
             return carry
@@ -215,7 +214,7 @@
                         edge_ref[c * 2 + k, at : at + 1] = value
 
         def joined(k, own):
-            span = slice(NEAR * fd + k * HALO, NEAR * fd + (k + 1) * HALO)
+            span = slice(fd + k * HALO, fd + (k + 1) * HALO)
             return jnp.concatenate([hb_ref[span], own, ha_ref[span]], axis=0)
 
         wet, shift = joined(0, wet), joined(3, shift)
@@ -278,8 +277,8 @@
                         g = growth(r, h)
                         add((0, r, h), advected)
                         if sums:
-                            pushed = (g - 1.0) * advected
-                            grown = advected + pushed
+                            grown = g * advected
+                            pushed = grown - advected
                             for b in range(2):
                                 add((1 + b, r, h), bands[b] * pushed)
                                 add((3 + b, r, h), bands[2 + b] * grown)
@@ -389,14 +388,18 @@
             at = c * ext + r + HALO
             windb[c, k] = jnp.broadcast_to(wind_ref[at : at + 1], (SUB, nx))
 
+    def load(place, at, h):
+        found, first = place
+        parts = [operands[k][pl.ds(pl.multiple_of(first + at, SUB), SUB), half(h)] for k in found]
+        return functools.reduce(lambda a, b: a + b, parts)
+
     def planes(at):
         sl = pl.ds(at, SUB)
         bw = wide(table_ref[s, sl, BW : BW + 1]) if raw else None
         we, wn = [wide(table_ref[s, sl, b : b + 1]) for b in (WE, WN)] if grow else (None, None)
 
         def energy(r, h):
-            operand, first = source[r]
-            value = operands[operand][pl.ds(pl.multiple_of(first + at, SUB), SUB), half(h)]
+            value = load(source[r], at, h)
             return bw * value if raw else value
 
         def factor(r, h):
@@ -406,8 +409,7 @@
                 value = 1.0 + jnp.maximum(drive - 0.05, 0.0)
                 growth_ref[pl.ds(pl.multiple_of(k * fd + at, SUB), SUB), half(h)] = value
                 return value
-            operand, first = growth[r]
-            return operands[operand][pl.ds(pl.multiple_of(first + at, SUB), SUB), half(h)]
+            return load(growth[r], at, h)
 
         return energy, factor
 
@@ -589,11 +591,11 @@
     vm = pltpu.VMEM
     params = pltpu.CompilerParams(vmem_limit_bytes=24 << 20)
 
-    def up(x):
-        return lax.ppermute(x, "tile", [(i, i + 1) for i in range(t_n - 1)])
-
-    def down(x):
-        return lax.ppermute(x, "tile", [(i + 1, i) for i in range(t_n - 1)])
+    def up(x, without=None):
+        return lax.ppermute(x, "tile", [(i, i + 1) for i in range(t_n - 1) if i + 1 != without])
+
+    def down(x, without=None):
+        return lax.ppermute(x, "tile", [(i + 1, i) for i in range(t_n - 1) if i + 1 != without])
 
     def others(x):
         return added(lax.ppermute(x, "spec", [(i, (i + k) % s_n) for i in range(s_n)]) for k in range(1, s_n))
@@ -608,25 +610,32 @@
         )(*args)
 
     ext = rows + 2 * HALO
-    near, far = f32(NEAR * fd + 4 * HALO, nx), f32((HALO - NEAR) * fd, nx)
+    near, second, far = f32(fd + 4 * HALO, nx), f32(fd, nx), f32((HALO - 2) * fd, nx)
 
     def hbm(shape):
         return pltpu.HBM(shape.shape, shape.dtype)
 
-    send, level_rim, near_lo, near_hi, far_lo, far_hi = call(
+    send, level_rim, near_lo, near_hi, next_lo, next_hi, far_lo, far_hi = call(
         functools.partial(start_kernel, (t_n, s_n, rows, cols, own, ny, fd, nx, chunks)),
         (levels, natural, in_hbm(ocean.reshape(3 * own, cols, ny)), in_hbm(sea), in_hbm(land_mask), in_hbm(wind), in_hbm(intersection)),
         [SM] + [HB] * 6,
-        (f32(devices, ext, 4 * cols), f32(3, 2, cols, ny), hbm(near), hbm(near), hbm(far), hbm(far)),
-        (VM,) * 2 + (HB,) * 4,
+        (f32(devices, ext, 4 * cols), f32(3, 2, cols, ny), hbm(near), hbm(near), hbm(second), hbm(second), hbm(far), hbm(far)),
+        (VM,) * 2 + (HB,) * 6,
         [vm((fd, rows, nx), jnp.float32), vm((3 * own, cols, ny), jnp.float32), vm((cols, ny), jnp.float32),
          vm((rows, nx), jnp.int32), vm((2, rows, nx), jnp.float32), vm((rows, nx), jnp.int32),
-         vm(near.shape, jnp.float32), vm(near.shape, jnp.float32), vm(far.shape, jnp.float32), vm(far.shape, jnp.float32),
-         pltpu.SemaphoreType.DMA((chunks + 5,)), pltpu.SemaphoreType.DMA((chunks, 4, 3))],
+         vm(near.shape, jnp.float32), vm(near.shape, jnp.float32),
+         vm(second.shape, jnp.float32), vm(second.shape, jnp.float32), vm(far.shape, jnp.float32), vm(far.shape, jnp.float32),
+         pltpu.SemaphoreType.DMA((chunks + 5,)), pltpu.SemaphoreType.DMA((chunks, 6, HALO + 1))],
     )
     hb, ha = up(near_hi), down(near_lo)
     arrived = lax.all_to_all(send, AXES, 0, 0, tiled=True)
-    hbf, haf = up(far_hi), down(far_lo)
+    hbn, han = up(next_hi), down(next_lo)
+    middle = t_n // 2
+    turn_up = lax.ppermute(far_hi, "tile", [(middle - 1, t_n - 1)])
+    turn_down = lax.ppermute(far_lo, "tile", [(middle, 0)])
+    hbf, haf = up(far_hi, middle), down(far_lo, middle)
+    hbt = lax.ppermute(turn_up, "tile", [(t_n - 1, middle)])
+    hat = lax.ppermute(turn_down, "tile", [(0, middle - 1)])
 
     geo = call(
         functools.partial(pick_kernel, (t_n, s_n, rows, cols, nx, fd), False),
@@ -652,14 +661,15 @@
 
     planes = {k: {} for k in range(WSTEPS + 1)}
     for j in range(HALO):
-        for base, sign, (a, b) in ((-1, -1, (hb, hbf)), (rows, 1, (ha, haf))):
-            planes[0][base + sign * j] = (a if j < NEAR else b, (j % NEAR) * fd)
-    for j in range(NEAR):
-        planes[0][j] = (near_lo, j * fd)
-        planes[0][rows - 1 - j] = (near_hi, j * fd)
+        k, at = min(j, 2), max(j - 2, 0) * fd
+        planes[0][-1 - j] = (((hb,), (hbn,), (hbf, hbt))[k], at)
+        planes[0][rows + j] = (((ha,), (han,), (haf, hat))[k], at)
+        if j < 2:
+            planes[0][j] = (((near_lo,), (next_lo,))[j], 0)
+            planes[0][rows - 1 - j] = (((near_hi,), (next_hi,))[j], 0)
     for k, r in enumerate(range(1, rows - 1)):
-        planes[1][r] = (mid, k * fd)
-    grown = {r: (growth0, r * fd) for r in range(rows)}
+        planes[1][r] = ((mid,), k * fd)
+    grown = {r: ((growth0,), r * fd) for r in range(rows)}
     totals, gots = {1: total}, {}
 
     def advanced(step, segments, exchange=True):
@@ -668,12 +678,14 @@
         grow = [r for r in order if r not in grown]
         operands = []
 
-        def place(pair):
-            for k, array in enumerate(operands):
-                if array is pair[0]:
-                    return k, pair[1]
-            operands.append(pair[0])
-            return len(operands) - 1, pair[1]
+        def place(item):
+            found = []
+            for array in item[0]:
+                known = [k for k, other in enumerate(operands) if other is array]
+                if not known:
+                    operands.append(array)
+                found.append(known[0] if known else len(operands) - 1)
+            return tuple(found), item[1]
 
         source = {r: place(planes[step - 1][r]) for r in sorted({r + d for r in order for d in (-1, 0, 1)})}
         growth = {r: place(grown[r]) for r in order if r in grown}
@@ -697,9 +709,9 @@
             args, [VM] * len(args), tuple(shapes), (VM,) * len(shapes), scratch(5 if sums else 1, len(grow)),
         )
         for k, r in enumerate(order):
-            planes[step][r] = (outs[0], k * fd)
+            planes[step][r] = ((outs[0],), k * fd)
         for k, r in enumerate(grow):
-            grown[r] = (outs[2], k * fd)
+            grown[r] = ((outs[2],), k * fd)
         totals[step] = outs[1]
         if exchange and not sums:
             gots[step] = others(outs[1])
@@ -709,9 +721,9 @@
 
     advanced(1, pair(-1, 0))
     advanced(2, [list(range(rows))])
+    advanced(1, pair(-3, -2))
     advanced(3, [list(range(1, rows - 1))], exchange=False)
     level_got = others(level_rim)
-    advanced(1, pair(-3, -2))
     advanced(2, pair(-2, -1))
     advanced(3, pair(-1, 0))
     totals[3], level_got = lax.optimization_barrier((totals[3], level_got))
@@ -720,7 +732,7 @@
     landed = lax.all_to_all(totals[WSTEPS], AXES, 0, 0, tiled=True)
     pad = -(-ny // LANES) * LANES
     size = cols + 8
-    ins = (table, levels, landed, geo, planes[WSTEPS][0][0], ocean, sea, hb, ha, level_got)
+    ins = (table, levels, landed, geo, planes[WSTEPS][0][0][0], ocean, sea, hb, ha, level_got)
     waves, fields = call(
         functools.partial(last_kernel, (rows, fd, nx, t_n, s_n, cols, own, ny, chunks)),
         ins, [VM, SM] + [VM] * (len(ins) - 2), (f32(fd, rows, nx), f32(3, own, cols, ny)), (HB, HB),

time: 145 us -> 154 us (1.062)
  starting transfers between devices: 16.8 us -> 42.9 us
  blocking collectives: 65.4 us -> 48 us
    ppermute x4 -> x10, starting transfers between devices: 10.3 us -> 36.5 us  [the longest x3 18.2 us: up(): lax.ppermute(x, 'tile', [(i, i + 1) for i in range(t_n - 1) if i + 1 != w...]
    all_to_all x1, blocking collectives: 51 us -> 34.5 us  [program(): arrived = lax.all_to_all(send, AXES, 0, 0, tiled=True)]
  transfers between devices with their start and end apart: 10 -> 16, of which waited for: 1 -> 2; matrix products, arithmetic and copies ran while one was open for 0% -> 0% of each run, Pallas kernels for 27% -> 25%
where the time goes in v3:
time: 154 us; the launch traced here: 153 us
  Pallas kernels  58 us (38%)
  blocking collectives  48 us (31%)
  starting transfers between devices  42.9 us (28%)
  waiting for transfers between devices  2.81 us (2%)
    pallas_call x12, Pallas kernels, call(): pl.pallas_call(kernel, out_shape=shapes, in_specs=specs, out_specs=out_sp...  58 us
    all_to_all x1, blocking collectives, program(): arrived = lax.all_to_all(send, AXES, 0, 0, tiled=True)  34.5 us
    ppermute x3, starting transfers between devices, up(): lax.ppermute(x, 'tile', [(i, i + 1) for i in range(t_n - 1) if i + 1 != w...  18.2 us
    all_to_all x1, blocking collectives, program(): landed = lax.all_to_all(totals[WSTEPS], AXES, 0, 0, tiled=True)  13.5 us
    ppermute x1, starting transfers between devices, program(): hat = lax.ppermute(turn_down, 'tile', [(0, middle - 1)])  11.5 us
    ppermute x6, starting transfers between devices, others(): lax.ppermute(x, 'spec', [(i, (i + k) % s_n) for i in range(s_n)])  6.47 us
    ppermute x3, starting transfers between devices, down(): lax.ppermute(x, 'tile', [(i + 1, i) for i in range(t_n - 1) if i + 1 != w...  3.88 us
  transfers between devices with their start and end apart: 16, of which 2 were waited for; matrix products, arithmetic and copies ran while one was open for 0% of the time, Pallas kernels for 25%

profile of v3, /device:TPU:0, one launch (start us, length us, event | category | flops | bytes accessed | tf_op | source)
XLA Modules:
  0.0 153.4 jit_solution(6699001956540942832)
XLA Ops:
  0.6 0.0 copy-start.10
  0.6 0.7 copy-done.10
  1.3 6.2 %shard_map.95 = (f32[32,16,128]{2,1,0:T(8,128)S(1)}, f32[3,2,32,64]{3,2,1,0:T(8,128)S(1)}, f32[592,256]{1,0:T(8,128)}, f32[592,256]{1,0:T(8,128)}, f32[576,256]{...) custom-call(f32[2,3,12]{2,1,0:T(4,128)S(1)} %copy-done.10, f32[576,8,256]{2,1,0:T(8,128)} %bitcast.10, ...), custom_call_target="tpu_custom_call" | custom-call | tf_op jit(solution)/shard_map/pallas_call | solution.py:607
  7.5 0.0 copy-start
  7.5 0.9 collective-permute-start.5
  8.4 1.3 collective-permute-start.8
  9.7 1.9 %collective-permute-start = (f32[592,256]{1,0:T(8,128)}, f32[592,256]{1,0:T(8,128)S(1)}, u32[]{:S(2)}, u32[]{:S(2)}) collective-permute-start(f32[592,256]{1,0:T(8,128)} %get-tuple-element.37.refs_9_), channel_id=1, source_target_pairs={{0,2},{2,4},{4,6},{6,8},{8,10},{10,12},{12,14},{1,3},{3,5},{5,7},{... | collective-permute-start | bytes 1818632 | tf_op jit(solution)/shard_map/ppermute | solution.py:595
  11.6 4.5 %collective-permute-start.2 = (f32[576,256]{1,0:T(8,128)}, f32[576,256]{1,0:T(8,128)S(1)}, u32[]{:S(2)}, u32[]{:S(2)}) collective-permute-start(f32[576,256]{1,0:T(8,128)} %get-tuple-element.43.refs_8_), channel_id=1, source_target_pairs={{0,2},{2,4},{4,6},{6,8},{8,10},{10,12},{12,14},{1,3},{3,5},{5,7},{... | collective-permute-start | bytes 1769480 | tf_op jit(solution)/shard_map/ppermute | solution.py:595
  16.1 1.3 collective-permute-start.1
  17.4 0.5 collective-permute-done.2.refs_4_.refs_6_
  17.9 11.8 %collective-permute-start.4 = (f32[1152,256]{1,0:T(8,128)}, f32[1152,256]{1,0:T(8,128)S(1)}, u32[]{:S(2)}, u32[]{:S(2)}) collective-permute-start(f32[1152,256]{1,0:T(8,128)} %get-tuple-element.47), channel_id=1, source_target_pairs={{0,2},{2,4},{4,6},{8,10},{10,12},{12,14},{1,3},{3,5},{5,7},{9,11},... | collective-permute-start | bytes 3538952 | tf_op jit(solution)/shard_map/ppermute | solution.py:595
  29.7 0.0 collective-permute-done.refs_1_.refs_5_.refs_7_.hb_ref
  29.7 1.3 collective-permute-start.7
  31.0 0.0 collective-permute-done.5
  31.1 0.7 collective-permute-start.6
  31.8 0.0 collective-permute-done.8
  31.8 11.5 %collective-permute-start.9 = (f32[1152,256]{1,0:T(8,128)S(1)}, f32[1152,256]{1,0:T(8,128)S(1)}, u32[]{:S(2)}, u32[]{:S(2)}) collective-permute-start(f32[1152,256]{1,0:T(8,128)S(1)} %collective-permute-done.8), channel_id=1, source_target_pairs={{0,6},{1,7},{16,22},{17,23}} | collective-permute-start | bytes 3538952 | tf_op jit(solution)/shard_map/ppermute | solution.py:638
  43.3 0.0 collective-permute-done.1.refs_2_.refs_10_.refs_8_.ha_ref
  43.3 1.3 collective-permute-start.3
  44.6 34.5 %all_to_all.10.got_ref = f32[32,16,128]{2,1,0:T(8,128)S(1)} all-to-all(f32[32,16,128]{2,1,0:T(8,128)S(1)} %get-tuple-element.36), channel_id=1, replica_groups=mesh['grp'=2,'tile'=8,'spec'=2] {'grp','tile','spec'}, dimensions={0} | all-to-all | bytes 524288 | tf_op jit(solution)/shard_map/all_to_all | solution.py:631
  79.1 0.6 shard_map.96
  79.7 0.0 collective-permute-done.3.refs_11_.refs_9_
  79.7 0.6 collective-permute-start.14
  80.4 0.6 shard_map.97.geo_ref
  81.0 0.0 copy-done
  81.0 7.1 %shard_map.98 = (f32[3456,256]{1,0:T(8,128)S(1)}, f32[16,256]{1,0:T(8,128)S(1)}, f32[4608,256]{1,0:T(8,128)S(1)}) custom-call(f32[2,576,16]{2,1,0:T(8,128)S(1)} %copy-done, f32[64,256]{1,0:T(8,128)S(1)} %shard_map.97.geo_ref, f32[2,8,256]{2,1,0:T(8,128)S(1)} %copy-done.6, f32[576,8,256]{2,1,0:T(8,128)} %bitcast.11), custom_call_target="tpu_custom_call" | custom-call | tf_op jit(solution)/shard_map/pallas_call | solution.py:607
  88.2 4.8 %shard_map.99 = (f32[2304,256]{1,0:T(8,128)S(1)}, f32[16,256]{1,0:T(8,128)S(1)}, f32[1152,256]{1,0:T(8,128)S(1)}) custom-call(f32[2,576,16]{2,1,0:T(8,128)S(1)} %copy-done, f32[64,256]{1,0:T(8,128)S(1)} %get-tuple-element.40.refs_1_.geo_ref, f32[32,256]{1,0:T(8,128)S(1)} %get-tuple-element.41.refs_2_, f32[16,256]{1,0:T(8,128)S(1)} %get-tuple-element.42.refs_3_, ...), custom_call_target="tpu_custom_call" | custom-call | tf_op jit(solution)/shard_map/pallas_call | solution.py:607
  93.0 0.0 collective-permute-done.4.refs_4_
  93.0 1.5 collective-permute-start.11
  94.5 0.0 collective-permute-done.7.refs_10_
  94.5 0.0 collective-permute-done.6.refs_5_
  94.5 0.0 collective-permute-done.9.refs_11_
  94.5 4.8 %shard_map.100 = (f32[2304,256]{1,0:T(8,128)S(1)}, f32[16,256]{1,0:T(8,128)S(1)}, f32[2304,256]{1,0:T(8,128)S(1)}) custom-call(f32[2,576,16]{2,1,0:T(8,128)S(1)} %copy-done, f32[64,256]{1,0:T(8,128)S(1)} %get-tuple-element.40.refs_1_.geo_ref, f32[32,256]{1,0:T(8,128)S(1)} %get-tuple-element.41.refs_2_, f32[16,256]{1,0:T(8,128)S(1)} %get-tuple-element.46.refs_3_.refs_2_, ...), custom_call_target="tpu_custom_call" | custom-call | tf_op jit(solution)/shard_map/pallas_call | solution.py:607
  99.3 0.6 collective-permute-start.10
  99.9 6.0 %shard_map.101 = (f32[4608,256]{1,0:T(8,128)S(1)}, f32[16,256]{1,0:T(8,128)S(1)}) custom-call(f32[2,576,16]{2,1,0:T(8,128)S(1)} %copy-done, f32[64,256]{1,0:T(8,128)S(1)} %get-tuple-element.40.refs_1_.geo_ref, f32[16,256]{1,0:T(8,128)S(1)} %get-tuple-element.46.refs_3_.refs_2_, f32[16,256]{1,0:T(8,128)S(1)} %collective-permute-done.11.refs_3_, ...), custom_call_target="tpu_custom_call" | custom-call | tf_op jit(solution)/shard_map/pallas_call | solution.py:607
  105.9 1.5 collective-permute-start.13
  107.4 0.0 collective-permute-done.10.refs_3_
  107.4 4.7 %shard_map.102 = (f32[2304,256]{1,0:T(8,128)S(1)}, f32[16,256]{1,0:T(8,128)S(1)}) custom-call(f32[2,576,16]{2,1,0:T(8,128)S(1)} %copy-done, f32[64,256]{1,0:T(8,128)S(1)} %get-tuple-element.40.refs_1_.geo_ref, f32[16,256]{1,0:T(8,128)S(1)} %get-tuple-element.49.refs_2_, f32[16,256]{1,0:T(8,128)S(1)} %collective-permute-done.10.refs_3_, ...), custom_call_target="tpu_custom_call" | custom-call | tf_op jit(solution)/shard_map/pallas_call | solution.py:607
  112.1 0.6 collective-permute-start.12
  112.8 5.2 %shard_map.103 = (f32[3456,256]{1,0:T(8,128)S(1)}, f32[16,256]{1,0:T(8,128)S(1)}) custom-call(f32[2,576,16]{2,1,0:T(8,128)S(1)} %copy-done, f32[64,256]{1,0:T(8,128)S(1)} %get-tuple-element.40.refs_1_.geo_ref, f32[16,256]{1,0:T(8,128)S(1)} %get-tuple-element.52.refs_4_.refs_2_, f32[16,256]{1,0:T(8,128)S(1)} %collective-permute-done.13.refs_3_, ...), custom_call_target="tpu_custom_call" | custom-call | tf_op jit(solution)/shard_map/pallas_call | solution.py:607
  117.9 0.0 collective-permute-done.12.refs_3_
  118.0 4.8 %shard_map.104 = (f32[2304,256]{1,0:T(8,128)S(1)}, f32[16,256]{1,0:T(8,128)S(1)}) custom-call(f32[2,576,16]{2,1,0:T(8,128)S(1)} %copy-done, f32[64,256]{1,0:T(8,128)S(1)} %get-tuple-element.40.refs_1_.geo_ref, f32[16,256]{1,0:T(8,128)S(1)} %get-tuple-element.56.refs_2_, f32[16,256]{1,0:T(8,128)S(1)} %collective-permute-done.12.refs_3_, ...), custom_call_target="tpu_custom_call" | custom-call | tf_op jit(solution)/shard_map/pallas_call | solution.py:607
  122.8 1.5 collective-permute-start.15
  124.3 0.0 collective-permute-done.14.lev_ref
  124.3 2.3 %collective-permute-done.15.refs_3_ = f32[16,256]{1,0:T(8,128)S(1)} collective-permute-done((f32[16,256]{1,0:T(8,128)S(1)}, f32[16,256]{1,0:T(8,128)S(1)}, u32[]{:S(2)}, u32[]{:S(2)}) %collective-permute-start.15) | collective-permute-done | bytes 16416 | tf_op jit(solution)/shard_map/ppermute | solution.py:601
  126.6 8.0 %shard_map.105 = (f32[4608,256]{1,0:T(8,128)S(1)}, f32[32,8,256]{2,1,0:T(8,128)S(1)}) custom-call(f32[2,576,16]{2,1,0:T(8,128)S(1)} %copy-done, f32[64,256]{1,0:T(8,128)S(1)} %get-tuple-element.40.refs_1_.geo_ref, f32[16,256]{1,0:T(8,128)S(1)} %get-tuple-element.62.refs_2_, f32[16,256]{1,0:T(8,128)S(1)} %collective-permute-done.15.refs_3_, ...), custom_call_target="tpu_custom_call" | custom-call | tf_op jit(solution)/shard_map/pallas_call | solution.py:607
  134.6 13.5 %all_to_all.11.got_ref = f32[32,8,256]{2,1,0:T(8,128)S(1)} all-to-all(f32[32,8,256]{2,1,0:T(8,128)S(1)} %get-tuple-element.65), channel_id=1, replica_groups=mesh['grp'=2,'tile'=8,'spec'=2] {'grp','tile','spec'}, dimensions={0} | all-to-all | bytes 524288 | tf_op jit(solution)/shard_map/all_to_all | solution.py:732
  148.1 5.3 %shard_map.106 = (f32[576,8,256]{2,1,0:T(8,128)}, f32[3,8,32,64]{3,2,1,0:T(8,128)}) custom-call(f32[2,576,16]{2,1,0:T(8,128)S(1)} %copy-done, f32[2,3,12]{2,1,0:T(4,128)S(1)} %copy-done.11, f32[32,8,256]{2,1,0:T(8,128)S(1)} %all_to_all.11.got_ref, f32[64,256]{1,0:T(8,128)S(1)} %get-tuple-element.40.refs_1_.geo_ref, ...), custom_call_target="tpu_custom_call" | custom-call | tf_op jit(solution)/shard_map/pallas_call | solution.py:607
  (22 shorter events, 0.0 us)
Async XLA Ops:
  0.6 0.7 copy-start.10
  1.3 77.8 %copy-start.6 = (f32[2,8,256]{2,1,0:T(8,128)S(1)}, f32[2,8,256]{2,1,0:T(8,128)}, u32[]{:S(2)}) copy-start(f32[2,8,256]{2,1,0:T(8,128)} %wind_ref.1) | copy-start | bytes 49156
  1.3 77.8 %copy-start.7 = (s32[8,256]{1,0:T(8,128)S(1)}, s32[8,256]{1,0:T(8,128)}, u32[]{:S(2)}) copy-start(s32[8,256]{1,0:T(8,128)} %refs_4_.1) | copy-start | bytes 24580
  1.3 77.8 %copy-start.8 = (s32[8,256]{1,0:T(8,128)S(1)}, s32[8,256]{1,0:T(8,128)}, u32[]{:S(2)}) copy-start(s32[8,256]{1,0:T(8,128)} %mask_ref.3) | copy-start | bytes 24580
  7.5 73.5 %copy-start = (f32[2,576,16]{2,1,0:T(8,128)S(1)}, f32[2,576,16]{2,1,0:T(8,128)}, u32[]{:S(2)}) copy-start(f32[2,576,16]{2,1,0:T(8,128)} %constant.4.clone.table_ref.refs_0_) | copy-start | bytes 221188
  7.5 23.5 %collective-permute-start.5 = (f32[1152,256]{1,0:T(8,128)}, f32[1152,256]{1,0:T(8,128)S(1)}, u32[]{:S(2)}, u32[]{:S(2)}) collective-permute-start(f32[1152,256]{1,0:T(8,128)} %get-tuple-element.47), channel_id=1, source_target_pairs={{6,14},{7,15},{22,30},{23,31}} | collective-permute-start | bytes 3538952 | tf_op jit(solution)/shard_map/ppermute | solution.py:634
  8.4 23.4 %collective-permute-start.8 = (f32[1152,256]{1,0:T(8,128)}, f32[1152,256]{1,0:T(8,128)S(1)}, u32[]{:S(2)}, u32[]{:S(2)}) collective-permute-start(f32[1152,256]{1,0:T(8,128)} %get-tuple-element.48), channel_id=1, source_target_pairs={{8,0},{9,1},{24,16},{25,17}} | collective-permute-start | bytes 3538952 | tf_op jit(solution)/shard_map/ppermute | solution.py:635
  9.7 20.0 %collective-permute-start = (f32[592,256]{1,0:T(8,128)}, f32[592,256]{1,0:T(8,128)S(1)}, u32[]{:S(2)}, u32[]{:S(2)}) collective-permute-start(f32[592,256]{1,0:T(8,128)} %get-tuple-element.37.refs_9_), channel_id=1, source_target_pairs={{0,2},{2,4},{4,6},{6,8},{8,10},{10,12},{12,14},{1,3},{3,5},{5,7},{... | collective-permute-start | bytes 1818632 | tf_op jit(solution)/shard_map/ppermute | solution.py:595
  11.6 6.3 %collective-permute-start.2 = (f32[576,256]{1,0:T(8,128)}, f32[576,256]{1,0:T(8,128)S(1)}, u32[]{:S(2)}, u32[]{:S(2)}) collective-permute-start(f32[576,256]{1,0:T(8,128)} %get-tuple-element.43.refs_8_), channel_id=1, source_target_pairs={{0,2},{2,4},{4,6},{6,8},{8,10},{10,12},{12,14},{1,3},{3,5},{5,7},{... | collective-permute-start | bytes 1769480 | tf_op jit(solution)/shard_map/ppermute | solution.py:595
  16.1 27.2 %collective-permute-start.1 = (f32[592,256]{1,0:T(8,128)}, f32[592,256]{1,0:T(8,128)S(1)}, u32[]{:S(2)}, u32[]{:S(2)}) collective-permute-start(f32[592,256]{1,0:T(8,128)} %get-tuple-element.38.refs_6_), channel_id=1, source_target_pairs={{2,0},{4,2},{6,4},{8,6},{10,8},{12,10},{14,12},{3,1},{5,3},{7,5},{... | collective-permute-start | bytes 1818632 | tf_op jit(solution)/shard_map/ppermute | solution.py:598
  17.9 75.1 %collective-permute-start.4 = (f32[1152,256]{1,0:T(8,128)}, f32[1152,256]{1,0:T(8,128)S(1)}, u32[]{:S(2)}, u32[]{:S(2)}) collective-permute-start(f32[1152,256]{1,0:T(8,128)} %get-tuple-element.47), channel_id=1, source_target_pairs={{0,2},{2,4},{4,6},{8,10},{10,12},{12,14},{1,3},{3,5},{5,7},{9,11},... | collective-permute-start | bytes 3538952 | tf_op jit(solution)/shard_map/ppermute | solution.py:595
  29.7 64.7 %collective-permute-start.7 = (f32[1152,256]{1,0:T(8,128)}, f32[1152,256]{1,0:T(8,128)S(1)}, u32[]{:S(2)}, u32[]{:S(2)}) collective-permute-start(f32[1152,256]{1,0:T(8,128)} %get-tuple-element.48), channel_id=1, source_target_pairs={{2,0},{4,2},{6,4},{10,8},{12,10},{14,12},{3,1},{5,3},{7,5},{11,9},... | collective-permute-start | bytes 3538952 | tf_op jit(solution)/shard_map/ppermute | solution.py:598
  31.1 63.4 %collective-permute-start.6 = (f32[1152,256]{1,0:T(8,128)S(1)}, f32[1152,256]{1,0:T(8,128)S(1)}, u32[]{:S(2)}, u32[]{:S(2)}) collective-permute-start(f32[1152,256]{1,0:T(8,128)S(1)} %collective-permute-done.5), channel_id=1, source_target_pairs={{14,8},{15,9},{30,24},{31,25}} | collective-permute-start | bytes 3538952 | tf_op jit(solution)/shard_map/ppermute | solution.py:637
  31.8 62.7 %collective-permute-start.9 = (f32[1152,256]{1,0:T(8,128)S(1)}, f32[1152,256]{1,0:T(8,128)S(1)}, u32[]{:S(2)}, u32[]{:S(2)}) collective-permute-start(f32[1152,256]{1,0:T(8,128)S(1)} %collective-permute-done.8), channel_id=1, source_target_pairs={{0,6},{1,7},{16,22},{17,23}} | collective-permute-start | bytes 3538952 | tf_op jit(solution)/shard_map/ppermute | solution.py:638
  43.3 36.4 %collective-permute-start.3 = (f32[576,256]{1,0:T(8,128)}, f32[576,256]{1,0:T(8,128)S(1)}, u32[]{:S(2)}, u32[]{:S(2)}) collective-permute-start(f32[576,256]{1,0:T(8,128)} %get-tuple-element.44.refs_7_), channel_id=1, source_target_pairs={{2,0},{4,2},{6,4},{8,6},{10,8},{12,10},{14,12},{3,1},{5,3},{7,5},{... | collective-permute-start | bytes 1769480 | tf_op jit(solution)/shard_map/ppermute | solution.py:598
  79.7 44.6 %collective-permute-start.14 = (f32[6,40,64]{2,1,0:T(8,128)S(1)}, f32[6,40,64]{2,1,0:T(8,128)S(1)}, u32[]{:S(2)}, u32[]{:S(2)}) collective-permute-start(f32[6,40,64]{2,1,0:T(8,128)S(1)} %get-tuple-element.61), channel_id=1, source_target_pairs={{0,1},{1,0},{2,3},{3,2},{4,5},{5,4},{6,7},{7,6},{8,9},{9,8},{10,11... | collective-permute-start | bytes 184328 | tf_op jit(solution)/shard_map/ppermute | solution.py:601
  81.0 7.2 %copy-start.2 = (f32[592,256]{1,0:T(8,128)S(1)}, f32[592,256]{1,0:T(8,128)}, u32[]{:S(2)}) copy-start(f32[592,256]{1,0:T(8,128)} %get-tuple-element.38.refs_6_) | copy-start | bytes 1818628
  81.0 7.2 %copy-start.3 = (f32[592,256]{1,0:T(8,128)S(1)}, f32[592,256]{1,0:T(8,128)}, u32[]{:S(2)}) copy-start(f32[592,256]{1,0:T(8,128)} %get-tuple-element.37.refs_9_) | copy-start | bytes 1818628
  81.0 7.2 %copy-start.4 = (f32[576,256]{1,0:T(8,128)S(1)}, f32[576,256]{1,0:T(8,128)}, u32[]{:S(2)}) copy-start(f32[576,256]{1,0:T(8,128)} %get-tuple-element.44.refs_7_) | copy-start | bytes 1769476
  81.0 7.2 %copy-start.5 = (f32[576,256]{1,0:T(8,128)S(1)}, f32[576,256]{1,0:T(8,128)}, u32[]{:S(2)}) copy-start(f32[576,256]{1,0:T(8,128)} %get-tuple-element.43.refs_8_) | copy-start | bytes 1769476
  93.0 7.0 %collective-permute-start.11 = (f32[16,256]{1,0:T(8,128)S(1)}, f32[16,256]{1,0:T(8,128)S(1)}, u32[]{:S(2)}, u32[]{:S(2)}) collective-permute-start(f32[16,256]{1,0:T(8,128)S(1)} %get-tuple-element.46.refs_3_.refs_2_), channel_id=1, source_target_pairs={{0,1},{1,0},{2,3},{3,2},{4,5},{5,4},{6,7},{7,6},{8,9},{9,8},{10,11... | collective-permute-start | bytes 49160 | tf_op jit(solution)/shard_map/ppermute | solution.py:601
  99.3 8.1 %collective-permute-start.10 = (f32[16,256]{1,0:T(8,128)S(1)}, f32[16,256]{1,0:T(8,128)S(1)}, u32[]{:S(2)}, u32[]{:S(2)}) collective-permute-start(f32[16,256]{1,0:T(8,128)S(1)} %get-tuple-element.49.refs_2_), channel_id=1, source_target_pairs={{0,1},{1,0},{2,3},{3,2},{4,5},{5,4},{6,7},{7,6},{8,9},{9,8},{10,11... | collective-permute-start | bytes 49160 | tf_op jit(solution)/shard_map/ppermute | solution.py:601
  105.9 6.9 %collective-permute-start.13 = (f32[16,256]{1,0:T(8,128)S(1)}, f32[16,256]{1,0:T(8,128)S(1)}, u32[]{:S(2)}, u32[]{:S(2)}) collective-permute-start(f32[16,256]{1,0:T(8,128)S(1)} %get-tuple-element.52.refs_4_.refs_2_), channel_id=1, source_target_pairs={{0,1},{1,0},{2,3},{3,2},{4,5},{5,4},{6,7},{7,6},{8,9},{9,8},{10,11... | collective-permute-start | bytes 49160 | tf_op jit(solution)/shard_map/ppermute | solution.py:601
  112.1 5.8 %collective-permute-start.12 = (f32[16,256]{1,0:T(8,128)S(1)}, f32[16,256]{1,0:T(8,128)S(1)}, u32[]{:S(2)}, u32[]{:S(2)}) collective-permute-start(f32[16,256]{1,0:T(8,128)S(1)} %get-tuple-element.56.refs_2_), channel_id=1, source_target_pairs={{0,1},{1,0},{2,3},{3,2},{4,5},{5,4},{6,7},{7,6},{8,9},{9,8},{10,11... | collective-permute-start | bytes 49160 | tf_op jit(solution)/shard_map/ppermute | solution.py:601
  122.8 3.8 %collective-permute-start.15 = (f32[16,256]{1,0:T(8,128)S(1)}, f32[16,256]{1,0:T(8,128)S(1)}, u32[]{:S(2)}, u32[]{:S(2)}) collective-permute-start(f32[16,256]{1,0:T(8,128)S(1)} %get-tuple-element.62.refs_2_), channel_id=1, source_target_pairs={{0,1},{1,0},{2,3},{3,2},{4,5},{5,4},{6,7},{7,6},{8,9},{9,8},{10,11... | collective-permute-start | bytes 49160 | tf_op jit(solution)/shard_map/ppermute | solution.py:601
  126.6 21.5 %copy-start.1 = (f32[1,3,8,32,64]{4,3,2,1,0:T(8,128)S(1)}, f32[1,3,8,32,64]{4,3,2,1,0:T(8,128)}, u32[]{:S(2)}) copy-start(f32[1,3,8,32,64]{4,3,2,1,0:T(8,128)} %param.12) | copy-start | bytes 589828
  126.6 21.5 %copy-start.9 = (f32[1,32,64]{2,1,0:T(8,128)S(1)}, f32[1,32,64]{2,1,0:T(8,128)}, u32[]{:S(2)}) copy-start(f32[1,32,64]{2,1,0:T(8,128)} %param.13) | copy-start | bytes 24580
  126.6 21.5 %copy-start.11 = (f32[2,3,12]{2,1,0:T(4,128)S(1)}, f32[2,3,12]{2,1,0:T(4,128)}, u32[]{:S(2)}) copy-start(f32[2,3,12]{2,1,0:T(4,128)} %constant.5.clone.level_ref) | copy-start | bytes 868

commit v4 on v3

--- a/solution.py
+++ b/solution.py
@@ -92,7 +92,7 @@
 
 
 def start_kernel(n, level_ref, spectrum_ref, ocean_hbm, sea_hbm, mask_hbm, wind_hbm, cross_hbm,
-                 out_ref, rim_ref, near_lo_hbm, near_hi_hbm, next_lo_hbm, next_hi_hbm, far_lo_hbm, far_hi_hbm,
+                 out_ref, rim_ref, near_a, near_b, next_a, next_b, far_a, far_b, turn_hbm,
                  raw, ocean, sea, mask_ref, wind_ref, cross_ref, near_lo, near_hi, next_lo, next_hi, far_lo, far_hi, sem, out_sem):
     t_n, s_n, rows, cols, own, ny, fd, nx, chunks = n
     s = lax.axis_index("spec")
@@ -132,20 +132,29 @@
         near_hi[at : at + HALO] = value[rows - HALO : rows]
         near_lo[at : at + HALO] = value[0:HALO]
 
-    held = ((near_lo, near_lo_hbm), (near_hi, near_hi_hbm), (next_lo, next_lo_hbm), (next_hi, next_hi_hbm),
-            (far_lo, far_lo_hbm), (far_hi, far_hi_hbm))
+    held = ((near_lo, near_hi, near_a, near_b), (next_lo, next_hi, next_a, next_b), (far_lo, far_hi, far_a, far_b))
+    tile = lax.axis_index("tile")
+    even = tile % 2 == 0
     outward = []
 
     def send_out(c):
-        for k, (here, there) in enumerate(held):
-            for j in range(here.shape[0] // fd):
-                span = pl.ds(j * fd + c * part, part)
-                outward.append(pltpu.make_async_copy(here.at[span], there.at[span], out_sem.at[c, k, j]))
-                outward[-1].start()
-            if c == 0 and k < 2:
-                span = pl.ds(fd, 4 * HALO)
-                outward.append(pltpu.make_async_copy(here.at[span], there.at[span], out_sem.at[c, k, HALO]))
-                outward[-1].start()
+        moves = []
+        for k, (low, high, a, b) in enumerate(held):
+            spans = [pl.ds(j * fd + c * part, part) for j in range(low.shape[0] // fd)]
+            if c == 0 and k == 0:
+                spans.append(pl.ds(fd, 4 * HALO))
+            for j, span in enumerate(spans):
+                moves.append((low, high, a, span, out_sem.at[c, 2 * k, j]))
+                moves.append((high, low, b, span, out_sem.at[c, 2 * k + 1, j]))
+        for side in range(2):
+
+            @pl.when(even if side else jnp.logical_not(even))
+            def _():
+                for move in moves:
+                    source, target, span, mark = move[side], *move[2:]
+                    pltpu.make_async_copy(source.at[span], target.at[span], mark).start()
+
+        outward.extend(pltpu.make_async_copy(x.at[span], target.at[span], mark) for x, _, target, span, mark in moves)
 
     for c in range(chunks):
         copies[c].wait()
@@ -176,6 +185,14 @@
                 ref[2 * stack + k : 2 * stack + k + 1, 0:ny] = sea[at : at + 1, :]
 
     send_out(0)
+    for at, source in ((t_n // 2 - 1, far_hi), (t_n // 2, far_lo)):
+
+        @pl.when(tile == at)
+        def _():
+            copy = pltpu.make_async_copy(source, turn_hbm, sem.at[chunks + 5])
+            copy.start()
+            copy.wait()
+
     for copy in outward:
         copy.wait()
 
@@ -200,7 +217,11 @@
     whole = [jnp.concatenate(f, axis=1) for f in fields]
     wet, shift = mask_ref[...].astype(jnp.float32), cross_ref[...].astype(jnp.float32)
     if full:
-        wind_ref, hb_ref, ha_ref, rim_ref, geo_ref, out_ref, edge_ref = refs
+        wind_ref, a_ref, b_ref, rim_ref, geo_ref, out_ref, edge_ref, hb_ref, ha_ref = refs
+        even = lax.axis_index("tile") % 2 == 0
+        count = hb_ref.shape[0]
+        hb_ref[...] = jnp.where(even, b_ref[0:count], a_ref[0:count])
+        ha_ref[...] = jnp.where(even, a_ref[0:count], b_ref[0:count])
         own, ny = n[6], rim_ref.shape[3]
         low = lax.axis_index("spec") == 0
         for c in range(3):
@@ -215,7 +236,8 @@
 
         def joined(k, own):
             span = slice(fd + k * HALO, fd + (k + 1) * HALO)
-            return jnp.concatenate([hb_ref[span], own, ha_ref[span]], axis=0)
+            first, second = a_ref[span], b_ref[span]
+            return jnp.concatenate([jnp.where(even, second, first), own, jnp.where(even, first, second)], axis=0)
 
         wet, shift = joined(0, wet), joined(3, shift)
         for c in range(2):
@@ -388,10 +410,16 @@
             at = c * ext + r + HALO
             windb[c, k] = jnp.broadcast_to(wind_ref[at : at + 1], (SUB, nx))
 
+    tile = lax.axis_index("tile")
+    even = tile % 2 == 0
+
     def load(place, at, h):
-        found, first = place
+        found, first = place[:2]
         parts = [operands[k][pl.ds(pl.multiple_of(first + at, SUB), SUB), half(h)] for k in found]
-        return functools.reduce(lambda a, b: a + b, parts)
+        value = parts[0] if len(parts) == 1 else jnp.where(even, parts[0], parts[1])
+        if len(parts) == 3:
+            value = jnp.where(tile == (t_n // 2 if place[2] < 0 else t_n // 2 - 1), parts[2], value)
+        return value
 
     def planes(at):
         sl = pl.ds(at, SUB)
@@ -399,7 +427,7 @@
         we, wn = [wide(table_ref[s, sl, b : b + 1]) for b in (WE, WN)] if grow else (None, None)
 
         def energy(r, h):
-            value = load(source[r], at, h)
+            value = load(source[r] + (r,), at, h)
             return bw * value if raw else value
 
         def factor(r, h):
@@ -591,11 +619,9 @@
     vm = pltpu.VMEM
     params = pltpu.CompilerParams(vmem_limit_bytes=24 << 20)
 
-    def up(x, without=None):
-        return lax.ppermute(x, "tile", [(i, i + 1) for i in range(t_n - 1) if i + 1 != without])
-
-    def down(x, without=None):
-        return lax.ppermute(x, "tile", [(i + 1, i) for i in range(t_n - 1) if i + 1 != without])
+    def swapped(x, start, without=None):
+        lower = [i for i in range(start, t_n - 1, 2) if i + 1 != without]
+        return lax.ppermute(x, "tile", [(i, i + 1) for i in lower] + [(i + 1, i) for i in lower])
 
     def others(x):
         return added(lax.ppermute(x, "spec", [(i, (i + k) % s_n) for i in range(s_n)]) for k in range(1, s_n))
@@ -615,27 +641,25 @@
     def hbm(shape):
         return pltpu.HBM(shape.shape, shape.dtype)
 
-    send, level_rim, near_lo, near_hi, next_lo, next_hi, far_lo, far_hi = call(
+    send, level_rim, near_a, near_b, next_a, next_b, far_a, far_b, turn = call(
         functools.partial(start_kernel, (t_n, s_n, rows, cols, own, ny, fd, nx, chunks)),
         (levels, natural, in_hbm(ocean.reshape(3 * own, cols, ny)), in_hbm(sea), in_hbm(land_mask), in_hbm(wind), in_hbm(intersection)),
         [SM] + [HB] * 6,
-        (f32(devices, ext, 4 * cols), f32(3, 2, cols, ny), hbm(near), hbm(near), hbm(second), hbm(second), hbm(far), hbm(far)),
-        (VM,) * 2 + (HB,) * 6,
+        (f32(devices, ext, 4 * cols), f32(3, 2, cols, ny), hbm(near), hbm(near), hbm(second), hbm(second), hbm(far), hbm(far), hbm(far)),
+        (VM,) * 2 + (HB,) * 7,
         [vm((fd, rows, nx), jnp.float32), vm((3 * own, cols, ny), jnp.float32), vm((cols, ny), jnp.float32),
          vm((rows, nx), jnp.int32), vm((2, rows, nx), jnp.float32), vm((rows, nx), jnp.int32),
          vm(near.shape, jnp.float32), vm(near.shape, jnp.float32),
          vm(second.shape, jnp.float32), vm(second.shape, jnp.float32), vm(far.shape, jnp.float32), vm(far.shape, jnp.float32),
-         pltpu.SemaphoreType.DMA((chunks + 5,)), pltpu.SemaphoreType.DMA((chunks, 6, HALO + 1))],
+         pltpu.SemaphoreType.DMA((chunks + 6,)), pltpu.SemaphoreType.DMA((chunks, 6, HALO + 1))],
     )
-    hb, ha = up(near_hi), down(near_lo)
+    got_a, got_b = swapped(near_a, 0), swapped(near_b, 1)
     arrived = lax.all_to_all(send, AXES, 0, 0, tiled=True)
-    hbn, han = up(next_hi), down(next_lo)
+    next_got = swapped(next_a, 0), swapped(next_b, 1)
     middle = t_n // 2
-    turn_up = lax.ppermute(far_hi, "tile", [(middle - 1, t_n - 1)])
-    turn_down = lax.ppermute(far_lo, "tile", [(middle, 0)])
-    hbf, haf = up(far_hi, middle), down(far_lo, middle)
-    hbt = lax.ppermute(turn_up, "tile", [(t_n - 1, middle)])
-    hat = lax.ppermute(turn_down, "tile", [(0, middle - 1)])
+    turned = lax.ppermute(turn, "tile", [(middle - 1, t_n - 1), (middle, 0)])
+    far_got = swapped(far_a, 0, middle), swapped(far_b, 1, middle)
+    turned = lax.ppermute(turned, "tile", [(t_n - 1, middle), (0, middle - 1)])
 
     geo = call(
         functools.partial(pick_kernel, (t_n, s_n, rows, cols, nx, fd), False),
@@ -653,20 +677,24 @@
         [vm((fd, rows, nx), jnp.float32), vm((2, rows, SUB, nx), jnp.float32)] + scratch(1, 0)
         + [pltpu.SemaphoreType.DMA((chunks,))],
     )
-    geo, winds, level_rim = call(
+    riding = f32(-(-(6 * own + 2) // SUB) * SUB, nx)
+    geo, winds, level_rim, hb, ha = call(
         functools.partial(pick_kernel, (t_n, s_n, rows, cols, nx, fd, own), True),
-        (arrived, land_mask, intersection, wind, hb, ha, level_rim), [VM] * 7,
-        (f32(4 * ext, nx), f32(2 * ext, nx), f32(6, cols + 8, ny)), (VM,) * 3, [],
+        (arrived, land_mask, intersection, wind, got_a, got_b, level_rim), [VM] * 7,
+        (f32(4 * ext, nx), f32(2 * ext, nx), f32(6, cols + 8, ny), riding, riding), (VM,) * 5, [],
     )
 
     planes = {k: {} for k in range(WSTEPS + 1)}
     for j in range(HALO):
         k, at = min(j, 2), max(j - 2, 0) * fd
-        planes[0][-1 - j] = (((hb,), (hbn,), (hbf, hbt))[k], at)
-        planes[0][rows + j] = (((ha,), (han,), (haf, hat))[k], at)
+        a, b = ((got_a, got_b), next_got, far_got)[k]
+        corner = (turned,) if k == 2 else ()
+        planes[0][-1 - j] = ((b, a) + corner, at)
+        planes[0][rows + j] = ((a, b) + corner, at)
         if j < 2:
-            planes[0][j] = (((near_lo,), (next_lo,))[j], 0)
-            planes[0][rows - 1 - j] = (((near_hi,), (next_hi,))[j], 0)
+            a, b = ((near_a, near_b), (next_a, next_b))[j]
+            planes[0][j] = ((b, a), 0)
+            planes[0][rows - 1 - j] = ((a, b), 0)
     for k, r in enumerate(range(1, rows - 1)):
         planes[1][r] = ((mid,), k * fd)
     grown = {r: ((growth0,), r * fd) for r in range(rows)}

time: 154 us -> 136 us (0.88)
  starting transfers between devices: 42.9 us -> 20 us
  waiting for transfers between devices: 2.81 us -> 12.8 us
  blocking collectives: 48 us -> 42.9 us
    ppermute x10 -> x8, starting transfers between devices: 36.5 us -> 13.3 us  [the longest x6 10.1 us: swapped(): lax.ppermute(x, 'tile', [(i, i + 1) for i in lower] + [(i + 1, i) for i i...]
    ppermute x10 -> x8, waiting for transfers between devices: 0.51 us -> 9.06 us  [the longest x1 9.04 us: program(): turned = lax.ppermute(turn, 'tile', [(middle - 1, t_n - 1), (middle, 0)])]
    all_to_all x1, blocking collectives: 34.5 us -> 28.7 us  [program(): arrived = lax.all_to_all(send, AXES, 0, 0, tiled=True)]
  transfers between devices with their start and end apart: 16 -> 14, of which waited for: 2 -> 2; matrix products, arithmetic and copies ran while one was open for 0% -> 0% of each run, Pallas kernels for 25% -> 28%
where the time goes in v4:
time: 136 us; the launch traced here: 135 us
  Pallas kernels  58 us (43%)
  blocking collectives  42.9 us (32%)
  starting transfers between devices  20 us (15%)
  waiting for transfers between devices  12.8 us (9%)
    pallas_call x12, Pallas kernels, call(): pl.pallas_call(kernel, out_shape=shapes, in_specs=specs, out_specs=out_sp...  58 us
    all_to_all x1, blocking collectives, program(): arrived = lax.all_to_all(send, AXES, 0, 0, tiled=True)  28.7 us
    all_to_all x1, blocking collectives, program(): landed = lax.all_to_all(totals[WSTEPS], AXES, 0, 0, tiled=True)  14.3 us
    ppermute x6, starting transfers between devices, swapped(): lax.ppermute(x, 'tile', [(i, i + 1) for i in lower] + [(i + 1, i) for i i...  10.1 us
    ppermute x1, waiting for transfers between devices, program(): turned = lax.ppermute(turn, 'tile', [(middle - 1, t_n - 1), (middle, 0)])  9.04 us
    ppermute x6, starting transfers between devices, others(): lax.ppermute(x, 'spec', [(i, (i + k) % s_n) for i in range(s_n)])  6.66 us
    ppermute x6, waiting for transfers between devices, others(): lax.ppermute(x, 'spec', [(i, (i + k) % s_n) for i in range(s_n)])  3.72 us
  transfers between devices with their start and end apart: 14, of which 2 were waited for; matrix products, arithmetic and copies ran while one was open for 0% of the time, Pallas kernels for 28%

profile of v4, /device:TPU:0, one launch (start us, length us, event | category | flops | bytes accessed | tf_op | source)
XLA Modules:
  0.0 135.3 jit_solution(1517776183130335036)
XLA Ops:
  0.6 0.0 copy-start.10
  0.6 0.7 copy-done.10
  1.3 6.2 %shard_map.95 = (f32[32,16,128]{2,1,0:T(8,128)S(1)}, f32[3,2,32,64]{3,2,1,0:T(8,128)S(1)}, f32[592,256]{1,0:T(8,128)}, f32[592,256]{1,0:T(8,128)}, f32[576,256]{...) custom-call(f32[2,3,12]{2,1,0:T(4,128)S(1)} %copy-done.10, ...), custom_call_target="tpu_custom_call" | custom-call | tf_op jit(solution)/shard_map/pallas_call | solution.py:633
  7.5 0.0 copy-start
  7.5 1.4 %collective-permute-start.6 = (f32[1152,256]{1,0:T(8,128)}, f32[1152,256]{1,0:T(8,128)S(1)}, u32[]{:S(2)}, u32[]{:S(2)}) collective-permute-start(f32[1152,256]{1,0:T(8,128)} %get-tuple-element.52), channel_id=1, source_target_pairs={{6,14},{8,0},{7,15},{9,1},{22,30},{24,16},{23,31},{25,17}} | collective-permute-start | bytes 3538952 | tf_op jit(solution)/shard_map/ppermute | solution.py:660
  9.0 0.1 collective-permute-start
  9.0 0.7 collective-permute-start.1
  9.7 0.7 collective-permute-start.4
  10.5 7.3 %collective-permute-start.5 = (f32[1152,256]{1,0:T(8,128)}, f32[1152,256]{1,0:T(8,128)S(1)}, u32[]{:S(2)}, u32[]{:S(2)}) collective-permute-start(f32[1152,256]{1,0:T(8,128)} %get-tuple-element.51), channel_id=1, source_target_pairs={{0,2},{4,6},{8,10},{12,14},{2,0},{6,4},{10,8},{14,12},{1,3},{5,7},... | collective-permute-start | bytes 3538952 | tf_op jit(solution)/shard_map/ppermute | solution.py:624
  17.8 9.0 %collective-permute-done.6 = f32[1152,256]{1,0:T(8,128)S(1)} collective-permute-done((f32[1152,256]{1,0:T(8,128)}, f32[1152,256]{1,0:T(8,128)S(1)}, u32[]{:S(2)}, u32[]{:S(2)}) %collective-permute-start.6) | collective-permute-done | bytes 1179680 | tf_op jit(solution)/shard_map/ppermute | solution.py:660
  26.8 1.8 %collective-permute-start.7 = (f32[1152,256]{1,0:T(8,128)S(1)}, f32[1152,256]{1,0:T(8,128)S(1)}, u32[]{:S(2)}, u32[]{:S(2)}) collective-permute-start(f32[1152,256]{1,0:T(8,128)S(1)} %collective-permute-done.6), channel_id=1, source_target_pairs={{14,8},{0,6},{15,9},{1,7},{30,24},{16,22},{31,25},{17,23}} | collective-permute-start | bytes 3538952 | tf_op jit(solution)/shard_map/ppermute | solution.py:662
  28.6 0.0 collective-permute-done.refs_1_.refs_7_.refs_10_
  28.7 0.7 collective-permute-start.2
  29.4 0.0 collective-permute-done.1.refs_2_.refs_6_.refs_9_
  29.4 0.6 collective-permute-start.3
  29.9 28.7 %all_to_all.10.got_ref = f32[32,16,128]{2,1,0:T(8,128)S(1)} all-to-all(f32[32,16,128]{2,1,0:T(8,128)S(1)} %get-tuple-element.39), channel_id=1, replica_groups=mesh['grp'=2,'tile'=8,'spec'=2] {'grp','tile','spec'}, dimensions={0} | all-to-all | bytes 524288 | tf_op jit(solution)/shard_map/all_to_all | solution.py:657
  58.6 0.0 copy-done.6
  58.6 0.6 shard_map.96
  59.2 0.0 collective-permute-done.2.refs_4_.refs_7_
  59.2 2.3 %collective-permute-start.12 = (f32[6,40,64]{2,1,0:T(8,128)S(1)}, f32[6,40,64]{2,1,0:T(8,128)S(1)}, u32[]{:S(2)}, u32[]{:S(2)}) collective-permute-start(f32[6,40,64]{2,1,0:T(8,128)S(1)} %get-tuple-element.65), channel_id=1, source_target_pairs={{0,1},{1,0},{2,3},{3,2},{4,5},{5,4},{6,7},{7,6},{8,9},{9,8},{10,11... | collective-permute-start | bytes 184328 | tf_op jit(solution)/shard_map/ppermute | solution.py:627
  61.5 0.6 shard_map.97.geo_ref
  62.1 0.0 copy-done
  62.2 7.1 %shard_map.98 = (f32[3456,256]{1,0:T(8,128)S(1)}, f32[16,256]{1,0:T(8,128)S(1)}, f32[4608,256]{1,0:T(8,128)S(1)}) custom-call(f32[2,576,16]{2,1,0:T(8,128)S(1)} %copy-done, f32[64,256]{1,0:T(8,128)S(1)} %shard_map.97.geo_ref, f32[2,8,256]{2,1,0:T(8,128)S(1)} %copy-done.6, f32[576,8,256]{2,1,0:T(8,128)} %bitcast.11), custom_call_target="tpu_custom_call" | custom-call | tf_op jit(solution)/shard_map/pallas_call | solution.py:633
  69.3 0.0 collective-permute-done.3.refs_5_.refs_8_
  69.3 4.8 %shard_map.99 = (f32[2304,256]{1,0:T(8,128)S(1)}, f32[16,256]{1,0:T(8,128)S(1)}, f32[1152,256]{1,0:T(8,128)S(1)}) custom-call(f32[2,576,16]{2,1,0:T(8,128)S(1)} %copy-done, f32[64,256]{1,0:T(8,128)S(1)} %get-tuple-element.43.refs_1_.geo_ref, f32[32,256]{1,0:T(8,128)S(1)} %get-tuple-element.44.refs_2_, f32[16,256]{1,0:T(8,128)S(1)} %get-tuple-element.45.refs_3_, ...), custom_call_target="tpu_custom_call" | custom-call | tf_op jit(solution)/shard_map/pallas_call | solution.py:633
  74.1 0.1 collective-permute-start.9
  74.2 0.0 collective-permute-done.4.refs_4_
  74.2 0.0 collective-permute-done.5.refs_5_
  74.2 0.0 collective-permute-done.7.refs_6_
  74.3 4.8 %shard_map.100 = (f32[2304,256]{1,0:T(8,128)S(1)}, f32[16,256]{1,0:T(8,128)S(1)}, f32[2304,256]{1,0:T(8,128)S(1)}) custom-call(f32[2,576,16]{2,1,0:T(8,128)S(1)} %copy-done, f32[64,256]{1,0:T(8,128)S(1)} %get-tuple-element.43.refs_1_.geo_ref, f32[32,256]{1,0:T(8,128)S(1)} %get-tuple-element.44.refs_2_, f32[16,256]{1,0:T(8,128)S(1)} %get-tuple-element.49.refs_3_.refs_2_, ...), custom_call_target="tpu_custom_call" | custom-call | tf_op jit(solution)/shard_map/pallas_call | solution.py:633
  79.0 2.1 %collective-permute-start.8 = (f32[16,256]{1,0:T(8,128)S(1)}, f32[16,256]{1,0:T(8,128)S(1)}, u32[]{:S(2)}, u32[]{:S(2)}) collective-permute-start(f32[16,256]{1,0:T(8,128)S(1)} %get-tuple-element.53.refs_2_), channel_id=1, source_target_pairs={{0,1},{1,0},{2,3},{3,2},{4,5},{5,4},{6,7},{7,6},{8,9},{9,8},{10,11... | collective-permute-start | bytes 49160 | tf_op jit(solution)/shard_map/ppermute | solution.py:627
  81.1 0.0 collective-permute-done.9.refs_3_
  81.1 6.0 %shard_map.101 = (f32[4608,256]{1,0:T(8,128)S(1)}, f32[16,256]{1,0:T(8,128)S(1)}) custom-call(f32[2,576,16]{2,1,0:T(8,128)S(1)} %copy-done, f32[64,256]{1,0:T(8,128)S(1)} %get-tuple-element.43.refs_1_.geo_ref, f32[16,256]{1,0:T(8,128)S(1)} %get-tuple-element.49.refs_3_.refs_2_, f32[16,256]{1,0:T(8,128)S(1)} %collective-permute-done.9.refs_3_, ...), custom_call_target="tpu_custom_call" | custom-call | tf_op jit(solution)/shard_map/pallas_call | solution.py:633
  87.1 0.1 collective-permute-start.11
  87.2 0.0 collective-permute-done.8.refs_3_
  87.2 4.7 %shard_map.102 = (f32[2304,256]{1,0:T(8,128)S(1)}, f32[16,256]{1,0:T(8,128)S(1)}) custom-call(f32[2,576,16]{2,1,0:T(8,128)S(1)} %copy-done, f32[64,256]{1,0:T(8,128)S(1)} %get-tuple-element.43.refs_1_.geo_ref, f32[16,256]{1,0:T(8,128)S(1)} %get-tuple-element.53.refs_2_, f32[16,256]{1,0:T(8,128)S(1)} %collective-permute-done.8.refs_3_, ...), custom_call_target="tpu_custom_call" | custom-call | tf_op jit(solution)/shard_map/pallas_call | solution.py:633
  91.9 2.1 %collective-permute-start.10 = (f32[16,256]{1,0:T(8,128)S(1)}, f32[16,256]{1,0:T(8,128)S(1)}, u32[]{:S(2)}, u32[]{:S(2)}) collective-permute-start(f32[16,256]{1,0:T(8,128)S(1)} %get-tuple-element.60.refs_2_), channel_id=1, source_target_pairs={{0,1},{1,0},{2,3},{3,2},{4,5},{5,4},{6,7},{7,6},{8,9},{9,8},{10,11... | collective-permute-start | bytes 49160 | tf_op jit(solution)/shard_map/ppermute | solution.py:627
  93.9 0.0 collective-permute-done.11.refs_3_
  93.9 5.2 %shard_map.103 = (f32[3456,256]{1,0:T(8,128)S(1)}, f32[16,256]{1,0:T(8,128)S(1)}) custom-call(f32[2,576,16]{2,1,0:T(8,128)S(1)} %copy-done, f32[64,256]{1,0:T(8,128)S(1)} %get-tuple-element.43.refs_1_.geo_ref, f32[16,256]{1,0:T(8,128)S(1)} %get-tuple-element.56.refs_4_.refs_2_, f32[16,256]{1,0:T(8,128)S(1)} %collective-permute-done.11.refs_3_, ...), custom_call_target="tpu_custom_call" | custom-call | tf_op jit(solution)/shard_map/pallas_call | solution.py:633
  99.1 0.0 collective-permute-done.10.refs_3_
  99.1 4.8 %shard_map.104 = (f32[2304,256]{1,0:T(8,128)S(1)}, f32[16,256]{1,0:T(8,128)S(1)}) custom-call(f32[2,576,16]{2,1,0:T(8,128)S(1)} %copy-done, f32[64,256]{1,0:T(8,128)S(1)} %get-tuple-element.43.refs_1_.geo_ref, f32[16,256]{1,0:T(8,128)S(1)} %get-tuple-element.60.refs_2_, f32[16,256]{1,0:T(8,128)S(1)} %collective-permute-done.10.refs_3_, ...), custom_call_target="tpu_custom_call" | custom-call | tf_op jit(solution)/shard_map/pallas_call | solution.py:633
  103.9 0.1 collective-permute-start.13
  104.0 0.0 collective-permute-done.12.lev_ref
  104.0 3.7 %collective-permute-done.13.refs_3_ = f32[16,256]{1,0:T(8,128)S(1)} collective-permute-done((f32[16,256]{1,0:T(8,128)S(1)}, f32[16,256]{1,0:T(8,128)S(1)}, u32[]{:S(2)}, u32[]{:S(2)}) %collective-permute-start.13) | collective-permute-done | bytes 16416 | tf_op jit(solution)/shard_map/ppermute | solution.py:627
  107.8 8.0 %shard_map.105 = (f32[4608,256]{1,0:T(8,128)S(1)}, f32[32,8,256]{2,1,0:T(8,128)S(1)}) custom-call(f32[2,576,16]{2,1,0:T(8,128)S(1)} %copy-done, f32[64,256]{1,0:T(8,128)S(1)} %get-tuple-element.43.refs_1_.geo_ref, f32[16,256]{1,0:T(8,128)S(1)} %get-tuple-element.66.refs_2_, f32[16,256]{1,0:T(8,128)S(1)} %collective-permute-done.13.refs_3_, ...), custom_call_target="tpu_custom_call" | custom-call | tf_op jit(solution)/shard_map/pallas_call | solution.py:633
  115.7 14.3 %all_to_all.11.got_ref = f32[32,8,256]{2,1,0:T(8,128)S(1)} all-to-all(f32[32,8,256]{2,1,0:T(8,128)S(1)} %get-tuple-element.69), channel_id=1, replica_groups=mesh['grp'=2,'tile'=8,'spec'=2] {'grp','tile','spec'}, dimensions={0} | all-to-all | bytes 524288 | tf_op jit(solution)/shard_map/all_to_all | solution.py:760
  130.0 0.0 copy-done.9
  130.0 5.3 %shard_map.106 = (f32[576,8,256]{2,1,0:T(8,128)}, f32[3,8,32,64]{3,2,1,0:T(8,128)}) custom-call(f32[2,576,16]{2,1,0:T(8,128)S(1)} %copy-done, f32[2,3,12]{2,1,0:T(4,128)S(1)} %copy-done.11, f32[32,8,256]{2,1,0:T(8,128)S(1)} %all_to_all.11.got_ref, f32[64,256]{1,0:T(8,128)S(1)} %get-tuple-element.43.refs_1_.geo_ref, ...), custom_call_target="tpu_custom_call" | custom-call | tf_op jit(solution)/shard_map/pallas_call | solution.py:633
  (18 shorter events, 0.0 us)
Async XLA Ops:
  0.6 0.7 copy-start.10
  1.3 57.3 %copy-start.6 = (f32[2,8,256]{2,1,0:T(8,128)S(1)}, f32[2,8,256]{2,1,0:T(8,128)}, u32[]{:S(2)}) copy-start(f32[2,8,256]{2,1,0:T(8,128)} %wind_ref.1) | copy-start | bytes 49156
  1.3 57.3 %copy-start.7 = (s32[8,256]{1,0:T(8,128)S(1)}, s32[8,256]{1,0:T(8,128)}, u32[]{:S(2)}) copy-start(s32[8,256]{1,0:T(8,128)} %refs_4_.1) | copy-start | bytes 24580
  1.3 57.3 %copy-start.8 = (s32[8,256]{1,0:T(8,128)S(1)}, s32[8,256]{1,0:T(8,128)}, u32[]{:S(2)}) copy-start(s32[8,256]{1,0:T(8,128)} %mask_ref.3) | copy-start | bytes 24580
  7.5 54.6 %copy-start = (f32[2,576,16]{2,1,0:T(8,128)S(1)}, f32[2,576,16]{2,1,0:T(8,128)}, u32[]{:S(2)}) copy-start(f32[2,576,16]{2,1,0:T(8,128)} %constant.4.clone.table_ref.refs_0_) | copy-start | bytes 221188
  7.5 19.3 %collective-permute-start.6 = (f32[1152,256]{1,0:T(8,128)}, f32[1152,256]{1,0:T(8,128)S(1)}, u32[]{:S(2)}, u32[]{:S(2)}) collective-permute-start(f32[1152,256]{1,0:T(8,128)} %get-tuple-element.52), channel_id=1, source_target_pairs={{6,14},{8,0},{7,15},{9,1},{22,30},{24,16},{23,31},{25,17}} | collective-permute-start | bytes 3538952 | tf_op jit(solution)/shard_map/ppermute | solution.py:660
  9.0 19.7 %collective-permute-start = (f32[592,256]{1,0:T(8,128)}, f32[592,256]{1,0:T(8,128)S(1)}, u32[]{:S(2)}, u32[]{:S(2)}) collective-permute-start(f32[592,256]{1,0:T(8,128)} %get-tuple-element.40.refs_9_), channel_id=1, source_target_pairs={{0,2},{4,6},{8,10},{12,14},{2,0},{6,4},{10,8},{14,12},{1,3},{5,7},... | collective-permute-start | bytes 1818632 | tf_op jit(solution)/shard_map/ppermute | solution.py:624
  9.0 20.3 %collective-permute-start.1 = (f32[592,256]{1,0:T(8,128)}, f32[592,256]{1,0:T(8,128)S(1)}, u32[]{:S(2)}, u32[]{:S(2)}) collective-permute-start(f32[592,256]{1,0:T(8,128)} %get-tuple-element.41.refs_8_), channel_id=1, source_target_pairs={{2,4},{6,8},{10,12},{4,2},{8,6},{12,10},{3,5},{7,9},{11,13},{5,3},... | collective-permute-start | bytes 1818632 | tf_op jit(solution)/shard_map/ppermute | solution.py:624
  9.7 64.5 %collective-permute-start.4 = (f32[1152,256]{1,0:T(8,128)}, f32[1152,256]{1,0:T(8,128)S(1)}, u32[]{:S(2)}, u32[]{:S(2)}) collective-permute-start(f32[1152,256]{1,0:T(8,128)} %get-tuple-element.50), channel_id=1, source_target_pairs={{2,4},{10,12},{4,2},{12,10},{3,5},{11,13},{5,3},{13,11},{18,20},{2... | collective-permute-start | bytes 3538952 | tf_op jit(solution)/shard_map/ppermute | solution.py:624
  10.5 63.8 %collective-permute-start.5 = (f32[1152,256]{1,0:T(8,128)}, f32[1152,256]{1,0:T(8,128)S(1)}, u32[]{:S(2)}, u32[]{:S(2)}) collective-permute-start(f32[1152,256]{1,0:T(8,128)} %get-tuple-element.51), channel_id=1, source_target_pairs={{0,2},{4,6},{8,10},{12,14},{2,0},{6,4},{10,8},{14,12},{1,3},{5,7},... | collective-permute-start | bytes 3538952 | tf_op jit(solution)/shard_map/ppermute | solution.py:624
  26.8 47.4 %collective-permute-start.7 = (f32[1152,256]{1,0:T(8,128)S(1)}, f32[1152,256]{1,0:T(8,128)S(1)}, u32[]{:S(2)}, u32[]{:S(2)}) collective-permute-start(f32[1152,256]{1,0:T(8,128)S(1)} %collective-permute-done.6), channel_id=1, source_target_pairs={{14,8},{0,6},{15,9},{1,7},{30,24},{16,22},{31,25},{17,23}} | collective-permute-start | bytes 3538952 | tf_op jit(solution)/shard_map/ppermute | solution.py:662
  28.7 30.6 %collective-permute-start.2 = (f32[576,256]{1,0:T(8,128)}, f32[576,256]{1,0:T(8,128)S(1)}, u32[]{:S(2)}, u32[]{:S(2)}) collective-permute-start(f32[576,256]{1,0:T(8,128)} %get-tuple-element.46.refs_10_), channel_id=1, source_target_pairs={{2,4},{6,8},{10,12},{4,2},{8,6},{12,10},{3,5},{7,9},{11,13},{5,3},... | collective-permute-start | bytes 1769480 | tf_op jit(solution)/shard_map/ppermute | solution.py:624
  29.4 39.9 %collective-permute-start.3 = (f32[576,256]{1,0:T(8,128)}, f32[576,256]{1,0:T(8,128)S(1)}, u32[]{:S(2)}, u32[]{:S(2)}) collective-permute-start(f32[576,256]{1,0:T(8,128)} %get-tuple-element.47.refs_11_), channel_id=1, source_target_pairs={{0,2},{4,6},{8,10},{12,14},{2,0},{6,4},{10,8},{14,12},{1,3},{5,7},... | collective-permute-start | bytes 1769480 | tf_op jit(solution)/shard_map/ppermute | solution.py:624
  59.2 44.8 %collective-permute-start.12 = (f32[6,40,64]{2,1,0:T(8,128)S(1)}, f32[6,40,64]{2,1,0:T(8,128)S(1)}, u32[]{:S(2)}, u32[]{:S(2)}) collective-permute-start(f32[6,40,64]{2,1,0:T(8,128)S(1)} %get-tuple-element.65), channel_id=1, source_target_pairs={{0,1},{1,0},{2,3},{3,2},{4,5},{5,4},{6,7},{7,6},{8,9},{9,8},{10,11... | collective-permute-start | bytes 184328 | tf_op jit(solution)/shard_map/ppermute | solution.py:627
  62.1 7.2 %copy-start.2 = (f32[592,256]{1,0:T(8,128)S(1)}, f32[592,256]{1,0:T(8,128)}, u32[]{:S(2)}) copy-start(f32[592,256]{1,0:T(8,128)} %get-tuple-element.40.refs_9_) | copy-start | bytes 1818628
  62.1 7.2 %copy-start.3 = (f32[592,256]{1,0:T(8,128)S(1)}, f32[592,256]{1,0:T(8,128)}, u32[]{:S(2)}) copy-start(f32[592,256]{1,0:T(8,128)} %get-tuple-element.41.refs_8_) | copy-start | bytes 1818628
  62.1 7.2 %copy-start.4 = (f32[576,256]{1,0:T(8,128)S(1)}, f32[576,256]{1,0:T(8,128)}, u32[]{:S(2)}) copy-start(f32[576,256]{1,0:T(8,128)} %get-tuple-element.47.refs_11_) | copy-start | bytes 1769476
  62.1 7.2 %copy-start.5 = (f32[576,256]{1,0:T(8,128)S(1)}, f32[576,256]{1,0:T(8,128)}, u32[]{:S(2)}) copy-start(f32[576,256]{1,0:T(8,128)} %get-tuple-element.46.refs_10_) | copy-start | bytes 1769476
  74.1 6.9 %collective-permute-start.9 = (f32[16,256]{1,0:T(8,128)S(1)}, f32[16,256]{1,0:T(8,128)S(1)}, u32[]{:S(2)}, u32[]{:S(2)}) collective-permute-start(f32[16,256]{1,0:T(8,128)S(1)} %get-tuple-element.49.refs_3_.refs_2_), channel_id=1, source_target_pairs={{0,1},{1,0},{2,3},{3,2},{4,5},{5,4},{6,7},{7,6},{8,9},{9,8},{10,11... | collective-permute-start | bytes 49160 | tf_op jit(solution)/shard_map/ppermute | solution.py:627
  79.0 8.1 %collective-permute-start.8 = (f32[16,256]{1,0:T(8,128)S(1)}, f32[16,256]{1,0:T(8,128)S(1)}, u32[]{:S(2)}, u32[]{:S(2)}) collective-permute-start(f32[16,256]{1,0:T(8,128)S(1)} %get-tuple-element.53.refs_2_), channel_id=1, source_target_pairs={{0,1},{1,0},{2,3},{3,2},{4,5},{5,4},{6,7},{7,6},{8,9},{9,8},{10,11... | collective-permute-start | bytes 49160 | tf_op jit(solution)/shard_map/ppermute | solution.py:627
  87.1 6.9 %collective-permute-start.11 = (f32[16,256]{1,0:T(8,128)S(1)}, f32[16,256]{1,0:T(8,128)S(1)}, u32[]{:S(2)}, u32[]{:S(2)}) collective-permute-start(f32[16,256]{1,0:T(8,128)S(1)} %get-tuple-element.56.refs_4_.refs_2_), channel_id=1, source_target_pairs={{0,1},{1,0},{2,3},{3,2},{4,5},{5,4},{6,7},{7,6},{8,9},{9,8},{10,11... | collective-permute-start | bytes 49160 | tf_op jit(solution)/shard_map/ppermute | solution.py:627
  91.9 7.3 %collective-permute-start.10 = (f32[16,256]{1,0:T(8,128)S(1)}, f32[16,256]{1,0:T(8,128)S(1)}, u32[]{:S(2)}, u32[]{:S(2)}) collective-permute-start(f32[16,256]{1,0:T(8,128)S(1)} %get-tuple-element.60.refs_2_), channel_id=1, source_target_pairs={{0,1},{1,0},{2,3},{3,2},{4,5},{5,4},{6,7},{7,6},{8,9},{9,8},{10,11... | collective-permute-start | bytes 49160 | tf_op jit(solution)/shard_map/ppermute | solution.py:627
  103.9 3.8 %collective-permute-start.13 = (f32[16,256]{1,0:T(8,128)S(1)}, f32[16,256]{1,0:T(8,128)S(1)}, u32[]{:S(2)}, u32[]{:S(2)}) collective-permute-start(f32[16,256]{1,0:T(8,128)S(1)} %get-tuple-element.66.refs_2_), channel_id=1, source_target_pairs={{0,1},{1,0},{2,3},{3,2},{4,5},{5,4},{6,7},{7,6},{8,9},{9,8},{10,11... | collective-permute-start | bytes 49160 | tf_op jit(solution)/shard_map/ppermute | solution.py:627
  107.8 22.2 %copy-start.1 = (f32[1,3,8,32,64]{4,3,2,1,0:T(8,128)S(1)}, f32[1,3,8,32,64]{4,3,2,1,0:T(8,128)}, u32[]{:S(2)}) copy-start(f32[1,3,8,32,64]{4,3,2,1,0:T(8,128)} %param.12) | copy-start | bytes 589828
  107.8 22.2 %copy-start.9 = (f32[1,32,64]{2,1,0:T(8,128)S(1)}, f32[1,32,64]{2,1,0:T(8,128)}, u32[]{:S(2)}) copy-start(f32[1,32,64]{2,1,0:T(8,128)} %param.13) | copy-start | bytes 24580
  107.8 22.2 %copy-start.11 = (f32[2,3,12]{2,1,0:T(4,128)S(1)}, f32[2,3,12]{2,1,0:T(4,128)}, u32[]{:S(2)}) copy-start(f32[2,3,12]{2,1,0:T(4,128)} %constant.5.clone.level_ref) | copy-start | bytes 868

commit v5 on v4

--- a/solution.py
+++ b/solution.py
@@ -14,7 +14,8 @@
 HALO = WSTEPS
 LANES = 128
 SUB = 8
-UNROLL = 4
+UNROLL = 6
+UNROLL_SUMS = 4
 AXES = ("grp", "tile", "spec")
 
 BW, GE, GN, WE, WN, SX, SY, DX, DY, INV = range(10)
@@ -184,17 +185,18 @@
                     ref[k * stack + m : k * stack + m + 1, 0:ny] = ocean[m, at : at + 1, :]
                 ref[2 * stack + k : 2 * stack + k + 1, 0:ny] = sea[at : at + 1, :]
 
+    turns = [(t_n // 2 - 1, far_hi), (t_n // 2, far_lo)]
+
+    def turning(source):
+        return pltpu.make_async_copy(source, turn_hbm, sem.at[chunks + 5])
+
+    for at, source in turns:
+        pl.when(tile == at)(turning(source).start)
     send_out(0)
-    for at, source in ((t_n // 2 - 1, far_hi), (t_n // 2, far_lo)):
-
-        @pl.when(tile == at)
-        def _():
-            copy = pltpu.make_async_copy(source, turn_hbm, sem.at[chunks + 5])
-            copy.start()
-            copy.wait()
-
     for copy in outward:
         copy.wait()
+    for at, source in turns:
+        pl.when(tile == at)(turning(source).wait)
 
 
 def pick_kernel(n, full, got_ref, mask_ref, cross_ref, *refs):
@@ -255,6 +257,7 @@
 
 def advance(segments, fd, nx, s, table_ref, planes, store, splat, acc, sums, before=None):
     halves = nx // LANES
+    unroll = UNROLL_SUMS if sums else UNROLL
     lane = lanes_of((SUB, LANES))
     first, last = lane == 0, lane == LANES - 1
     acc[...] = jnp.zeros(acc.shape, jnp.float32)
@@ -267,8 +270,8 @@
         def add(key, value):
             totals[key] = totals[key] + value if key in totals else value
 
-        for k in range(UNROLL):
-            at = pl.multiple_of((i * UNROLL + k) * SUB, SUB)
+        for k in range(unroll):
+            at = pl.multiple_of((i * unroll + k) * SUB, SUB)
             sl = pl.ds(at, SUB)
             ge, gn = wide(table_ref[s, sl, GE : GE + 1]), wide(table_ref[s, sl, GN : GN + 1])
             bands = [wide(table_ref[s, sl, b : b + 1]) for b in (SX, SY, DX, DY)] if sums else None
@@ -312,7 +315,7 @@
             acc[kind, r + HALO, :, half(h)] += value
         return carry
 
-    lax.fori_loop(0, fd // (SUB * UNROLL), body, 0)
+    lax.fori_loop(0, fd // (SUB * unroll), body, 0)
 
 
 def folded(acc, kind, rows):
@@ -496,8 +499,8 @@
         for c in range(chunks):
 
             def finish(i, carry):
-                for k in range(2):
-                    at = pl.multiple_of(c * part + (2 * i + k) * SUB, SUB)
+                for k in range(4):
+                    at = pl.multiple_of(c * part + (4 * i + k) * SUB, SUB)
                     sl = pl.ds(at, SUB)
                     inv = wide(table_ref[s, sl, INV : INV + 1])
                     for h in range(nx // LANES):
@@ -507,7 +510,7 @@
                         raw[sl, :, half(h)] = jnp.swapaxes(jnp.stack(values), 0, 1)
                 return carry
 
-            lax.fori_loop(0, part // (2 * SUB), finish, 0)
+            lax.fori_loop(0, part // (4 * SUB), finish, 0)
             write(c, c).start()
         out[...] = jnp.zeros((3, own, cols, ny), jnp.float32)
         ocean_copy.start()

time: 136 us -> 128 us (0.941)
  Pallas kernels: 58 us -> 50.5 us
    pallas_call x12, Pallas kernels: 58 us -> 50.5 us  [call(): pl.pallas_call(kernel, out_shape=shapes, in_specs=specs, out_specs=out_sp...]
  transfers between devices with their start and end apart: 14 -> 14, of which waited for: 2 -> 2; matrix products, arithmetic and copies ran while one was open for 0% -> 0% of each run, Pallas kernels for 28% -> 25%
where the time goes in v5:
time: 128 us
  Pallas kernels  50.5 us (39%)
  blocking collectives  42.9 us (34%)
  starting transfers between devices  20 us (16%)
  waiting for transfers between devices  12.7 us (10%)
    pallas_call x12, Pallas kernels, call(): pl.pallas_call(kernel, out_shape=shapes, in_specs=specs, out_specs=out_sp...  50.5 us
    all_to_all x1, blocking collectives, program(): arrived = lax.all_to_all(send, AXES, 0, 0, tiled=True)  28.7 us
    all_to_all x1, blocking collectives, program(): landed = lax.all_to_all(totals[WSTEPS], AXES, 0, 0, tiled=True)  14.3 us
    ppermute x6, starting transfers between devices, swapped(): lax.ppermute(x, 'tile', [(i, i + 1) for i in lower] + [(i + 1, i) for i i...  9.97 us
    ppermute x1, waiting for transfers between devices, program(): turned = lax.ppermute(turn, 'tile', [(middle - 1, t_n - 1), (middle, 0)])  8.96 us
    ppermute x6, starting transfers between devices, others(): lax.ppermute(x, 'spec', [(i, (i + k) % s_n) for i in range(s_n)])  6.74 us
    ppermute x6, waiting for transfers between devices, others(): lax.ppermute(x, 'spec', [(i, (i + k) % s_n) for i in range(s_n)])  3.72 us
  transfers between devices with their start and end apart: 14, of which 2 were waited for; matrix products, arithmetic and copies ran while one was open for 0% of the time, Pallas kernels for 25%

profile of v5, /device:TPU:0, one launch (start us, length us, event | category | flops | bytes accessed | tf_op | source)
XLA Modules:
  0.0 127.9 jit_solution(10515003952027070571)
XLA Ops:
  0.6 0.0 copy-start.10
  0.6 0.7 copy-done.10
  1.3 6.2 %shard_map.95 = (f32[32,16,128]{2,1,0:T(8,128)S(1)}, f32[3,2,32,64]{3,2,1,0:T(8,128)S(1)}, f32[592,256]{1,0:T(8,128)}, f32[592,256]{1,0:T(8,128)}, f32[576,256]{...) custom-call(f32[2,3,12]{2,1,0:T(4,128)S(1)} %copy-done.10, ...), custom_call_target="tpu_custom_call" | custom-call | tf_op jit(solution)/shard_map/pallas_call | solution.py:636
  7.5 0.0 copy-start
  7.5 1.4 %collective-permute-start.6 = (f32[1152,256]{1,0:T(8,128)}, f32[1152,256]{1,0:T(8,128)S(1)}, u32[]{:S(2)}, u32[]{:S(2)}) collective-permute-start(f32[1152,256]{1,0:T(8,128)} %get-tuple-element.52), channel_id=1, source_target_pairs={{6,14},{8,0},{7,15},{9,1},{22,30},{24,16},{23,31},{25,17}} | collective-permute-start | bytes 3538952 | tf_op jit(solution)/shard_map/ppermute | solution.py:663
  9.0 0.1 collective-permute-start
  9.0 0.7 collective-permute-start.1
  9.7 0.7 collective-permute-start.4
  10.5 7.3 %collective-permute-start.5 = (f32[1152,256]{1,0:T(8,128)}, f32[1152,256]{1,0:T(8,128)S(1)}, u32[]{:S(2)}, u32[]{:S(2)}) collective-permute-start(f32[1152,256]{1,0:T(8,128)} %get-tuple-element.51), channel_id=1, source_target_pairs={{0,2},{4,6},{8,10},{12,14},{2,0},{6,4},{10,8},{14,12},{1,3},{5,7},... | collective-permute-start | bytes 3538952 | tf_op jit(solution)/shard_map/ppermute | solution.py:627
  17.8 9.0 %collective-permute-done.6 = f32[1152,256]{1,0:T(8,128)S(1)} collective-permute-done((f32[1152,256]{1,0:T(8,128)}, f32[1152,256]{1,0:T(8,128)S(1)}, u32[]{:S(2)}, u32[]{:S(2)}) %collective-permute-start.6) | collective-permute-done | bytes 1179680 | tf_op jit(solution)/shard_map/ppermute | solution.py:663
  26.7 1.9 %collective-permute-start.7 = (f32[1152,256]{1,0:T(8,128)S(1)}, f32[1152,256]{1,0:T(8,128)S(1)}, u32[]{:S(2)}, u32[]{:S(2)}) collective-permute-start(f32[1152,256]{1,0:T(8,128)S(1)} %collective-permute-done.6), channel_id=1, source_target_pairs={{14,8},{0,6},{15,9},{1,7},{30,24},{16,22},{31,25},{17,23}} | collective-permute-start | bytes 3538952 | tf_op jit(solution)/shard_map/ppermute | solution.py:665
  28.6 0.0 collective-permute-done.refs_1_.refs_7_.refs_10_
  28.7 0.7 collective-permute-start.2
  29.4 0.0 collective-permute-done.1.refs_2_.refs_6_.refs_9_
  29.4 0.5 collective-permute-start.3
  29.9 28.7 %all_to_all.10.got_ref = f32[32,16,128]{2,1,0:T(8,128)S(1)} all-to-all(f32[32,16,128]{2,1,0:T(8,128)S(1)} %get-tuple-element.39), channel_id=1, replica_groups=mesh['grp'=2,'tile'=8,'spec'=2] {'grp','tile','spec'}, dimensions={0} | all-to-all | bytes 524288 | tf_op jit(solution)/shard_map/all_to_all | solution.py:660
  58.5 0.0 copy-done.7
  58.5 0.6 shard_map.96
  59.1 0.0 collective-permute-done.2.refs_4_.refs_7_
  59.2 2.4 %collective-permute-start.12 = (f32[6,40,64]{2,1,0:T(8,128)S(1)}, f32[6,40,64]{2,1,0:T(8,128)S(1)}, u32[]{:S(2)}, u32[]{:S(2)}) collective-permute-start(f32[6,40,64]{2,1,0:T(8,128)S(1)} %get-tuple-element.65), channel_id=1, source_target_pairs={{0,1},{1,0},{2,3},{3,2},{4,5},{5,4},{6,7},{7,6},{8,9},{9,8},{10,11... | collective-permute-start | bytes 184328 | tf_op jit(solution)/shard_map/ppermute | solution.py:630
  61.5 0.6 shard_map.97.geo_ref
  62.1 0.0 copy-done
  62.2 7.1 %shard_map.98 = (f32[3456,256]{1,0:T(8,128)S(1)}, f32[16,256]{1,0:T(8,128)S(1)}, f32[4608,256]{1,0:T(8,128)S(1)}) custom-call(f32[2,576,16]{2,1,0:T(8,128)S(1)} %copy-done, f32[64,256]{1,0:T(8,128)S(1)} %shard_map.97.geo_ref, f32[2,8,256]{2,1,0:T(8,128)S(1)} %copy-done.6, f32[576,8,256]{2,1,0:T(8,128)} %bitcast.11), custom_call_target="tpu_custom_call" | custom-call | tf_op jit(solution)/shard_map/pallas_call | solution.py:636
  69.3 0.0 collective-permute-done.3.refs_5_.refs_8_
  69.3 3.7 %shard_map.99 = (f32[2304,256]{1,0:T(8,128)S(1)}, f32[16,256]{1,0:T(8,128)S(1)}, f32[1152,256]{1,0:T(8,128)S(1)}) custom-call(f32[2,576,16]{2,1,0:T(8,128)S(1)} %copy-done, f32[64,256]{1,0:T(8,128)S(1)} %get-tuple-element.43.refs_1_.geo_ref, f32[32,256]{1,0:T(8,128)S(1)} %get-tuple-element.44.refs_2_, f32[16,256]{1,0:T(8,128)S(1)} %get-tuple-element.45.refs_3_, ...), custom_call_target="tpu_custom_call" | custom-call | tf_op jit(solution)/shard_map/pallas_call | solution.py:636
  73.0 0.1 collective-permute-start.9
  73.1 0.0 collective-permute-done.4.refs_4_
  73.1 0.0 collective-permute-done.5.refs_5_
  73.1 0.0 collective-permute-done.7.refs_6_
  73.1 3.8 %shard_map.100 = (f32[2304,256]{1,0:T(8,128)S(1)}, f32[16,256]{1,0:T(8,128)S(1)}, f32[2304,256]{1,0:T(8,128)S(1)}) custom-call(f32[2,576,16]{2,1,0:T(8,128)S(1)} %copy-done, f32[64,256]{1,0:T(8,128)S(1)} %get-tuple-element.43.refs_1_.geo_ref, f32[32,256]{1,0:T(8,128)S(1)} %get-tuple-element.44.refs_2_, f32[16,256]{1,0:T(8,128)S(1)} %get-tuple-element.49.refs_3_.refs_2_, ...), custom_call_target="tpu_custom_call" | custom-call | tf_op jit(solution)/shard_map/pallas_call | solution.py:636
  76.9 2.1 %collective-permute-start.8 = (f32[16,256]{1,0:T(8,128)S(1)}, f32[16,256]{1,0:T(8,128)S(1)}, u32[]{:S(2)}, u32[]{:S(2)}) collective-permute-start(f32[16,256]{1,0:T(8,128)S(1)} %get-tuple-element.53.refs_2_), channel_id=1, source_target_pairs={{0,1},{1,0},{2,3},{3,2},{4,5},{5,4},{6,7},{7,6},{8,9},{9,8},{10,11... | collective-permute-start | bytes 49160 | tf_op jit(solution)/shard_map/ppermute | solution.py:630
  79.0 0.0 collective-permute-done.9.refs_3_
  79.0 5.3 %shard_map.101 = (f32[4608,256]{1,0:T(8,128)S(1)}, f32[16,256]{1,0:T(8,128)S(1)}) custom-call(f32[2,576,16]{2,1,0:T(8,128)S(1)} %copy-done, f32[64,256]{1,0:T(8,128)S(1)} %get-tuple-element.43.refs_1_.geo_ref, f32[16,256]{1,0:T(8,128)S(1)} %get-tuple-element.49.refs_3_.refs_2_, f32[16,256]{1,0:T(8,128)S(1)} %collective-permute-done.9.refs_3_, ...), custom_call_target="tpu_custom_call" | custom-call | tf_op jit(solution)/shard_map/pallas_call | solution.py:636
  84.3 0.1 collective-permute-start.11
  84.4 0.0 collective-permute-done.8.refs_3_
  84.4 3.5 %shard_map.102 = (f32[2304,256]{1,0:T(8,128)S(1)}, f32[16,256]{1,0:T(8,128)S(1)}) custom-call(f32[2,576,16]{2,1,0:T(8,128)S(1)} %copy-done, f32[64,256]{1,0:T(8,128)S(1)} %get-tuple-element.43.refs_1_.geo_ref, f32[16,256]{1,0:T(8,128)S(1)} %get-tuple-element.53.refs_2_, f32[16,256]{1,0:T(8,128)S(1)} %collective-permute-done.8.refs_3_, ...), custom_call_target="tpu_custom_call" | custom-call | tf_op jit(solution)/shard_map/pallas_call | solution.py:636
  88.0 2.1 %collective-permute-start.10 = (f32[16,256]{1,0:T(8,128)S(1)}, f32[16,256]{1,0:T(8,128)S(1)}, u32[]{:S(2)}, u32[]{:S(2)}) collective-permute-start(f32[16,256]{1,0:T(8,128)S(1)} %get-tuple-element.60.refs_2_), channel_id=1, source_target_pairs={{0,1},{1,0},{2,3},{3,2},{4,5},{5,4},{6,7},{7,6},{8,9},{9,8},{10,11... | collective-permute-start | bytes 49160 | tf_op jit(solution)/shard_map/ppermute | solution.py:630
  90.0 0.0 collective-permute-done.11.refs_3_
  90.0 4.1 %shard_map.103 = (f32[3456,256]{1,0:T(8,128)S(1)}, f32[16,256]{1,0:T(8,128)S(1)}) custom-call(f32[2,576,16]{2,1,0:T(8,128)S(1)} %copy-done, f32[64,256]{1,0:T(8,128)S(1)} %get-tuple-element.43.refs_1_.geo_ref, f32[16,256]{1,0:T(8,128)S(1)} %get-tuple-element.56.refs_4_.refs_2_, f32[16,256]{1,0:T(8,128)S(1)} %collective-permute-done.11.refs_3_, ...), custom_call_target="tpu_custom_call" | custom-call | tf_op jit(solution)/shard_map/pallas_call | solution.py:636
  94.2 0.0 collective-permute-done.10.refs_3_
  94.2 3.6 %shard_map.104 = (f32[2304,256]{1,0:T(8,128)S(1)}, f32[16,256]{1,0:T(8,128)S(1)}) custom-call(f32[2,576,16]{2,1,0:T(8,128)S(1)} %copy-done, f32[64,256]{1,0:T(8,128)S(1)} %get-tuple-element.43.refs_1_.geo_ref, f32[16,256]{1,0:T(8,128)S(1)} %get-tuple-element.60.refs_2_, f32[16,256]{1,0:T(8,128)S(1)} %collective-permute-done.10.refs_3_, ...), custom_call_target="tpu_custom_call" | custom-call | tf_op jit(solution)/shard_map/pallas_call | solution.py:636
  97.8 0.1 collective-permute-start.13
  97.9 0.0 collective-permute-done.12.lev_ref
  97.9 3.7 %collective-permute-done.13.refs_3_ = f32[16,256]{1,0:T(8,128)S(1)} collective-permute-done((f32[16,256]{1,0:T(8,128)S(1)}, f32[16,256]{1,0:T(8,128)S(1)}, u32[]{:S(2)}, u32[]{:S(2)}) %collective-permute-start.13) | collective-permute-done | bytes 16416 | tf_op jit(solution)/shard_map/ppermute | solution.py:630
  101.6 8.0 %shard_map.105 = (f32[4608,256]{1,0:T(8,128)S(1)}, f32[32,8,256]{2,1,0:T(8,128)S(1)}) custom-call(f32[2,576,16]{2,1,0:T(8,128)S(1)} %copy-done, f32[64,256]{1,0:T(8,128)S(1)} %get-tuple-element.43.refs_1_.geo_ref, f32[16,256]{1,0:T(8,128)S(1)} %get-tuple-element.66.refs_2_, f32[16,256]{1,0:T(8,128)S(1)} %collective-permute-done.13.refs_3_, ...), custom_call_target="tpu_custom_call" | custom-call | tf_op jit(solution)/shard_map/pallas_call | solution.py:636
  109.6 14.3 %all_to_all.11.got_ref = f32[32,8,256]{2,1,0:T(8,128)S(1)} all-to-all(f32[32,8,256]{2,1,0:T(8,128)S(1)} %get-tuple-element.69), channel_id=1, replica_groups=mesh['grp'=2,'tile'=8,'spec'=2] {'grp','tile','spec'}, dimensions={0} | all-to-all | bytes 524288 | tf_op jit(solution)/shard_map/all_to_all | solution.py:763
  123.8 0.0 copy-done.9
  123.8 4.0 %shard_map.106 = (f32[576,8,256]{2,1,0:T(8,128)}, f32[3,8,32,64]{3,2,1,0:T(8,128)}) custom-call(f32[2,576,16]{2,1,0:T(8,128)S(1)} %copy-done, f32[2,3,12]{2,1,0:T(4,128)S(1)} %copy-done.11, f32[32,8,256]{2,1,0:T(8,128)S(1)} %all_to_all.11.got_ref, f32[64,256]{1,0:T(8,128)S(1)} %get-tuple-element.43.refs_1_.geo_ref, ...), custom_call_target="tpu_custom_call" | custom-call | tf_op jit(solution)/shard_map/pallas_call | solution.py:636
  (18 shorter events, 0.0 us)
Async XLA Ops:
  0.6 0.7 copy-start.10
  1.3 57.2 %copy-start.6 = (f32[2,8,256]{2,1,0:T(8,128)S(1)}, f32[2,8,256]{2,1,0:T(8,128)}, u32[]{:S(2)}) copy-start(f32[2,8,256]{2,1,0:T(8,128)} %wind_ref.1) | copy-start | bytes 49156
  1.3 57.2 %copy-start.7 = (s32[8,256]{1,0:T(8,128)S(1)}, s32[8,256]{1,0:T(8,128)}, u32[]{:S(2)}) copy-start(s32[8,256]{1,0:T(8,128)} %refs_4_.1) | copy-start | bytes 24580
  1.3 57.2 %copy-start.8 = (s32[8,256]{1,0:T(8,128)S(1)}, s32[8,256]{1,0:T(8,128)}, u32[]{:S(2)}) copy-start(s32[8,256]{1,0:T(8,128)} %mask_ref.3) | copy-start | bytes 24580
  7.5 54.6 %copy-start = (f32[2,576,16]{2,1,0:T(8,128)S(1)}, f32[2,576,16]{2,1,0:T(8,128)}, u32[]{:S(2)}) copy-start(f32[2,576,16]{2,1,0:T(8,128)} %constant.4.clone.table_ref.refs_0_) | copy-start | bytes 221188
  7.5 19.2 %collective-permute-start.6 = (f32[1152,256]{1,0:T(8,128)}, f32[1152,256]{1,0:T(8,128)S(1)}, u32[]{:S(2)}, u32[]{:S(2)}) collective-permute-start(f32[1152,256]{1,0:T(8,128)} %get-tuple-element.52), channel_id=1, source_target_pairs={{6,14},{8,0},{7,15},{9,1},{22,30},{24,16},{23,31},{25,17}} | collective-permute-start | bytes 3538952 | tf_op jit(solution)/shard_map/ppermute | solution.py:663
  9.0 19.7 %collective-permute-start = (f32[592,256]{1,0:T(8,128)}, f32[592,256]{1,0:T(8,128)S(1)}, u32[]{:S(2)}, u32[]{:S(2)}) collective-permute-start(f32[592,256]{1,0:T(8,128)} %get-tuple-element.40.refs_9_), channel_id=1, source_target_pairs={{0,2},{4,6},{8,10},{12,14},{2,0},{6,4},{10,8},{14,12},{1,3},{5,7},... | collective-permute-start | bytes 1818632 | tf_op jit(solution)/shard_map/ppermute | solution.py:627
  9.0 20.3 %collective-permute-start.1 = (f32[592,256]{1,0:T(8,128)}, f32[592,256]{1,0:T(8,128)S(1)}, u32[]{:S(2)}, u32[]{:S(2)}) collective-permute-start(f32[592,256]{1,0:T(8,128)} %get-tuple-element.41.refs_8_), channel_id=1, source_target_pairs={{2,4},{6,8},{10,12},{4,2},{8,6},{12,10},{3,5},{7,9},{11,13},{5,3},... | collective-permute-start | bytes 1818632 | tf_op jit(solution)/shard_map/ppermute | solution.py:627
  9.7 63.4 %collective-permute-start.4 = (f32[1152,256]{1,0:T(8,128)}, f32[1152,256]{1,0:T(8,128)S(1)}, u32[]{:S(2)}, u32[]{:S(2)}) collective-permute-start(f32[1152,256]{1,0:T(8,128)} %get-tuple-element.50), channel_id=1, source_target_pairs={{2,4},{10,12},{4,2},{12,10},{3,5},{11,13},{5,3},{13,11},{18,20},{2... | collective-permute-start | bytes 3538952 | tf_op jit(solution)/shard_map/ppermute | solution.py:627
  10.5 62.6 %collective-permute-start.5 = (f32[1152,256]{1,0:T(8,128)}, f32[1152,256]{1,0:T(8,128)S(1)}, u32[]{:S(2)}, u32[]{:S(2)}) collective-permute-start(f32[1152,256]{1,0:T(8,128)} %get-tuple-element.51), channel_id=1, source_target_pairs={{0,2},{4,6},{8,10},{12,14},{2,0},{6,4},{10,8},{14,12},{1,3},{5,7},... | collective-permute-start | bytes 3538952 | tf_op jit(solution)/shard_map/ppermute | solution.py:627
  26.7 46.4 %collective-permute-start.7 = (f32[1152,256]{1,0:T(8,128)S(1)}, f32[1152,256]{1,0:T(8,128)S(1)}, u32[]{:S(2)}, u32[]{:S(2)}) collective-permute-start(f32[1152,256]{1,0:T(8,128)S(1)} %collective-permute-done.6), channel_id=1, source_target_pairs={{14,8},{0,6},{15,9},{1,7},{30,24},{16,22},{31,25},{17,23}} | collective-permute-start | bytes 3538952 | tf_op jit(solution)/shard_map/ppermute | solution.py:665
  28.7 30.5 %collective-permute-start.2 = (f32[576,256]{1,0:T(8,128)}, f32[576,256]{1,0:T(8,128)S(1)}, u32[]{:S(2)}, u32[]{:S(2)}) collective-permute-start(f32[576,256]{1,0:T(8,128)} %get-tuple-element.46.refs_10_), channel_id=1, source_target_pairs={{2,4},{6,8},{10,12},{4,2},{8,6},{12,10},{3,5},{7,9},{11,13},{5,3},... | collective-permute-start | bytes 1769480 | tf_op jit(solution)/shard_map/ppermute | solution.py:627
  29.4 39.9 %collective-permute-start.3 = (f32[576,256]{1,0:T(8,128)}, f32[576,256]{1,0:T(8,128)S(1)}, u32[]{:S(2)}, u32[]{:S(2)}) collective-permute-start(f32[576,256]{1,0:T(8,128)} %get-tuple-element.47.refs_11_), channel_id=1, source_target_pairs={{0,2},{4,6},{8,10},{12,14},{2,0},{6,4},{10,8},{14,12},{1,3},{5,7},... | collective-permute-start | bytes 1769480 | tf_op jit(solution)/shard_map/ppermute | solution.py:627
  59.2 38.7 %collective-permute-start.12 = (f32[6,40,64]{2,1,0:T(8,128)S(1)}, f32[6,40,64]{2,1,0:T(8,128)S(1)}, u32[]{:S(2)}, u32[]{:S(2)}) collective-permute-start(f32[6,40,64]{2,1,0:T(8,128)S(1)} %get-tuple-element.65), channel_id=1, source_target_pairs={{0,1},{1,0},{2,3},{3,2},{4,5},{5,4},{6,7},{7,6},{8,9},{9,8},{10,11... | collective-permute-start | bytes 184328 | tf_op jit(solution)/shard_map/ppermute | solution.py:630
  62.1 7.2 %copy-start.2 = (f32[592,256]{1,0:T(8,128)S(1)}, f32[592,256]{1,0:T(8,128)}, u32[]{:S(2)}) copy-start(f32[592,256]{1,0:T(8,128)} %get-tuple-element.40.refs_9_) | copy-start | bytes 1818628
  62.1 7.2 %copy-start.3 = (f32[592,256]{1,0:T(8,128)S(1)}, f32[592,256]{1,0:T(8,128)}, u32[]{:S(2)}) copy-start(f32[592,256]{1,0:T(8,128)} %get-tuple-element.41.refs_8_) | copy-start | bytes 1818628
  62.1 7.2 %copy-start.4 = (f32[576,256]{1,0:T(8,128)S(1)}, f32[576,256]{1,0:T(8,128)}, u32[]{:S(2)}) copy-start(f32[576,256]{1,0:T(8,128)} %get-tuple-element.47.refs_11_) | copy-start | bytes 1769476
  62.1 7.2 %copy-start.5 = (f32[576,256]{1,0:T(8,128)S(1)}, f32[576,256]{1,0:T(8,128)}, u32[]{:S(2)}) copy-start(f32[576,256]{1,0:T(8,128)} %get-tuple-element.46.refs_10_) | copy-start | bytes 1769476
  73.0 6.0 %collective-permute-start.9 = (f32[16,256]{1,0:T(8,128)S(1)}, f32[16,256]{1,0:T(8,128)S(1)}, u32[]{:S(2)}, u32[]{:S(2)}) collective-permute-start(f32[16,256]{1,0:T(8,128)S(1)} %get-tuple-element.49.refs_3_.refs_2_), channel_id=1, source_target_pairs={{0,1},{1,0},{2,3},{3,2},{4,5},{5,4},{6,7},{7,6},{8,9},{9,8},{10,11... | collective-permute-start | bytes 49160 | tf_op jit(solution)/shard_map/ppermute | solution.py:630
  76.9 7.5 %collective-permute-start.8 = (f32[16,256]{1,0:T(8,128)S(1)}, f32[16,256]{1,0:T(8,128)S(1)}, u32[]{:S(2)}, u32[]{:S(2)}) collective-permute-start(f32[16,256]{1,0:T(8,128)S(1)} %get-tuple-element.53.refs_2_), channel_id=1, source_target_pairs={{0,1},{1,0},{2,3},{3,2},{4,5},{5,4},{6,7},{7,6},{8,9},{9,8},{10,11... | collective-permute-start | bytes 49160 | tf_op jit(solution)/shard_map/ppermute | solution.py:630
  84.3 5.7 %collective-permute-start.11 = (f32[16,256]{1,0:T(8,128)S(1)}, f32[16,256]{1,0:T(8,128)S(1)}, u32[]{:S(2)}, u32[]{:S(2)}) collective-permute-start(f32[16,256]{1,0:T(8,128)S(1)} %get-tuple-element.56.refs_4_.refs_2_), channel_id=1, source_target_pairs={{0,1},{1,0},{2,3},{3,2},{4,5},{5,4},{6,7},{7,6},{8,9},{9,8},{10,11... | collective-permute-start | bytes 49160 | tf_op jit(solution)/shard_map/ppermute | solution.py:630
  88.0 6.2 %collective-permute-start.10 = (f32[16,256]{1,0:T(8,128)S(1)}, f32[16,256]{1,0:T(8,128)S(1)}, u32[]{:S(2)}, u32[]{:S(2)}) collective-permute-start(f32[16,256]{1,0:T(8,128)S(1)} %get-tuple-element.60.refs_2_), channel_id=1, source_target_pairs={{0,1},{1,0},{2,3},{3,2},{4,5},{5,4},{6,7},{7,6},{8,9},{9,8},{10,11... | collective-permute-start | bytes 49160 | tf_op jit(solution)/shard_map/ppermute | solution.py:630
  97.8 3.8 %collective-permute-start.13 = (f32[16,256]{1,0:T(8,128)S(1)}, f32[16,256]{1,0:T(8,128)S(1)}, u32[]{:S(2)}, u32[]{:S(2)}) collective-permute-start(f32[16,256]{1,0:T(8,128)S(1)} %get-tuple-element.66.refs_2_), channel_id=1, source_target_pairs={{0,1},{1,0},{2,3},{3,2},{4,5},{5,4},{6,7},{7,6},{8,9},{9,8},{10,11... | collective-permute-start | bytes 49160 | tf_op jit(solution)/shard_map/ppermute | solution.py:630
  101.6 22.2 %copy-start.1 = (f32[1,3,8,32,64]{4,3,2,1,0:T(8,128)S(1)}, f32[1,3,8,32,64]{4,3,2,1,0:T(8,128)}, u32[]{:S(2)}) copy-start(f32[1,3,8,32,64]{4,3,2,1,0:T(8,128)} %param.12) | copy-start | bytes 589828
  101.6 22.2 %copy-start.9 = (f32[1,32,64]{2,1,0:T(8,128)S(1)}, f32[1,32,64]{2,1,0:T(8,128)}, u32[]{:S(2)}) copy-start(f32[1,32,64]{2,1,0:T(8,128)} %param.13) | copy-start | bytes 24580
  101.6 22.2 %copy-start.11 = (f32[2,3,12]{2,1,0:T(4,128)S(1)}, f32[2,3,12]{2,1,0:T(4,128)}, u32[]{:S(2)}) copy-start(f32[2,3,12]{2,1,0:T(4,128)} %constant.5.clone.level_ref) | copy-start | bytes 868
